TPU v7x, 32 devices: a whole 2x2x4 slice. The times are simulated.
32 devices in a mesh: grp: 2 (over y), col: 4 (over z), seq: 4 (over x, core).
Axes of the slice: x: 2, y: 2, z: 4, core: 2. Of those that a mesh axis runs over, the one named last changes fastest.
Arguments:
- row_query: bfloat16 [256, 16, 768], P(('grp', 'seq'), 'col'), parts along dimension 0, may hold values from -6 to 6
- row_key: bfloat16 [256, 16, 768], P(('grp', 'seq'), 'col'), parts along dimension 0, may hold values from -6 to 6
- row_value: bfloat16 [256, 16, 768], P(('grp', 'seq'), 'col'), parts along dimension 0, may hold values from -6 to 6
- row_grad: bfloat16 [256, 16, 768], P(('grp', 'seq'), 'col'), parts along dimension 0, may hold values from -48 to 48
- col_query: bfloat16 [256, 16, 768], P(('grp', 'seq'), 'col'), parts along dimension 0, may hold values from -11 to 11
- col_key: bfloat16 [256, 16, 768], P(('grp', 'seq'), 'col'), parts along dimension 0, may hold values from -11 to 11
- col_value: bfloat16 [256, 16, 768], P(('grp', 'seq'), 'col'), parts along dimension 0, may hold values from -6 to 6
- col_grad: bfloat16 [256, 16, 768], P(('grp', 'seq'), 'col'), parts along dimension 0, may hold values from -48 to 48
Outputs:
- row_dquery: bfloat16 [256, 16, 768], P(('grp', 'seq'), 'col'), parts along dimension 0
- row_dkey: bfloat16 [256, 16, 768], P(('grp', 'seq'), 'col'), parts along dimension 0
- row_dvalue: bfloat16 [256, 16, 768], P(('grp', 'seq'), 'col'), parts along dimension 0
- col_dquery: bfloat16 [256, 16, 768], P(('grp', 'seq'), 'col'), parts along dimension 0
- col_dkey: bfloat16 [256, 16, 768], P(('grp', 'seq'), 'col'), parts along dimension 0
- col_dvalue: bfloat16 [256, 16, 768], P(('grp', 'seq'), 'col'), parts along dimension 0
There are 2 independent parts, one for each index of `grp`. A program takes and returns all parts, laid end to end along the dimension named above; each array names one. Nothing has to cross between parts.
All inputs are finite; a program needn't handle non-finite values.
Results may differ from a plain program's by a relative error of at most 0.009.
Values may be sent and summed in bfloat16 or wider, within the bound.
No kernel may reach another device: no remote copies, remote signals or barrier semaphores. Data moves between devices by JAX's collectives and lax.ppermute only.
A program may use at most 64 MiB of HBM per device.

v0:
```python
import jax
import jax.numpy as jnp
from jax import lax
from jax.sharding import PartitionSpec as P

HEADS = 12
HEAD = 64


def tied_terms(scores, prob_grad, row_scale):
    row_probs = jax.nn.softmax(scores, axis=-1)
    row_delta = jnp.sum(row_probs * prob_grad, axis=-1, keepdims=True)
    score_gradient_part = row_probs * (prob_grad - row_delta) * row_scale
    return (row_probs.astype(jnp.bfloat16), score_gradient_part.astype(jnp.bfloat16))


def split_heads(block):
    return block.reshape(block.shape[0], block.shape[1] // HEAD, HEAD)


def column_core(query_row_block, key_row_block, value_row_block, gradient_row_block, col_scale):
    scores = (
        jnp.einsum(
            "qzd,izd->zqi", query_row_block, key_row_block, preferred_element_type=jnp.float32
        )
        * col_scale
    )
    prob_grad = jnp.einsum(
        "qzd,izd->zqi", gradient_row_block, value_row_block, preferred_element_type=jnp.float32
    )
    col_probs = jax.nn.softmax(scores, axis=-1)
    col_delta = jnp.sum(col_probs * prob_grad, axis=-1, keepdims=True)
    score_gradient_part = (col_probs * (prob_grad - col_delta) * col_scale).astype(jnp.bfloat16)
    attention_weight_rows = col_probs.astype(jnp.bfloat16)
    query_grad = jnp.einsum(
        "qvc,cqb->vqb", score_gradient_part, key_row_block, preferred_element_type=jnp.float32
    )
    key_gradient_part = jnp.einsum(
        "wzc,zwi->cwi", score_gradient_part, query_row_block, preferred_element_type=jnp.float32
    )
    value_gradient_part = jnp.einsum(
        "wzc,zwi->cwi",
        attention_weight_rows,
        gradient_row_block,
        preferred_element_type=jnp.float32,
    )
    return (
        query_grad.astype(jnp.bfloat16),
        key_gradient_part.astype(jnp.bfloat16),
        value_gradient_part.astype(jnp.bfloat16),
    )


def local(row_query, row_key, row_value, row_grad, col_query, col_key, col_value, col_grad):
    seq_dev, col_dev, width = row_query.shape
    seqs = seq_dev * lax.axis_size("seq")
    cols = col_dev * lax.axis_size("col")
    row_scale = HEAD ** (-0.5) * seqs ** (-0.5)
    col_scale = HEAD ** (-0.5)
    moved = (
        lax.all_to_all(row_query, "col", split_axis=0, concat_axis=1, tiled=True),
        lax.all_to_all(row_key, "col", split_axis=0, concat_axis=1, tiled=True),
        lax.all_to_all(row_value, "col", split_axis=0, concat_axis=1, tiled=True),
        lax.all_to_all(row_grad, "col", split_axis=0, concat_axis=1, tiled=True),
    )
    own_rows = moved[0].shape[0]
    shape_four = (own_rows, cols, HEADS, HEAD)
    query_row_block = moved[0].reshape(shape_four)
    key_row_block = moved[1].reshape(shape_four)
    value_row_block = moved[2].reshape(shape_four)
    gradient_row_block = moved[3].reshape(shape_four)
    score_part = (
        jnp.einsum(
            "sihe,sjhe->hij", query_row_block, key_row_block, preferred_element_type=jnp.float32
        )
        * row_scale
    )
    prob_part = jnp.einsum(
        "sihe,sjhe->hij", gradient_row_block, value_row_block, preferred_element_type=jnp.float32
    )
    scores, prob_grad = lax.psum((score_part, prob_part), ("col", "seq"))
    attention_weight_rows, score_gradient_part = tied_terms(scores, prob_grad, row_scale)
    query_grad = jnp.einsum(
        "hij,sjhe->sihe", score_gradient_part, key_row_block, preferred_element_type=jnp.float32
    )
    key_gradient_part = jnp.einsum(
        "hij,sihe->sjhe", score_gradient_part, query_row_block, preferred_element_type=jnp.float32
    )
    value_gradient_part = jnp.einsum(
        "hij,sihe->sjhe",
        attention_weight_rows,
        gradient_row_block,
        preferred_element_type=jnp.float32,
    )
    row_back = (
        lax.all_to_all(
            query_grad.astype(jnp.bfloat16).reshape(own_rows, cols, width),
            "col",
            split_axis=1,
            concat_axis=0,
            tiled=True,
        ),
        lax.all_to_all(
            key_gradient_part.astype(jnp.bfloat16).reshape(own_rows, cols, width),
            "col",
            split_axis=1,
            concat_axis=0,
            tiled=True,
        ),
        lax.all_to_all(
            value_gradient_part.astype(jnp.bfloat16).reshape(own_rows, cols, width),
            "col",
            split_axis=1,
            concat_axis=0,
            tiled=True,
        ),
    )
    flat_width = col_dev * width
    col_moved = (
        lax.all_to_all(
            col_query.reshape(seq_dev, flat_width), "seq", split_axis=1, concat_axis=0, tiled=True
        ),
        lax.all_to_all(
            col_key.reshape(seq_dev, flat_width), "seq", split_axis=1, concat_axis=0, tiled=True
        ),
        lax.all_to_all(
            col_value.reshape(seq_dev, flat_width), "seq", split_axis=1, concat_axis=0, tiled=True
        ),
        lax.all_to_all(
            col_grad.reshape(seq_dev, flat_width), "seq", split_axis=1, concat_axis=0, tiled=True
        ),
    )
    col_grads = column_core(
        split_heads(col_moved[0]),
        split_heads(col_moved[1]),
        split_heads(col_moved[2]),
        split_heads(col_moved[3]),
        col_scale,
    )
    share_width = col_moved[0].shape[1]
    col_back = (
        lax.all_to_all(
            col_grads[0].reshape(seqs, share_width), "seq", split_axis=0, concat_axis=1, tiled=True
        ),
        lax.all_to_all(
            col_grads[1].reshape(seqs, share_width), "seq", split_axis=0, concat_axis=1, tiled=True
        ),
        lax.all_to_all(
            col_grads[2].reshape(seqs, share_width), "seq", split_axis=0, concat_axis=1, tiled=True
        ),
    )
    return (
        row_back[0],
        row_back[1],
        row_back[2],
        col_back[0].reshape(seq_dev, col_dev, width),
        col_back[1].reshape(seq_dev, col_dev, width),
        col_back[2].reshape(seq_dev, col_dev, width),
    )


def solution(mesh):
    in_specs = (
        P(("grp", "seq"), "col", None),
        P(("grp", "seq"), "col", None),
        P(("grp", "seq"), "col", None),
        P(("grp", "seq"), "col", None),
        P(("grp", "seq"), "col", None),
        P(("grp", "seq"), "col", None),
        P(("grp", "seq"), "col", None),
        P(("grp", "seq"), "col", None),
    )
    out_specs = (
        P(("grp", "seq"), "col", None),
        P(("grp", "seq"), "col", None),
        P(("grp", "seq"), "col", None),
        P(("grp", "seq"), "col", None),
        P(("grp", "seq"), "col", None),
        P(("grp", "seq"), "col", None),
    )
    return jax.shard_map(local, mesh=mesh, in_specs=in_specs, out_specs=out_specs, check_vma=False)
```

profile of v0, /device:TPU:0, one launch (start us, length us, event | category | flops | bytes accessed | tf_op | source)
XLA Modules:
  0.0 195.9 jit_solution(17410516336404553708)
XLA Ops:
  2.3 4.3 %all-to-all-start.8 = ((bf16[32,4,768]{2,0,1:T(8,128)(2,1)}), bf16[32,4,768]{2,0,1:T(8,128)(2,1)S(1)}, u32[]{:S(2)}, u32[]{:S(2)}) async-start(bf16[32,4,768]{2,0,1:T(8,128)(2,1)} %copy.133), calls=%async_computation.8 | async-start | bytes 393216 | tf_op jit(solution)/shard_map/all_to_all | solution.py:123
  7.3 4.6 %all-to-all-done.8 = bf16[32,4,768]{2,0,1:T(8,128)(2,1)S(1)} async-done(((bf16[32,4,768]{2,0,1:T(8,128)(2,1)}), bf16[32,4,768]{2,0,1:T(8,128)(2,1)S(1)}, u32[]{:S(2)}, u32[]{:S(2)}) %all-to-all-start.8) | async-done | bytes 196640 | tf_op jit(solution)/shard_map/all_to_all | solution.py:123
  11.9 3.4 %all-to-all-start.9 = ((bf16[32,4,768]{2,0,1:T(8,128)(2,1)}), bf16[32,4,768]{2,0,1:T(8,128)(2,1)S(1)}, u32[]{:S(2)}, u32[]{:S(2)}) async-start(bf16[32,4,768]{2,0,1:T(8,128)(2,1)} %copy.136), calls=%async_computation.9 | async-start | bytes 393216 | tf_op jit(solution)/shard_map/all_to_all | solution.py:129
  16.0 4.6 %all-to-all-done.9 = bf16[32,4,768]{2,0,1:T(8,128)(2,1)S(1)} async-done(((bf16[32,4,768]{2,0,1:T(8,128)(2,1)}), bf16[32,4,768]{2,0,1:T(8,128)(2,1)S(1)}, u32[]{:S(2)}, u32[]{:S(2)}) %all-to-all-start.9) | async-done | bytes 196640 | tf_op jit(solution)/shard_map/all_to_all | solution.py:129
  20.6 3.4 %all-to-all-start.10 = ((bf16[32,4,768]{2,0,1:T(8,128)(2,1)}), bf16[32,4,768]{2,0,1:T(8,128)(2,1)S(1)}, u32[]{:S(2)}, u32[]{:S(2)}) async-start(bf16[32,4,768]{2,0,1:T(8,128)(2,1)} %copy.137), calls=%async_computation.10 | async-start | bytes 393216 | tf_op jit(solution)/shard_map/all_to_all | solution.py:126
  24.0 5.2 %all-to-all-done.10 = bf16[32,4,768]{2,0,1:T(8,128)(2,1)S(1)} async-done(((bf16[32,4,768]{2,0,1:T(8,128)(2,1)}), bf16[32,4,768]{2,0,1:T(8,128)(2,1)S(1)}, u32[]{:S(2)}, u32[]{:S(2)}) %all-to-all-start.10) | async-done | bytes 196640 | tf_op jit(solution)/shard_map/all_to_all | solution.py:126
  29.3 7.7 %all_to_all.214 = bf16[32,4,768]{2,0,1:T(8,128)(2,1)S(1)} all-to-all(bf16[32,4,768]{2,0,1:T(8,128)(2,1)S(1)} %copy.132), channel_id=1, replica_groups=mesh['grp'=2,'col'=4,'seq'=4] {'seq'}, dimensions={1} | all-to-all | bytes 393216 | tf_op jit(solution)/shard_map/all_to_all | solution.py:120
  37.0 12.7 %all_to_all.215 = bf16[32,4,768]{2,1,0:T(4,128)(2,1)S(1)} all-to-all(bf16[32,4,768]{2,1,0:T(4,128)(2,1)S(1)} %copy-done.3), channel_id=1, replica_groups=mesh['grp'=2,'col'=4,'seq'=4] {'col'}, dimensions={0} | all-to-all | bytes 393216 | tf_op jit(solution)/shard_map/all_to_all | solution.py:63
  49.7 3.4 %all-to-all-start.2 = ((bf16[32,4,768]{2,1,0:T(4,128)(2,1)}), bf16[32,4,768]{2,1,0:T(4,128)(2,1)S(1)}, u32[]{:S(2)}, u32[]{:S(2)}) async-start(bf16[32,4,768]{2,1,0:T(4,128)(2,1)} %param.11), calls=%async_computation.2 | async-start | bytes 393216 | tf_op jit(solution)/shard_map/all_to_all | solution.py:64
  55.8 3.5 %all-to-all-done.2 = bf16[32,4,768]{2,1,0:T(4,128)(2,1)S(1)} async-done(((bf16[32,4,768]{2,1,0:T(4,128)(2,1)}), bf16[32,4,768]{2,1,0:T(4,128)(2,1)S(1)}, u32[]{:S(2)}, u32[]{:S(2)}) %all-to-all-start.2) | async-done | bytes 196640 | tf_op jit(solution)/shard_map/all_to_all | solution.py:64
  59.4 3.4 %all-to-all-start.1 = ((bf16[32,4,768]{2,1,0:T(4,128)(2,1)}), bf16[32,4,768]{2,1,0:T(4,128)(2,1)S(1)}, u32[]{:S(2)}, u32[]{:S(2)}) async-start(bf16[32,4,768]{2,1,0:T(4,128)(2,1)} %param.9), calls=%async_computation.1 | async-start | bytes 393216 | tf_op jit(solution)/shard_map/all_to_all | solution.py:62
  63.5 5.4 %all-to-all-done.1 = bf16[32,4,768]{2,1,0:T(4,128)(2,1)S(1)} async-done(((bf16[32,4,768]{2,1,0:T(4,128)(2,1)}), bf16[32,4,768]{2,1,0:T(4,128)(2,1)S(1)}, u32[]{:S(2)}, u32[]{:S(2)}) %all-to-all-start.1) | async-done | bytes 196640 | tf_op jit(solution)/shard_map/all_to_all | solution.py:62
  68.9 3.4 %all-to-all-start = ((bf16[32,4,768]{2,1,0:T(4,128)(2,1)}), bf16[32,4,768]{2,1,0:T(4,128)(2,1)S(1)}, u32[]{:S(2)}, u32[]{:S(2)}) async-start(bf16[32,4,768]{2,1,0:T(4,128)(2,1)} %param.8), calls=%async_computation | async-start | bytes 393216 | tf_op jit(solution)/shard_map/all_to_all | solution.py:61
  78.7 3.4 %all-to-all-start.11 = ((bf16[4,32,768]{2,1,0:T(8,128)(2,1)}), bf16[4,32,768]{2,1,0:T(8,128)(2,1)S(1)}, u32[]{:S(2)}, u32[]{:S(2)}) async-start(bf16[4,32,768]{2,1,0:T(8,128)(2,1)} %all_to_all.191), calls=%async_computation.11 | async-start | bytes 393216 | tf_op jit(solution)/shard_map/all_to_all | solution.py:142
  83.5 64.1 %all-reduce = (f32[12,16,16]{2,1,0:T(8,128)S(1)}, f32[12,16,16]{2,1,0:T(8,128)S(1)}) all-reduce(f32[12,16,16]{2,1,0:T(8,128)S(1)} %convolution_bitcast_fusion, f32[12,16,16]{2,1,0:T(8,128)S(1)} %fusion.21), channel_id=1, replica_groups=mesh['grp'=2,'col'=4,'seq'=4] {'col','seq'}, use_global_device_ids=true, to_apply=%region_3.0 | all-reduce | flops 6144 | bytes 49152 | tf_op jit(solution)/shard_map/psum | solution.py:81
  147.6 3.4 %all-to-all-start.12 = ((bf16[4,32,768]{2,1,0:T(8,128)(2,1)}), bf16[4,32,768]{2,1,0:T(8,128)(2,1)S(1)}, u32[]{:S(2)}, u32[]{:S(2)}) async-start(bf16[4,32,768]{2,1,0:T(8,128)(2,1)} %all_to_all.194), calls=%async_computation.12 | async-start | bytes 393216 | tf_op jit(solution)/shard_map/all_to_all | solution.py:145
  152.9 3.4 %all-to-all-done.12 = bf16[4,32,768]{2,1,0:T(8,128)(2,1)S(1)} async-done(((bf16[4,32,768]{2,1,0:T(8,128)(2,1)}), bf16[4,32,768]{2,1,0:T(8,128)(2,1)S(1)}, u32[]{:S(2)}, u32[]{:S(2)}) %all-to-all-start.12) | async-done | bytes 196640 | tf_op jit(solution)/shard_map/all_to_all | solution.py:145
  156.3 3.4 %all-to-all-start.13 = ((bf16[4,32,768]{2,1,0:T(8,128)(2,1)}), bf16[4,32,768]{2,1,0:T(8,128)(2,1)S(1)}, u32[]{:S(2)}, u32[]{:S(2)}) async-start(bf16[4,32,768]{2,1,0:T(8,128)(2,1)} %all_to_all.197), calls=%async_computation.13 | async-start | bytes 393216 | tf_op jit(solution)/shard_map/all_to_all | solution.py:148
  161.7 3.3 %all-to-all-done.13 = bf16[4,32,768]{2,1,0:T(8,128)(2,1)S(1)} async-done(((bf16[4,32,768]{2,1,0:T(8,128)(2,1)}), bf16[4,32,768]{2,1,0:T(8,128)(2,1)S(1)}, u32[]{:S(2)}, u32[]{:S(2)}) %all-to-all-start.13) | async-done | bytes 196640 | tf_op jit(solution)/shard_map/all_to_all | solution.py:148
  165.0 3.5 %all-to-all-start.4 = ((bf16[8,16,768]{2,0,1:T(8,128)(2,1)}), bf16[8,16,768]{2,0,1:T(8,128)(2,1)S(1)}, u32[]{:S(2)}, u32[]{:S(2)}) async-start(bf16[8,16,768]{2,0,1:T(8,128)(2,1)} %reshape.116), calls=%async_computation.4 | async-start | bytes 393216 | tf_op jit(solution)/shard_map/all_to_all | solution.py:96
  170.6 5.3 %all-to-all-done.4 = bf16[8,16,768]{2,0,1:T(8,128)(2,1)S(1)} async-done(((bf16[8,16,768]{2,0,1:T(8,128)(2,1)}), bf16[8,16,768]{2,0,1:T(8,128)(2,1)S(1)}, u32[]{:S(2)}, u32[]{:S(2)}) %all-to-all-start.4) | async-done | bytes 196640 | tf_op jit(solution)/shard_map/all_to_all | solution.py:96
  175.9 3.4 %all-to-all-start.5 = ((bf16[8,16,768]{2,0,1:T(8,128)(2,1)}), bf16[8,16,768]{2,0,1:T(8,128)(2,1)S(1)}, u32[]{:S(2)}, u32[]{:S(2)}) async-start(bf16[8,16,768]{2,0,1:T(8,128)(2,1)} %reshape.117), calls=%async_computation.5 | async-start | bytes 393216 | tf_op jit(solution)/shard_map/all_to_all | solution.py:103
  181.3 4.2 %all-to-all-done.5 = bf16[8,16,768]{2,0,1:T(8,128)(2,1)S(1)} async-done(((bf16[8,16,768]{2,0,1:T(8,128)(2,1)}), bf16[8,16,768]{2,0,1:T(8,128)(2,1)S(1)}, u32[]{:S(2)}, u32[]{:S(2)}) %all-to-all-start.5) | async-done | bytes 196640 | tf_op jit(solution)/shard_map/all_to_all | solution.py:103
  185.5 3.4 %all-to-all-start.6 = ((bf16[8,16,768]{2,0,1:T(8,128)(2,1)}), bf16[8,16,768]{2,0,1:T(8,128)(2,1)S(1)}, u32[]{:S(2)}, u32[]{:S(2)}) async-start(bf16[8,16,768]{2,0,1:T(8,128)(2,1)} %reshape.118), calls=%async_computation.6 | async-start | bytes 393216 | tf_op jit(solution)/shard_map/all_to_all | solution.py:110
  (62 shorter events, 29.3 us)
Async XLA Ops:
  2.3 4.3 %copy-start = (bf16[32,4,768]{2,1,0:T(4,128)(2,1)S(1)}, bf16[32,4,768]{2,1,0:T(4,128)(2,1)}, u32[]{:S(2)}) copy-start(bf16[32,4,768]{2,1,0:T(4,128)(2,1)} %param.15) | copy-start | bytes 589828
  2.3 9.7 %all-to-all-start.8 = ((bf16[32,4,768]{2,0,1:T(8,128)(2,1)}), bf16[32,4,768]{2,0,1:T(8,128)(2,1)S(1)}, u32[]{:S(2)}, u32[]{:S(2)}) async-start(bf16[32,4,768]{2,0,1:T(8,128)(2,1)} %copy.133), calls=%async_computation.8 | async-start | bytes 393216 | tf_op jit(solution)/shard_map/all_to_all | solution.py:123
  7.3 8.0 %copy-start.1 = (bf16[32,4,768]{2,1,0:T(4,128)(2,1)S(1)}, bf16[32,4,768]{2,1,0:T(4,128)(2,1)}, u32[]{:S(2)}) copy-start(bf16[32,4,768]{2,1,0:T(4,128)(2,1)} %param.14) | copy-start | bytes 589828
  11.9 8.7 %all-to-all-start.9 = ((bf16[32,4,768]{2,0,1:T(8,128)(2,1)}), bf16[32,4,768]{2,0,1:T(8,128)(2,1)S(1)}, u32[]{:S(2)}, u32[]{:S(2)}) async-start(bf16[32,4,768]{2,0,1:T(8,128)(2,1)} %copy.136), calls=%async_computation.9 | async-start | bytes 393216 | tf_op jit(solution)/shard_map/all_to_all | solution.py:129
  16.0 8.0 %copy-start.2 = (bf16[32,4,768]{2,1,0:T(4,128)(2,1)S(1)}, bf16[32,4,768]{2,1,0:T(4,128)(2,1)}, u32[]{:S(2)}) copy-start(bf16[32,4,768]{2,1,0:T(4,128)(2,1)} %param.12) | copy-start | bytes 589828
  20.6 8.7 %all-to-all-start.10 = ((bf16[32,4,768]{2,0,1:T(8,128)(2,1)}), bf16[32,4,768]{2,0,1:T(8,128)(2,1)S(1)}, u32[]{:S(2)}, u32[]{:S(2)}) async-start(bf16[32,4,768]{2,0,1:T(8,128)(2,1)} %copy.137), calls=%async_computation.10 | async-start | bytes 393216 | tf_op jit(solution)/shard_map/all_to_all | solution.py:126
  24.0 13.0 %copy-start.3 = (bf16[32,4,768]{2,1,0:T(4,128)(2,1)S(1)}, bf16[32,4,768]{2,1,0:T(4,128)(2,1)}, u32[]{:S(2)}) copy-start(bf16[32,4,768]{2,1,0:T(4,128)(2,1)} %param.10) | copy-start | bytes 589828
  49.7 9.7 %all-to-all-start.2 = ((bf16[32,4,768]{2,1,0:T(4,128)(2,1)}), bf16[32,4,768]{2,1,0:T(4,128)(2,1)S(1)}, u32[]{:S(2)}, u32[]{:S(2)}) async-start(bf16[32,4,768]{2,1,0:T(4,128)(2,1)} %param.11), calls=%async_computation.2 | async-start | bytes 393216 | tf_op jit(solution)/shard_map/all_to_all | solution.py:64
  59.4 9.6 %all-to-all-start.1 = ((bf16[32,4,768]{2,1,0:T(4,128)(2,1)}), bf16[32,4,768]{2,1,0:T(4,128)(2,1)S(1)}, u32[]{:S(2)}, u32[]{:S(2)}) async-start(bf16[32,4,768]{2,1,0:T(4,128)(2,1)} %param.9), calls=%async_computation.1 | async-start | bytes 393216 | tf_op jit(solution)/shard_map/all_to_all | solution.py:62
  68.9 9.8 %all-to-all-start = ((bf16[32,4,768]{2,1,0:T(4,128)(2,1)}), bf16[32,4,768]{2,1,0:T(4,128)(2,1)S(1)}, u32[]{:S(2)}, u32[]{:S(2)}) async-start(bf16[32,4,768]{2,1,0:T(4,128)(2,1)} %param.8), calls=%async_computation | async-start | bytes 393216 | tf_op jit(solution)/shard_map/all_to_all | solution.py:61
  78.7 68.9 %all-to-all-start.11 = ((bf16[4,32,768]{2,1,0:T(8,128)(2,1)}), bf16[4,32,768]{2,1,0:T(8,128)(2,1)S(1)}, u32[]{:S(2)}, u32[]{:S(2)}) async-start(bf16[4,32,768]{2,1,0:T(8,128)(2,1)} %all_to_all.191), calls=%async_computation.11 | async-start | bytes 393216 | tf_op jit(solution)/shard_map/all_to_all | solution.py:142
  147.6 8.7 %all-to-all-start.12 = ((bf16[4,32,768]{2,1,0:T(8,128)(2,1)}), bf16[4,32,768]{2,1,0:T(8,128)(2,1)S(1)}, u32[]{:S(2)}, u32[]{:S(2)}) async-start(bf16[4,32,768]{2,1,0:T(8,128)(2,1)} %all_to_all.194), calls=%async_computation.12 | async-start | bytes 393216 | tf_op jit(solution)/shard_map/all_to_all | solution.py:145
  156.3 8.7 %all-to-all-start.13 = ((bf16[4,32,768]{2,1,0:T(8,128)(2,1)}), bf16[4,32,768]{2,1,0:T(8,128)(2,1)S(1)}, u32[]{:S(2)}, u32[]{:S(2)}) async-start(bf16[4,32,768]{2,1,0:T(8,128)(2,1)} %all_to_all.197), calls=%async_computation.13 | async-start | bytes 393216 | tf_op jit(solution)/shard_map/all_to_all | solution.py:148
  165.0 10.9 %all-to-all-start.4 = ((bf16[8,16,768]{2,0,1:T(8,128)(2,1)}), bf16[8,16,768]{2,0,1:T(8,128)(2,1)S(1)}, u32[]{:S(2)}, u32[]{:S(2)}) async-start(bf16[8,16,768]{2,0,1:T(8,128)(2,1)} %reshape.116), calls=%async_computation.4 | async-start | bytes 393216 | tf_op jit(solution)/shard_map/all_to_all | solution.py:96
  175.9 9.6 %all-to-all-start.5 = ((bf16[8,16,768]{2,0,1:T(8,128)(2,1)}), bf16[8,16,768]{2,0,1:T(8,128)(2,1)S(1)}, u32[]{:S(2)}, u32[]{:S(2)}) async-start(bf16[8,16,768]{2,0,1:T(8,128)(2,1)} %reshape.117), calls=%async_computation.5 | async-start | bytes 393216 | tf_op jit(solution)/shard_map/all_to_all | solution.py:103
  185.5 9.6 %all-to-all-start.6 = ((bf16[8,16,768]{2,0,1:T(8,128)(2,1)}), bf16[8,16,768]{2,0,1:T(8,128)(2,1)S(1)}, u32[]{:S(2)}, u32[]{:S(2)}) async-start(bf16[8,16,768]{2,0,1:T(8,128)(2,1)} %reshape.118), calls=%async_computation.6 | async-start | bytes 393216 | tf_op jit(solution)/shard_map/all_to_all | solution.py:110
where the time goes:
time: 197 us; the launch traced here: 196 us
  blocking collectives  84.5 us (43%)
  starting transfers between devices  41.6 us (21%)
  waiting for transfers between devices  41.6 us (21%)
  local copies, waits for them, and re-layouts  19.9 us (10%)
  matrix products  5.4 us (3%)
    psum x1, blocking collectives, local(): scores, prob_grad = lax.psum((score_part, prob_part), ('col', 'seq'))  64.1 us
    all_to_all x1, blocking collectives, local(): lax.all_to_all(row_value, 'col', split_axis=0, concat_axis=1, tiled=True)  12.7 us
    unnamed x18, local copies, waits for them, and re-layouts  8.05 us
    all_to_all x1, blocking collectives, local(): lax.all_to_all(col_query.reshape(seq_dev, flat_width), 'seq', split_axis=...  7.69 us
    all_to_all x1, waiting for transfers between devices, local(): lax.all_to_all(row_key, 'col', split_axis=0, concat_axis=1, tiled=True)  5.42 us
    all_to_all x1, waiting for transfers between devices, local(): lax.all_to_all(query_grad.astype(jnp.bfloat16).reshape(own_rows, cols, wi...  5.29 us
    all_to_all x1, waiting for transfers between devices, local(): lax.all_to_all(col_value.reshape(seq_dev, flat_width), 'seq', split_axis=...  5.25 us
    all_to_all x1, waiting for transfers between devices, local(): lax.all_to_all(col_key.reshape(seq_dev, flat_width), 'seq', split_axis=1,...  4.63 us
  transfers between devices with their start and end apart: 12, of which 10 were waited for; matrix products, arithmetic and copies ran while one was open for 11% of the time, Pallas kernels for 0%

commit v1 on v0

v1 whole, which is shorter than its diff:
```python
import functools

import jax
import jax.numpy as jnp
from jax import lax
from jax.experimental import pallas as pl
from jax.experimental.pallas import tpu as pltpu
from jax.sharding import PartitionSpec as P

HEADS = 12
HEAD = 64
LANES = 128
BF16 = jnp.bfloat16
F32 = jnp.float32


def nn(a, b):
    return lax.dot_general(a, b, (((1,), (0,)), ((), ())), preferred_element_type=F32)


def nt(a, b):
    return lax.dot_general(a, b, (((1,), (1,)), ((), ())), preferred_element_type=F32)


def tn(a, b):
    return lax.dot_general(a, b, (((0,), (0,)), ((), ())), preferred_element_type=F32)


def iota(shape, axis):
    return lax.broadcasted_iota(jnp.int32, shape, axis)


def pack_kernel(axis, *refs):
    arrays, blocks = refs[:4], refs[4:]
    me = lax.axis_index(axis)
    lane = iota((16, 4, LANES), 2)
    for d in range(4):
        dst = me ^ d
        full = pl.multiple_of(dst * LANES, LANES)
        tail = pl.multiple_of((4 + (dst >> 1)) * LANES, LANES)
        odd = (dst & 1) == 1
        for a, x in enumerate(arrays):
            blocks[d][a * 32 : (a + 1) * 32] = x[:, :, pl.ds(full, LANES)]
            low = x[0:16, :, pl.ds(tail, LANES)]
            high = x[16:32, :, pl.ds(tail, LANES)]
            low = jnp.where(odd, pltpu.roll(low, HEAD, 2), low)
            high = jnp.where(odd, high, pltpu.roll(high, HEAD, 2))
            start = 128 + a * 16
            blocks[d][start : start + 16] = jnp.where(lane < HEAD, low, high)


def unpack_kernel(axis, *refs):
    blocks, outs = refs[:4], refs[4:]
    me = lax.axis_index(axis)
    lane = iota((16, 4, LANES), 2)
    odd = (me & 1) == 1
    for a, out in enumerate(outs):
        for d in range(4):
            full = pl.multiple_of((me ^ d) * LANES, LANES)
            out[:, :, pl.ds(full, LANES)] = blocks[d][a * 32 : (a + 1) * 32]
        start = 96 + a * 16
        for d in (0, 2):
            tail = pl.multiple_of((4 + ((me ^ d) >> 1)) * LANES, LANES)
            x = blocks[d][start : start + 16]
            y = blocks[d + 1][start : start + 16]
            even = jnp.where(odd, y, x)
            other = jnp.where(odd, x, y)
            out[0:16, :, pl.ds(tail, LANES)] = jnp.where(lane < HEAD, even, pltpu.roll(other, HEAD, 2))
            out[16:32, :, pl.ds(tail, LANES)] = jnp.where(lane < HEAD, pltpu.roll(even, HEAD, 2), other)


def row_group(blocks, array, part):
    start = array * 128 + part * 64 if part < 2 else 512 + array * 64
    return jnp.concatenate([b[start : start + 64, :] for b in blocks], axis=0)


def same_sequence(shape):
    return ((iota(shape, 0) >> 2) & 15) == ((iota(shape, 1) >> 2) & 15)


def row_score_kernel(b0, b1, b2, b3, out):
    blocks = (b0, b1, b2, b3)
    lane = iota((256, LANES), 1)
    mask = same_sequence((256, 256))
    partials = []
    for left, right in ((0, 1), (2, 3)):
        first = second = None
        for part in (0, 1):
            x = row_group(blocks, left, part)
            y = row_group(blocks, right, part)
            zero = jnp.zeros_like(x)
            f = nt(jnp.where(lane < HEAD, x, zero), y)
            s = nt(jnp.where(lane < HEAD, zero, x), y)
            first = f if first is None else first + f
            second = s if second is None else second + s
        third = nt(row_group(blocks, left, 2), row_group(blocks, right, 2))
        for g in (first, second, third):
            g = jnp.where(mask, g, 0.0)
            partials.append(g.reshape(4, 8, 8, 256).sum(axis=1).reshape(32, 256))
    total = jnp.zeros((32, LANES), F32)
    row = iota((256, LANES), 0)
    column = ((row >> 6) << 2) + (row & 3)
    for k, t in enumerate(partials):
        place = (iota((256, LANES), 1) == column + 16 * k).astype(BF16)
        for _ in range(3):
            high = t.astype(BF16)
            total = total + nn(high, place)
            t = t - high.astype(F32)
    r = iota((16, 32), 0)
    c = iota((16, 32), 1)
    fold = (((c >> 3) == (r >> 2)) & ((c & 3) == (r & 3))).astype(BF16)
    result = jnp.zeros((16, LANES), F32)
    for _ in range(3):
        high = total.astype(BF16)
        result = result + nn(fold, high)
        total = total - high.astype(F32)
    out[...] = result


def row_grad_kernel(row_scale, p0, p1, p2, p3, b0, b1, b2, b3, *outs):
    blocks = (b0, b1, b2, b3)
    total = (p0[...] + p1[...]) + (p2[...] + p3[...])
    lane = iota((256, LANES), 1)
    mask = same_sequence((256, 256))
    row = iota((256, 16), 0)
    spread = (iota((256, 16), 1) == ((row >> 6) << 2) + (row & 3)).astype(BF16)

    def expand(small, transposed):
        half = (nt if transposed else nn)(spread, small).astype(BF16)
        return jnp.where(mask, nt(half, spread), 0.0).astype(BF16)

    mats = []
    for h in range(3):
        scores = total[:, 16 * h : 16 * h + 16] * row_scale
        dprob = total[:, 48 + 16 * h : 64 + 16 * h]
        e = jnp.exp(scores - jnp.max(scores, axis=1, keepdims=True))
        probs = e / jnp.sum(e, axis=1, keepdims=True)
        delta = jnp.sum(probs * dprob, axis=1, keepdims=True)
        dscore = (probs * (dprob - delta) * row_scale).astype(BF16)
        weights = probs.astype(BF16)
        mats.append((expand(dscore, False), expand(dscore, True), expand(weights, True)))
    for k, array in enumerate((1, 0, 2)):
        for part in (0, 1, 2):
            x = row_group(blocks, array, part)
            if part < 2:
                y = jnp.where(lane < HEAD, nn(mats[0][k], x), nn(mats[1][k], x))
                start = k * 128 + part * 64
            else:
                y = nn(mats[2][k], x)
                start = 384 + k * 64
            y = y.astype(BF16)
            for d in range(4):
                outs[d][start : start + 64, :] = y[d * 64 : (d + 1) * 64, :]


def reorder(rows, inner):
    bits = {16: 4, 32: 5}[inner]
    r = iota((rows, rows), 0)
    c = iota((rows, rows), 1)
    group = 4 * inner - 1
    source = (r & ~group) + ((r & (inner - 1)) << 2) + ((r & group) >> bits)
    return (c == source).astype(BF16)


def restore(rows, inner):
    bits = {16: 4, 32: 5}[inner]
    r = iota((rows, rows), 0)
    c = iota((rows, rows), 1)
    group = 4 * inner - 1
    source = (c & ~group) + ((c & (inner - 1)) << 2) + ((c & group) >> bits)
    return (r == source).astype(BF16)


def column_kernel(col_scale, *refs):
    blocks, outs, work, grads = refs[:4], refs[4:8], refs[8], refs[9]
    pair_order, single_order = reorder(128, 32), reorder(128, 16)
    for d in range(4):
        for a in range(4):
            x = blocks[d][a * 128 : (a + 1) * 128, :]
            work[d, a * 128 : (a + 1) * 128, :] = nn(pair_order, x).astype(BF16)
        for a in range(2):
            x = blocks[d][512 + a * 128 : 640 + a * 128, :]
            work[d, 512 + a * 128 : 640 + a * 128, :] = nn(single_order, x).astype(BF16)
    lane = iota((128, LANES), 1)

    def core(query, key, value, grad):
        scores = nt(key, query) * col_scale
        dprob = nt(value, grad)
        e = jnp.exp(scores - jnp.max(scores, axis=0, keepdims=True))
        probs = e * (1.0 / jnp.sum(e, axis=0, keepdims=True))
        delta = jnp.sum(probs * dprob, axis=0, keepdims=True)
        dscore = (probs * (dprob - delta) * col_scale).astype(BF16)
        return dscore, probs.astype(BF16)

    for c in range(4):
        x = []
        for a in range(4):
            start = a * 128 + c * 32
            x.append(jnp.concatenate([work[d, start : start + 32, :] for d in range(4)], axis=0))
        query, key, grad, value = x[0], x[1], x[2], x[3]
        zero = jnp.zeros_like(query)
        results = []
        for h in range(2):
            keep = (lane < HEAD) if h == 0 else (lane >= HEAD)
            dscore, weights = core(query, jnp.where(keep, key, zero), jnp.where(keep, value, zero), grad)
            results.append((tn(dscore, key), nn(dscore, query), nn(weights, grad)))
        for k in range(3):
            y = jnp.where(lane < HEAD, results[0][k], results[1][k]).astype(BF16)
            for d in range(4):
                grads[d, k * 128 + c * 32 : k * 128 + (c + 1) * 32, :] = y[d * 32 : (d + 1) * 32, :]
        x = []
        for a in range(4):
            start = 512 + a * 64 + c * 16
            y = jnp.concatenate([work[d, start : start + 16, :] for d in range(4)], axis=0)
            x.append(jnp.concatenate([y[:, :HEAD], y[:, HEAD:]], axis=0))
        query, key, grad, value = x[0], x[1], x[2], x[3]
        dscore, weights = core(query, key, value, grad)
        for k, y in enumerate((tn(dscore, key), nn(dscore, query), nn(weights, grad))):
            y = jnp.concatenate([y[:64], y[64:]], axis=1).astype(BF16)
            for d in range(4):
                start = 384 + k * 64 + c * 16
                grads[d, start : start + 16, :] = y[d * 16 : (d + 1) * 16, :]
    pair_back, single_back = restore(128, 32), restore(64, 16)
    for d in range(4):
        for k in range(3):
            x = grads[d, k * 128 : (k + 1) * 128, :]
            outs[d][k * 128 : (k + 1) * 128, :] = nn(pair_back, x).astype(BF16)
            x = grads[d, 384 + k * 64 : 448 + k * 64, :]
            outs[d][384 + k * 64 : 448 + k * 64, :] = nn(single_back, x).astype(BF16)


VMEM = pl.BlockSpec(memory_space=pltpu.VMEM)
LIMIT = 40 * 1024 * 1024


def call(body, shapes, dtype, operands, name, flops, scratch=()):
    return pl.pallas_call(
        body,
        out_shape=[jax.ShapeDtypeStruct(s, dtype) for s in shapes],
        in_specs=[VMEM] * len(operands),
        out_specs=[VMEM] * len(shapes),
        scratch_shapes=list(scratch),
        compiler_params=pltpu.CompilerParams(vmem_limit_bytes=LIMIT),
        cost_estimate=pl.CostEstimate(flops=flops, bytes_accessed=1 << 20, transcendentals=0),
        name=name,
    )(*operands)


def exchange(blocks, axis):
    moved = [blocks[0]]
    for d in range(1, 4):
        moved.append(lax.ppermute(blocks[d], axis, [(i, i ^ d) for i in range(4)]))
    return moved


def pack(arrays, axis, name):
    blocks = call(functools.partial(pack_kernel, axis), [(192, 4, LANES)] * 4, BF16, arrays, name, 1 << 20)
    return [b.reshape(768, LANES) for b in blocks]


def unpack(blocks, axis, shape, name):
    blocks = [b.reshape(144, 4, LANES) for b in blocks]
    return call(functools.partial(unpack_kernel, axis), [shape] * 3, BF16, blocks, name, 1 << 20)


def local_fast(row_query, row_key, row_value, row_grad, col_query, col_key, col_value, col_grad):
    shape = row_query.shape
    seqs = shape[0] * lax.axis_size("seq")
    row_scale = HEAD ** (-0.5) * seqs ** (-0.5)
    col_scale = HEAD ** (-0.5)
    row_blocks = exchange(pack((row_query, row_key, row_grad, row_value), "col", "row_pack"), "col")
    col_blocks = exchange(pack((col_query, col_key, col_grad, col_value), "seq", "col_pack"), "seq")
    (part,) = call(row_score_kernel, [(16, LANES)], F32, row_blocks, "row_scores", 1 << 28)
    parts = exchange([part] * 4, "seq")
    col_out = call(
        functools.partial(column_kernel, col_scale),
        [(576, LANES)] * 4,
        BF16,
        col_blocks,
        "col_grads",
        1 << 30,
        scratch=(pltpu.VMEM((4, 768, LANES), BF16), pltpu.VMEM((4, 576, LANES), BF16)),
    )
    col_back = exchange(col_out, "seq")
    row_out = call(
        functools.partial(row_grad_kernel, row_scale),
        [(576, LANES)] * 4,
        BF16,
        parts + row_blocks,
        "row_grads",
        1 << 28,
    )
    row_back = exchange(row_out, "col")
    col_result = unpack(col_back, "seq", shape, "col_unpack")
    row_result = unpack(row_back, "col", shape, "row_unpack")
    return (*row_result, *col_result)


def tied_terms(scores, prob_grad, row_scale):
    row_probs = jax.nn.softmax(scores, axis=-1)
    row_delta = jnp.sum(row_probs * prob_grad, axis=-1, keepdims=True)
    score_gradient_part = row_probs * (prob_grad - row_delta) * row_scale
    return (row_probs.astype(BF16), score_gradient_part.astype(BF16))


def einsum(spec, a, b):
    return jnp.einsum(spec, a, b, preferred_element_type=F32)


def column_core(query, key, value, grad, col_scale):
    scores = einsum("qzd,izd->zqi", query, key) * col_scale
    prob_grad = einsum("qzd,izd->zqi", grad, value)
    weights, dscore = tied_terms(scores, prob_grad, col_scale)
    return (
        einsum("zqi,izd->qzd", dscore, key).astype(BF16),
        einsum("zqi,qzd->izd", dscore, query).astype(BF16),
        einsum("zqi,qzd->izd", weights, grad).astype(BF16),
    )


def local_general(row_query, row_key, row_value, row_grad, col_query, col_key, col_value, col_grad):
    seq_dev, col_dev, width = row_query.shape
    seqs = seq_dev * lax.axis_size("seq")
    cols = col_dev * lax.axis_size("col")
    row_scale = HEAD ** (-0.5) * seqs ** (-0.5)
    col_scale = HEAD ** (-0.5)
    moved = [
        lax.all_to_all(x, "col", split_axis=0, concat_axis=1, tiled=True)
        for x in (row_query, row_key, row_value, row_grad)
    ]
    own_rows = moved[0].shape[0]
    query, key, value, grad = (x.reshape(own_rows, cols, HEADS, HEAD) for x in moved)
    score_part = einsum("sihe,sjhe->hij", query, key) * row_scale
    prob_part = einsum("sihe,sjhe->hij", grad, value)
    scores, prob_grad = lax.psum((score_part, prob_part), ("col", "seq"))
    weights, dscore = tied_terms(scores, prob_grad, row_scale)
    row_back = [
        lax.all_to_all(
            y.astype(BF16).reshape(own_rows, cols, width), "col", split_axis=1, concat_axis=0, tiled=True
        )
        for y in (
            einsum("hij,sjhe->sihe", dscore, key),
            einsum("hij,sihe->sjhe", dscore, query),
            einsum("hij,sihe->sjhe", weights, grad),
        )
    ]
    col_moved = [
        lax.all_to_all(
            x.reshape(seq_dev, col_dev * width), "seq", split_axis=1, concat_axis=0, tiled=True
        )
        for x in (col_query, col_key, col_value, col_grad)
    ]
    share = col_moved[0].shape[1]
    col_grads = column_core(*(x.reshape(seqs, share // HEAD, HEAD) for x in col_moved), col_scale)
    col_back = [
        lax.all_to_all(y.reshape(seqs, share), "seq", split_axis=0, concat_axis=1, tiled=True)
        for y in col_grads
    ]
    return (*row_back, *(y.reshape(seq_dev, col_dev, width) for y in col_back))


def local(*arrays):
    sizes = (lax.axis_size("col"), lax.axis_size("seq"))
    if sizes == (4, 4) and arrays[0].shape == (32, 4, HEADS * HEAD):
        return local_fast(*arrays)
    return local_general(*arrays)


def solution(mesh):
    spec = P(("grp", "seq"), "col", None)
    return jax.shard_map(
        local, mesh=mesh, in_specs=(spec,) * 8, out_specs=(spec,) * 6, check_vma=False
    )
```

time: 197 us -> 54.4 us (0.28)
  blocking collectives: 84.5 us -> 0 us
  starting transfers between devices: 41.6 us -> 18.2 us
  waiting for transfers between devices: 41.6 us -> 20.9 us
  local copies, waits for them, and re-layouts: 19.9 us -> 3.71 us
  Pallas kernels: 0 us -> 10.5 us
  matrix products: 5.4 us -> 0 us
    psum x1 -> x0, blocking collectives: 64.1 us -> none  [local(): scores, prob_grad = lax.psum((score_part, prob_part), ('col', 'seq'))]
    all_to_all x12 -> x0, waiting for transfers between devices: 41.6 us -> none  [the longest x1 5.42 us: local(): lax.all_to_all(row_key, 'col', split_axis=0, concat_axis=1, tiled=True)]
    all_to_all x12 -> x0, starting transfers between devices: 41.6 us -> none  [the longest x1 4.34 us: local(): lax.all_to_all(col_key.reshape(seq_dev, flat_width), 'seq', split_axis=1,...]
    ppermute x0 -> x15, waiting for transfers between devices: none -> 20.9 us  [exchange(): moved.append(lax.ppermute(blocks[d], axis, [(i, i ^ d) for i in range(4)]))]
    all_to_all x2 -> x0, blocking collectives: 20.4 us -> none  [the longest x1 12.7 us: local(): lax.all_to_all(row_value, 'col', split_axis=0, concat_axis=1, tiled=True)]
    ppermute x0 -> x15, starting transfers between devices: none -> 18.2 us  [exchange(): moved.append(lax.ppermute(blocks[d], axis, [(i, i ^ d) for i in range(4)]))]
    pallas_call x0 -> x7, Pallas kernels: none -> 10.5 us  [call(): pl.pallas_call(body, out_shape=[jax.ShapeDtypeStruct(s, dtype) for s in s...]
    reshape x17 -> x0, local copies, waits for them, and re-layouts: 7.51 us -> none  [the longest x7 2.45 us: split_heads(): return block.reshape(block.shape[0], block.shape[1] // HEAD, HEAD)]
  transfers between devices with their start and end apart: 12 -> 15, of which waited for: 10 -> 6; matrix products, arithmetic and copies ran while one was open for 11% -> 0% of each run, Pallas kernels for 0% -> 16%
where the time goes in v1:
time: 54.4 us; the launch traced here: 53.9 us
  waiting for transfers between devices  20.9 us (38%)
  starting transfers between devices  18.2 us (33%)
  Pallas kernels  10.5 us (19%)
  local copies, waits for them, and re-layouts  3.71 us (7%)
  between operations  0.7 us (1%)
    ppermute x15, waiting for transfers between devices, exchange(): moved.append(lax.ppermute(blocks[d], axis, [(i, i ^ d) for i in range(4)]))  20.9 us
    ppermute x15, starting transfers between devices, exchange(): moved.append(lax.ppermute(blocks[d], axis, [(i, i ^ d) for i in range(4)]))  18.2 us
    pallas_call x7, Pallas kernels, call(): pl.pallas_call(body, out_shape=[jax.ShapeDtypeStruct(s, dtype) for s in s...  10.5 us
    unnamed x16, local copies, waits for them, and re-layouts  3.71 us
  transfers between devices with their start and end apart: 15, of which 6 were waited for; matrix products, arithmetic and copies ran while one was open for 0% of the time, Pallas kernels for 16%

profile of v1, /device:TPU:0, one launch (start us, length us, event | category | flops | bytes accessed | tf_op | source)
XLA Modules:
  0.0 53.9 jit_solution(2933578334647053847)
XLA Ops:
  0.6 0.9 %copy-done = bf16[32,4,768]{2,1,0:T(4,128)(2,1)S(1)} copy-done((bf16[32,4,768]{2,1,0:T(4,128)(2,1)S(1)}, bf16[32,4,768]{2,1,0:T(4,128)(2,1)}, u32[]{:S(2)}) %copy-start) | copy-done | bytes 196632
  1.6 0.9 %copy-done.1 = bf16[32,4,768]{2,1,0:T(4,128)(2,1)S(1)} copy-done((bf16[32,4,768]{2,1,0:T(4,128)(2,1)S(1)}, bf16[32,4,768]{2,1,0:T(4,128)(2,1)}, u32[]{:S(2)}) %copy-start.1) | copy-done | bytes 196632
  2.5 0.9 %copy-done.2 = bf16[32,4,768]{2,1,0:T(4,128)(2,1)S(1)} copy-done((bf16[32,4,768]{2,1,0:T(4,128)(2,1)S(1)}, bf16[32,4,768]{2,1,0:T(4,128)(2,1)}, u32[]{:S(2)}) %copy-start.2) | copy-done | bytes 196632
  3.4 0.9 %copy-done.3 = bf16[32,4,768]{2,1,0:T(4,128)(2,1)S(1)} copy-done((bf16[32,4,768]{2,1,0:T(4,128)(2,1)S(1)}, bf16[32,4,768]{2,1,0:T(4,128)(2,1)}, u32[]{:S(2)}) %copy-start.3) | copy-done | bytes 196632
  4.4 0.7 %col_pack.1 = (bf16[192,4,128]{2,1,0:T(4,128)(2,1)S(1)}, bf16[192,4,128]{2,1,0:T(4,128)(2,1)S(1)}, bf16[192,4,128]{2,1,0:T(4,128)(2,1)S(1)}, bf16[192,4,128]{2,1,0:T(4,128)(2,1)S(1)}) custom-call(bf16[32,4,768]{2,1,0:T(4,128)(2,1)S(1)} %copy-done, bf16[32,4,768]{2,1,0:T(4,128)(2,1)S(1)} %copy-done.1, bf16[32,4,768]{2,1,0:T(4,128)(2,1)S(1)} %copy-done.2, ...), custom_call_target="tpu_custom_call" | custom-call | flops 1048576 | bytes 1048576 | tf_op jit(solution)/shard_map/col_pack/pallas_call | solution.py:237
  5.0 0.5 collective-permute-start.9
  5.6 2.6 %collective-permute-start.10 = (bf16[768,128]{1,0:T(8,128)(2,1)S(1)}, bf16[768,128]{1,0:T(8,128)(2,1)S(1)}, u32[]{:S(2)}, u32[]{:S(2)}) collective-permute-start(bf16[768,128]{1,0:T(8,128)(2,1)S(1)} %bitcast.31), channel_id=1, source_target_pairs={{0,2},{1,3},{2,0},{3,1},{4,6},{5,7},{6,4},{7,5},{8,10},{9,11},{10,... | collective-permute-start | bytes 589832 | tf_op jit(solution)/shard_map/ppermute | solution.py:252
  8.2 0.7 %row_pack.1 = (bf16[192,4,128]{2,1,0:T(4,128)(2,1)S(1)}, bf16[192,4,128]{2,1,0:T(4,128)(2,1)S(1)}, bf16[192,4,128]{2,1,0:T(4,128)(2,1)S(1)}, bf16[192,4,128]{2,1,0:T(4,128)(2,1)S(1)}) custom-call(bf16[32,4,768]{2,1,0:T(4,128)(2,1)S(1)} %copy-done.4, bf16[32,4,768]{2,1,0:T(4,128)(2,1)S(1)} %copy-done.5, bf16[32,4,768]{2,1,0:T(4,128)(2,1)S(1)} %copy-done.6, ...), custom_call_target="tpu_custom_call" | custom-call | flops 1048576 | bytes 1048576 | tf_op jit(solution)/shard_map/row_pack/pallas_call | solution.py:237
  8.9 1.9 %collective-permute-start = (bf16[768,128]{1,0:T(8,128)(2,1)S(1)}, bf16[768,128]{1,0:T(8,128)(2,1)S(1)}, u32[]{:S(2)}, u32[]{:S(2)}) collective-permute-start(bf16[768,128]{1,0:T(8,128)(2,1)S(1)} %bitcast.29), channel_id=1, source_target_pairs={{0,4},{4,0},{8,12},{12,8},{1,5},{5,1},{9,13},{13,9},{2,6},{6,2},{1... | collective-permute-start | bytes 589832 | tf_op jit(solution)/shard_map/ppermute | solution.py:252
  10.8 2.6 %collective-permute-start.1 = (bf16[768,128]{1,0:T(8,128)(2,1)S(1)}, bf16[768,128]{1,0:T(8,128)(2,1)S(1)}, u32[]{:S(2)}, u32[]{:S(2)}) collective-permute-start(bf16[768,128]{1,0:T(8,128)(2,1)S(1)} %bitcast.28), channel_id=1, source_target_pairs={{0,8},{4,12},{8,0},{12,4},{1,9},{5,13},{9,1},{13,5},{2,10},{6,14},... | collective-permute-start | bytes 589832 | tf_op jit(solution)/shard_map/ppermute | solution.py:252
  13.9 3.7 %collective-permute-done.11.refs_3_ = bf16[768,128]{1,0:T(8,128)(2,1)S(1)} collective-permute-done((bf16[768,128]{1,0:T(8,128)(2,1)S(1)}, bf16[768,128]{1,0:T(8,128)(2,1)S(1)}, u32[]{:S(2)}, u32[]{:S(2)}) %collective-permute-start.11) | collective-permute-done | bytes 196640 | tf_op jit(solution)/shard_map/ppermute | solution.py:252
  17.6 3.9 %col_grads.1 = (bf16[576,128]{1,0:T(8,128)(2,1)S(1)}, bf16[576,128]{1,0:T(8,128)(2,1)S(1)}, bf16[576,128]{1,0:T(8,128)(2,1)S(1)}, bf16[576,128]{1,0:T(8,128)(2,1)S(1)}) custom-call(bf16[768,128]{1,0:T(8,128)(2,1)S(1)} %bitcast.27, bf16[768,128]{1,0:T(8,128)(2,1)S(1)} %collective-permute-done.9.refs_1_, bf16[768,128]{1,0:T(8,128)(2,1)S(1)} %collective-permute-done.10.refs_2_, ...), custom_call_target="tpu_custom_call" | custom-call | flops 1073741824 | bytes 1048576 | tf_op jit(solution)/shard_map/col_grads/pallas_call | solution.py:237
  21.9 6.0 %collective-permute-done.1.b2 = bf16[768,128]{1,0:T(8,128)(2,1)S(1)} collective-permute-done((bf16[768,128]{1,0:T(8,128)(2,1)S(1)}, bf16[768,128]{1,0:T(8,128)(2,1)S(1)}, u32[]{:S(2)}, u32[]{:S(2)}) %collective-permute-start.1) | collective-permute-done | bytes 196640 | tf_op jit(solution)/shard_map/ppermute | solution.py:252
  27.9 0.8 %row_scores.1.p0 = f32[16,128]{1,0:T(8,128)S(1)} custom-call(bf16[768,128]{1,0:T(8,128)(2,1)S(1)} %bitcast.24, bf16[768,128]{1,0:T(8,128)(2,1)S(1)} %collective-permute-done.b1, bf16[768,128]{1,0:T(8,128)(2,1)S(1)} %collective-permute-done.1.b2, bf16[768,128]{1,0:T(8,128)(2,1)S(1)} %collective-permute-done.2.b3), custom_call_target="tpu_custom_call" | custom-call | flops 268435456 | bytes 1048576 | tf_op jit(solution)/shard_map/row_scores/pallas_call | solution.py:237
  28.7 1.5 %collective-permute-start.4 = (f32[16,128]{1,0:T(8,128)S(1)}, f32[16,128]{1,0:T(8,128)S(1)}, u32[]{:S(2)}, u32[]{:S(2)}) collective-permute-start(f32[16,128]{1,0:T(8,128)S(1)} %row_scores.1.p0), channel_id=1, source_target_pairs={{0,2},{1,3},{2,0},{3,1},{4,6},{5,7},{6,4},{7,5},{8,10},{9,11},{10,... | collective-permute-start | bytes 24584 | tf_op jit(solution)/shard_map/ppermute | solution.py:252
  30.6 1.5 %collective-permute-start.13 = (bf16[576,128]{1,0:T(8,128)(2,1)S(1)}, bf16[576,128]{1,0:T(8,128)(2,1)S(1)}, u32[]{:S(2)}, u32[]{:S(2)}) collective-permute-start(bf16[576,128]{1,0:T(8,128)(2,1)S(1)} %get-tuple-element.45), channel_id=1, source_target_pairs={{0,2},{1,3},{2,0},{3,1},{4,6},{5,7},{6,4},{7,5},{8,10},{9,11},{10,... | collective-permute-start | bytes 442376 | tf_op jit(solution)/shard_map/ppermute | solution.py:252
  32.4 2.3 %row_grads.1 = (bf16[576,128]{1,0:T(8,128)(2,1)S(1)}, bf16[576,128]{1,0:T(8,128)(2,1)S(1)}, bf16[576,128]{1,0:T(8,128)(2,1)S(1)}, bf16[576,128]{1,0:T(8,128)(2,1)S(1)}) custom-call(f32[16,128]{1,0:T(8,128)S(1)} %row_scores.1.p0, f32[16,128]{1,0:T(8,128)S(1)} %collective-permute-done.3.p1, f32[16,128]{1,0:T(8,128)S(1)} %collective-permute-done.4.p2, ...), custom_call_target="tpu_custom_call" | custom-call | flops 268435456 | bytes 1048576 | tf_op jit(solution)/shard_map/row_grads/pallas_call | solution.py:237
  34.7 4.2 %collective-permute-start.6 = (bf16[576,128]{1,0:T(8,128)(2,1)S(1)}, bf16[576,128]{1,0:T(8,128)(2,1)S(1)}, u32[]{:S(2)}, u32[]{:S(2)}) collective-permute-start(bf16[576,128]{1,0:T(8,128)(2,1)S(1)} %get-tuple-element.33), channel_id=1, source_target_pairs={{0,4},{4,0},{8,12},{12,8},{1,5},{5,1},{9,13},{13,9},{2,6},{6,2},{1... | collective-permute-start | bytes 442376 | tf_op jit(solution)/shard_map/ppermute | solution.py:252
  38.9 1.1 %collective-permute-start.7 = (bf16[576,128]{1,0:T(8,128)(2,1)S(1)}, bf16[576,128]{1,0:T(8,128)(2,1)S(1)}, u32[]{:S(2)}, u32[]{:S(2)}) collective-permute-start(bf16[576,128]{1,0:T(8,128)(2,1)S(1)} %get-tuple-element.34), channel_id=1, source_target_pairs={{0,8},{4,12},{8,0},{12,4},{1,9},{5,13},{9,1},{13,5},{2,10},{6,14},... | collective-permute-start | bytes 442376 | tf_op jit(solution)/shard_map/ppermute | solution.py:252
  40.0 1.4 %collective-permute-start.8 = (bf16[576,128]{1,0:T(8,128)(2,1)S(1)}, bf16[576,128]{1,0:T(8,128)(2,1)S(1)}, u32[]{:S(2)}, u32[]{:S(2)}) collective-permute-start(bf16[576,128]{1,0:T(8,128)(2,1)S(1)} %get-tuple-element.35), channel_id=1, source_target_pairs={{0,12},{4,8},{8,4},{12,0},{1,13},{5,9},{9,5},{13,1},{2,14},{6,10},... | collective-permute-start | bytes 442376 | tf_op jit(solution)/shard_map/ppermute | solution.py:252
  41.4 1.1 %col_unpack.1 = (bf16[32,4,768]{2,1,0:T(4,128)(2,1)}, bf16[32,4,768]{2,1,0:T(4,128)(2,1)}, bf16[32,4,768]{2,1,0:T(4,128)(2,1)}) custom-call(bf16[144,4,128]{2,1,0:T(4,128)(2,1)S(1)} %bitcast.16, bf16[144,4,128]{2,1,0:T(4,128)(2,1)S(1)} %bitcast.17, bf16[144,4,128]{2,1,0:T(4,128)(2,1)S(1)} %bitcast.19, bf16[144,4,128]{2,1,0:T(4,128)(2,1)S(1)} %bitcast.20), custom_call_target="tpu_custom_call" | custom-call | flops 1048576 | bytes 1048576 | tf_op jit(solution)/shard_map/col_unpack/pallas_call | solution.py:237
  42.5 4.0 %collective-permute-done.6 = bf16[576,128]{1,0:T(8,128)(2,1)S(1)} collective-permute-done((bf16[576,128]{1,0:T(8,128)(2,1)S(1)}, bf16[576,128]{1,0:T(8,128)(2,1)S(1)}, u32[]{:S(2)}, u32[]{:S(2)}) %collective-permute-start.6) | collective-permute-done | bytes 147488 | tf_op jit(solution)/shard_map/ppermute | solution.py:252
  46.5 6.4 %collective-permute-done.7 = bf16[576,128]{1,0:T(8,128)(2,1)S(1)} collective-permute-done((bf16[576,128]{1,0:T(8,128)(2,1)S(1)}, bf16[576,128]{1,0:T(8,128)(2,1)S(1)}, u32[]{:S(2)}, u32[]{:S(2)}) %collective-permute-start.7) | collective-permute-done | bytes 147488 | tf_op jit(solution)/shard_map/ppermute | solution.py:252
  52.8 1.1 %row_unpack.1 = (bf16[32,4,768]{2,1,0:T(4,128)(2,1)}, bf16[32,4,768]{2,1,0:T(4,128)(2,1)}, bf16[32,4,768]{2,1,0:T(4,128)(2,1)}) custom-call(bf16[144,4,128]{2,1,0:T(4,128)(2,1)S(1)} %bitcast.18, bf16[144,4,128]{2,1,0:T(4,128)(2,1)S(1)} %bitcast.21, bf16[144,4,128]{2,1,0:T(4,128)(2,1)S(1)} %bitcast.22, bf16[144,4,128]{2,1,0:T(4,128)(2,1)S(1)} %bitcast.23), custom_call_target="tpu_custom_call" | custom-call | flops 1048576 | bytes 1048576 | tf_op jit(solution)/shard_map/row_unpack/pallas_call | solution.py:237
  (29 shorter events, 1.7 us)
Async XLA Ops:
  0.6 0.9 %copy-start = (bf16[32,4,768]{2,1,0:T(4,128)(2,1)S(1)}, bf16[32,4,768]{2,1,0:T(4,128)(2,1)}, u32[]{:S(2)}) copy-start(bf16[32,4,768]{2,1,0:T(4,128)(2,1)} %refs_0_.3) | copy-start | bytes 589828
  1.6 0.9 %copy-start.1 = (bf16[32,4,768]{2,1,0:T(4,128)(2,1)S(1)}, bf16[32,4,768]{2,1,0:T(4,128)(2,1)}, u32[]{:S(2)}) copy-start(bf16[32,4,768]{2,1,0:T(4,128)(2,1)} %refs_1_.3) | copy-start | bytes 589828
  2.5 0.9 %copy-start.2 = (bf16[32,4,768]{2,1,0:T(4,128)(2,1)S(1)}, bf16[32,4,768]{2,1,0:T(4,128)(2,1)}, u32[]{:S(2)}) copy-start(bf16[32,4,768]{2,1,0:T(4,128)(2,1)} %refs_2_.3) | copy-start | bytes 589828
  3.4 0.9 %copy-start.3 = (bf16[32,4,768]{2,1,0:T(4,128)(2,1)S(1)}, bf16[32,4,768]{2,1,0:T(4,128)(2,1)}, u32[]{:S(2)}) copy-start(bf16[32,4,768]{2,1,0:T(4,128)(2,1)} %refs_3_.3) | copy-start | bytes 589828
  4.3 3.8 %copy-start.4 = (bf16[32,4,768]{2,1,0:T(4,128)(2,1)S(1)}, bf16[32,4,768]{2,1,0:T(4,128)(2,1)}, u32[]{:S(2)}) copy-start(bf16[32,4,768]{2,1,0:T(4,128)(2,1)} %refs_0_.2) | copy-start | bytes 589828
  4.3 3.8 %copy-start.5 = (bf16[32,4,768]{2,1,0:T(4,128)(2,1)S(1)}, bf16[32,4,768]{2,1,0:T(4,128)(2,1)}, u32[]{:S(2)}) copy-start(bf16[32,4,768]{2,1,0:T(4,128)(2,1)} %refs_1_.2) | copy-start | bytes 589828
  4.3 3.8 %copy-start.6 = (bf16[32,4,768]{2,1,0:T(4,128)(2,1)S(1)}, bf16[32,4,768]{2,1,0:T(4,128)(2,1)}, u32[]{:S(2)}) copy-start(bf16[32,4,768]{2,1,0:T(4,128)(2,1)} %refs_2_.2) | copy-start | bytes 589828
  4.4 3.8 %copy-start.7 = (bf16[32,4,768]{2,1,0:T(4,128)(2,1)S(1)}, bf16[32,4,768]{2,1,0:T(4,128)(2,1)}, u32[]{:S(2)}) copy-start(bf16[32,4,768]{2,1,0:T(4,128)(2,1)} %refs_3_.2) | copy-start | bytes 589828
  5.0 8.3 %collective-permute-start.9 = (bf16[768,128]{1,0:T(8,128)(2,1)S(1)}, bf16[768,128]{1,0:T(8,128)(2,1)S(1)}, u32[]{:S(2)}, u32[]{:S(2)}) collective-permute-start(bf16[768,128]{1,0:T(8,128)(2,1)S(1)} %bitcast.32), channel_id=1, source_target_pairs={{0,1},{1,0},{2,3},{3,2},{4,5},{5,4},{6,7},{7,6},{8,9},{9,8},{10,11... | collective-permute-start | bytes 589832 | tf_op jit(solution)/shard_map/ppermute | solution.py:252
  5.6 8.3 %collective-permute-start.10 = (bf16[768,128]{1,0:T(8,128)(2,1)S(1)}, bf16[768,128]{1,0:T(8,128)(2,1)S(1)}, u32[]{:S(2)}, u32[]{:S(2)}) collective-permute-start(bf16[768,128]{1,0:T(8,128)(2,1)S(1)} %bitcast.31), channel_id=1, source_target_pairs={{0,2},{1,3},{2,0},{3,1},{4,6},{5,7},{6,4},{7,5},{8,10},{9,11},{10,... | collective-permute-start | bytes 589832 | tf_op jit(solution)/shard_map/ppermute | solution.py:252
  8.1 9.4 %collective-permute-start.11 = (bf16[768,128]{1,0:T(8,128)(2,1)S(1)}, bf16[768,128]{1,0:T(8,128)(2,1)S(1)}, u32[]{:S(2)}, u32[]{:S(2)}) collective-permute-start(bf16[768,128]{1,0:T(8,128)(2,1)S(1)} %bitcast.30), channel_id=1, source_target_pairs={{0,3},{1,2},{2,1},{3,0},{4,7},{5,6},{6,5},{7,4},{8,11},{9,10},{10,... | collective-permute-start | bytes 589832 | tf_op jit(solution)/shard_map/ppermute | solution.py:252
  8.9 13.0 %collective-permute-start = (bf16[768,128]{1,0:T(8,128)(2,1)S(1)}, bf16[768,128]{1,0:T(8,128)(2,1)S(1)}, u32[]{:S(2)}, u32[]{:S(2)}) collective-permute-start(bf16[768,128]{1,0:T(8,128)(2,1)S(1)} %bitcast.29), channel_id=1, source_target_pairs={{0,4},{4,0},{8,12},{12,8},{1,5},{5,1},{9,13},{13,9},{2,6},{6,2},{1... | collective-permute-start | bytes 589832 | tf_op jit(solution)/shard_map/ppermute | solution.py:252
  10.8 17.1 %collective-permute-start.1 = (bf16[768,128]{1,0:T(8,128)(2,1)S(1)}, bf16[768,128]{1,0:T(8,128)(2,1)S(1)}, u32[]{:S(2)}, u32[]{:S(2)}) collective-permute-start(bf16[768,128]{1,0:T(8,128)(2,1)S(1)} %bitcast.28), channel_id=1, source_target_pairs={{0,8},{4,12},{8,0},{12,4},{1,9},{5,13},{9,1},{13,5},{2,10},{6,14},... | collective-permute-start | bytes 589832 | tf_op jit(solution)/shard_map/ppermute | solution.py:252
  13.4 14.5 %collective-permute-start.2 = (bf16[768,128]{1,0:T(8,128)(2,1)S(1)}, bf16[768,128]{1,0:T(8,128)(2,1)S(1)}, u32[]{:S(2)}, u32[]{:S(2)}) collective-permute-start(bf16[768,128]{1,0:T(8,128)(2,1)S(1)} %bitcast.26), channel_id=1, source_target_pairs={{0,12},{4,8},{8,4},{12,0},{1,13},{5,9},{9,5},{13,1},{2,14},{6,10},... | collective-permute-start | bytes 589832 | tf_op jit(solution)/shard_map/ppermute | solution.py:252
  21.5 18.5 %collective-permute-start.12 = (bf16[576,128]{1,0:T(8,128)(2,1)S(1)}, bf16[576,128]{1,0:T(8,128)(2,1)S(1)}, u32[]{:S(2)}, u32[]{:S(2)}) collective-permute-start(bf16[576,128]{1,0:T(8,128)(2,1)S(1)} %get-tuple-element.44), channel_id=1, source_target_pairs={{0,1},{1,0},{2,3},{3,2},{4,5},{5,4},{6,7},{7,6},{8,9},{9,8},{10,11... | collective-permute-start | bytes 442376 | tf_op jit(solution)/shard_map/ppermute | solution.py:252
  28.7 3.4 %collective-permute-start.5 = (f32[16,128]{1,0:T(8,128)S(1)}, f32[16,128]{1,0:T(8,128)S(1)}, u32[]{:S(2)}, u32[]{:S(2)}) collective-permute-start(f32[16,128]{1,0:T(8,128)S(1)} %row_scores.1.p0), channel_id=1, source_target_pairs={{0,3},{1,2},{2,1},{3,0},{4,7},{5,6},{6,5},{7,4},{8,11},{9,10},{10,... | collective-permute-start | bytes 24584 | tf_op jit(solution)/shard_map/ppermute | solution.py:252
  28.7 3.7 %collective-permute-start.4 = (f32[16,128]{1,0:T(8,128)S(1)}, f32[16,128]{1,0:T(8,128)S(1)}, u32[]{:S(2)}, u32[]{:S(2)}) collective-permute-start(f32[16,128]{1,0:T(8,128)S(1)} %row_scores.1.p0), channel_id=1, source_target_pairs={{0,2},{1,3},{2,0},{3,1},{4,6},{5,7},{6,4},{7,5},{8,10},{9,11},{10,... | collective-permute-start | bytes 24584 | tf_op jit(solution)/shard_map/ppermute | solution.py:252
  30.2 2.2 %collective-permute-start.3 = (f32[16,128]{1,0:T(8,128)S(1)}, f32[16,128]{1,0:T(8,128)S(1)}, u32[]{:S(2)}, u32[]{:S(2)}) collective-permute-start(f32[16,128]{1,0:T(8,128)S(1)} %row_scores.1.p0), channel_id=1, source_target_pairs={{0,1},{1,0},{2,3},{3,2},{4,5},{5,4},{6,7},{7,6},{8,9},{9,8},{10,11... | collective-permute-start | bytes 24584 | tf_op jit(solution)/shard_map/ppermute | solution.py:252
  30.6 10.8 %collective-permute-start.13 = (bf16[576,128]{1,0:T(8,128)(2,1)S(1)}, bf16[576,128]{1,0:T(8,128)(2,1)S(1)}, u32[]{:S(2)}, u32[]{:S(2)}) collective-permute-start(bf16[576,128]{1,0:T(8,128)(2,1)S(1)} %get-tuple-element.45), channel_id=1, source_target_pairs={{0,2},{1,3},{2,0},{3,1},{4,6},{5,7},{6,4},{7,5},{8,10},{9,11},{10,... | collective-permute-start | bytes 442376 | tf_op jit(solution)/shard_map/ppermute | solution.py:252
  32.1 9.3 %collective-permute-start.14 = (bf16[576,128]{1,0:T(8,128)(2,1)S(1)}, bf16[576,128]{1,0:T(8,128)(2,1)S(1)}, u32[]{:S(2)}, u32[]{:S(2)}) collective-permute-start(bf16[576,128]{1,0:T(8,128)(2,1)S(1)} %get-tuple-element.46), channel_id=1, source_target_pairs={{0,3},{1,2},{2,1},{3,0},{4,7},{5,6},{6,5},{7,4},{8,11},{9,10},{10,... | collective-permute-start | bytes 442376 | tf_op jit(solution)/shard_map/ppermute | solution.py:252
  34.7 11.8 %collective-permute-start.6 = (bf16[576,128]{1,0:T(8,128)(2,1)S(1)}, bf16[576,128]{1,0:T(8,128)(2,1)S(1)}, u32[]{:S(2)}, u32[]{:S(2)}) collective-permute-start(bf16[576,128]{1,0:T(8,128)(2,1)S(1)} %get-tuple-element.33), channel_id=1, source_target_pairs={{0,4},{4,0},{8,12},{12,8},{1,5},{5,1},{9,13},{13,9},{2,6},{6,2},{1... | collective-permute-start | bytes 442376 | tf_op jit(solution)/shard_map/ppermute | solution.py:252
  38.9 13.9 %collective-permute-start.7 = (bf16[576,128]{1,0:T(8,128)(2,1)S(1)}, bf16[576,128]{1,0:T(8,128)(2,1)S(1)}, u32[]{:S(2)}, u32[]{:S(2)}) collective-permute-start(bf16[576,128]{1,0:T(8,128)(2,1)S(1)} %get-tuple-element.34), channel_id=1, source_target_pairs={{0,8},{4,12},{8,0},{12,4},{1,9},{5,13},{9,1},{13,5},{2,10},{6,14},... | collective-permute-start | bytes 442376 | tf_op jit(solution)/shard_map/ppermute | solution.py:252
  40.0 12.8 %collective-permute-start.8 = (bf16[576,128]{1,0:T(8,128)(2,1)S(1)}, bf16[576,128]{1,0:T(8,128)(2,1)S(1)}, u32[]{:S(2)}, u32[]{:S(2)}) collective-permute-start(bf16[576,128]{1,0:T(8,128)(2,1)S(1)} %get-tuple-element.35), channel_id=1, source_target_pairs={{0,12},{4,8},{8,4},{12,0},{1,13},{5,9},{9,5},{13,1},{2,14},{6,10},... | collective-permute-start | bytes 442376 | tf_op jit(solution)/shard_map/ppermute | solution.py:252

commit v2 on v1

--- a/solution.py
+++ b/solution.py
@@ -30,43 +30,68 @@
     return lax.broadcasted_iota(jnp.int32, shape, axis)
 
 
+def roll_half(x):
+    return pltpu.roll(x, HEAD, 2)
+
+
 def pack_kernel(axis, *refs):
-    arrays, blocks = refs[:4], refs[4:]
+    arrays, blocks, (held, sem) = refs[:4], refs[4:8], refs[8:]
     me = lax.axis_index(axis)
+    copies = []
+    for a in range(4):
+        for q in range(CHUNKS):
+            rows = pl.ds(q * (32 // CHUNKS), 32 // CHUNKS)
+            copy = pltpu.make_async_copy(arrays[a].at[rows], held.at[a, rows], sem.at[a * CHUNKS + q])
+            copy.start()
+            copies.append(copy)
     lane = iota((16, 4, LANES), 2)
-    for d in range(4):
-        dst = me ^ d
-        full = pl.multiple_of(dst * LANES, LANES)
-        tail = pl.multiple_of((4 + (dst >> 1)) * LANES, LANES)
-        odd = (dst & 1) == 1
-        for a, x in enumerate(arrays):
-            blocks[d][a * 32 : (a + 1) * 32] = x[:, :, pl.ds(full, LANES)]
-            low = x[0:16, :, pl.ds(tail, LANES)]
-            high = x[16:32, :, pl.ds(tail, LANES)]
-            low = jnp.where(odd, pltpu.roll(low, HEAD, 2), low)
-            high = jnp.where(odd, high, pltpu.roll(high, HEAD, 2))
+    for a in range(4):
+        for copy in copies[a * CHUNKS : (a + 1) * CHUNKS]:
+            copy.wait()
+        for d in (2, 3, 1, 0):
+            dst = me ^ d
+            full = pl.multiple_of(dst * LANES, LANES)
+            tail = pl.multiple_of((4 + (dst >> 1)) * LANES, LANES)
+            odd = (dst & 1) == 1
+            blocks[d][a * 32 : (a + 1) * 32] = held[a, :, :, pl.ds(full, LANES)]
+            low = held[a, 0:16, :, pl.ds(tail, LANES)]
+            high = held[a, 16:32, :, pl.ds(tail, LANES)]
+            low = jnp.where(odd, roll_half(low), low)
+            high = jnp.where(odd, high, roll_half(high))
             start = 128 + a * 16
             blocks[d][start : start + 16] = jnp.where(lane < HEAD, low, high)
 
 
-def unpack_kernel(axis, *refs):
-    blocks, outs = refs[:4], refs[4:]
-    me = lax.axis_index(axis)
+def unpack_kernel(*refs):
+    outs, (held, sem) = refs[8:14], refs[14:]
     lane = iota((16, 4, LANES), 2)
-    odd = (me & 1) == 1
-    for a, out in enumerate(outs):
-        for d in range(4):
-            full = pl.multiple_of((me ^ d) * LANES, LANES)
-            out[:, :, pl.ds(full, LANES)] = blocks[d][a * 32 : (a + 1) * 32]
-        start = 96 + a * 16
-        for d in (0, 2):
-            tail = pl.multiple_of((4 + ((me ^ d) >> 1)) * LANES, LANES)
-            x = blocks[d][start : start + 16]
-            y = blocks[d + 1][start : start + 16]
-            even = jnp.where(odd, y, x)
-            other = jnp.where(odd, x, y)
-            out[0:16, :, pl.ds(tail, LANES)] = jnp.where(lane < HEAD, even, pltpu.roll(other, HEAD, 2))
-            out[16:32, :, pl.ds(tail, LANES)] = jnp.where(lane < HEAD, pltpu.roll(even, HEAD, 2), other)
+    copies = []
+    for side, axis in ((1, "seq"), (0, "col")):
+        b2, b3, b1, b0 = refs[4 * side : 4 * side + 4]
+        blocks = (b0, b1, b2, b3)
+        me = lax.axis_index(axis)
+        odd = (me & 1) == 1
+        for k in range(3):
+            a = 3 * side + k
+            for d in range(4):
+                full = pl.multiple_of((me ^ d) * LANES, LANES)
+                held[a, :, :, pl.ds(full, LANES)] = blocks[d][k * 32 : (k + 1) * 32]
+            start = 96 + k * 16
+            for d in (0, 2):
+                tail = pl.multiple_of((4 + ((me ^ d) >> 1)) * LANES, LANES)
+                x = blocks[d][start : start + 16]
+                y = blocks[d + 1][start : start + 16]
+                even = jnp.where(odd, y, x)
+                other = jnp.where(odd, x, y)
+                held[a, 0:16, :, pl.ds(tail, LANES)] = jnp.where(lane < HEAD, even, roll_half(other))
+                held[a, 16:32, :, pl.ds(tail, LANES)] = jnp.where(lane < HEAD, roll_half(even), other)
+            for q in range(CHUNKS):
+                rows = pl.ds(q * (32 // CHUNKS), 32 // CHUNKS)
+                copy = pltpu.make_async_copy(held.at[a, rows], outs[a].at[rows], sem.at[a * CHUNKS + q])
+                copy.start()
+                copies.append(copy)
+    for copy in copies:
+        copy.wait()
 
 
 def row_group(blocks, array, part):
@@ -78,7 +103,7 @@
     return ((iota(shape, 0) >> 2) & 15) == ((iota(shape, 1) >> 2) & 15)
 
 
-def row_score_kernel(b0, b1, b2, b3, out):
+def row_score_kernel(b2, b3, b1, b0, out):
     blocks = (b0, b1, b2, b3)
     lane = iota((256, LANES), 1)
     mask = same_sequence((256, 256))
@@ -117,7 +142,7 @@
     out[...] = result
 
 
-def row_grad_kernel(row_scale, p0, p1, p2, p3, b0, b1, b2, b3, *outs):
+def row_grad_kernel(row_scale, p0, p1, p2, p3, b2, b3, b1, b0, *outs):
     blocks = (b0, b1, b2, b3)
     total = (p0[...] + p1[...]) + (p2[...] + p3[...])
     lane = iota((256, LANES), 1)
@@ -171,41 +196,48 @@
     return (r == source).astype(BF16)
 
 
-def column_kernel(col_scale, *refs):
-    blocks, outs, work, grads = refs[:4], refs[4:8], refs[8], refs[9]
+def column_kernel(col_scale, b2, b3, b1, b0, after, o0, o1, o2, o3, work, grads):
+    blocks, outs = (b0, b1, b2, b3), (o0, o1, o2, o3)
+    del after
     pair_order, single_order = reorder(128, 32), reorder(128, 16)
     for d in range(4):
-        for a in range(4):
-            x = blocks[d][a * 128 : (a + 1) * 128, :]
-            work[d, a * 128 : (a + 1) * 128, :] = nn(pair_order, x).astype(BF16)
-        for a in range(2):
-            x = blocks[d][512 + a * 128 : 640 + a * 128, :]
-            work[d, 512 + a * 128 : 640 + a * 128, :] = nn(single_order, x).astype(BF16)
+        x = [blocks[d][a * 128 : (a + 1) * 128, :] for a in range(6)]
+        for a in (0, 2):
+            y = nn(pair_order, jnp.concatenate([x[a], x[a + 1]], axis=1)).astype(BF16)
+            work[d, a * 128 : (a + 1) * 128, :] = y[:, :LANES]
+            work[d, (a + 1) * 128 : (a + 2) * 128, :] = y[:, LANES:]
+        y = nn(single_order, jnp.concatenate([x[4], x[5]], axis=1)).astype(BF16)
+        work[d, 512:640, :] = y[:, :LANES]
+        work[d, 640:768, :] = y[:, LANES:]
     lane = iota((128, LANES), 1)
 
     def core(query, key, value, grad):
-        scores = nt(key, query) * col_scale
-        dprob = nt(value, grad)
-        e = jnp.exp(scores - jnp.max(scores, axis=0, keepdims=True))
-        probs = e * (1.0 / jnp.sum(e, axis=0, keepdims=True))
-        delta = jnp.sum(probs * dprob, axis=0, keepdims=True)
-        dscore = (probs * (dprob - delta) * col_scale).astype(BF16)
-        return dscore, probs.astype(BF16)
+        heads = key.shape[0] // 128
+        shape = (heads, 128, 128)
+        scores = (nt(key, query) * col_scale).reshape(shape)
+        dprob = nt(value, grad).reshape(shape)
+        e = jnp.exp(scores - jnp.max(scores, axis=1, keepdims=True))
+        probs = e * (1.0 / jnp.sum(e, axis=1, keepdims=True))
+        delta = jnp.sum(probs * dprob, axis=1, keepdims=True)
+        dscore = (probs * (dprob - delta) * col_scale).astype(BF16).reshape(heads * 128, 128)
+        weights = probs.astype(BF16).reshape(heads * 128, 128)
+        return tn(dscore, key), nn(dscore, query), nn(weights, grad)
+
+    def both(x):
+        zero = jnp.zeros_like(x)
+        return jnp.concatenate([jnp.where(lane < HEAD, x, zero), jnp.where(lane < HEAD, zero, x)], axis=0)
 
     for c in range(4):
         x = []
         for a in range(4):
             start = a * 128 + c * 32
             x.append(jnp.concatenate([work[d, start : start + 32, :] for d in range(4)], axis=0))
-        query, key, grad, value = x[0], x[1], x[2], x[3]
-        zero = jnp.zeros_like(query)
-        results = []
-        for h in range(2):
-            keep = (lane < HEAD) if h == 0 else (lane >= HEAD)
-            dscore, weights = core(query, jnp.where(keep, key, zero), jnp.where(keep, value, zero), grad)
-            results.append((tn(dscore, key), nn(dscore, query), nn(weights, grad)))
-        for k in range(3):
-            y = jnp.where(lane < HEAD, results[0][k], results[1][k]).astype(BF16)
+        query, key, grad, value = x
+        dquery, dkey, dvalue = core(query, both(key), both(value), grad)
+        dkey = jnp.where(lane < HEAD, dkey[:128], dkey[128:])
+        dvalue = jnp.where(lane < HEAD, dvalue[:128], dvalue[128:])
+        for k, y in enumerate((dquery, dkey, dvalue)):
+            y = y.astype(BF16)
             for d in range(4):
                 grads[d, k * 128 + c * 32 : k * 128 + (c + 1) * 32, :] = y[d * 32 : (d + 1) * 32, :]
         x = []
@@ -213,54 +245,70 @@
             start = 512 + a * 64 + c * 16
             y = jnp.concatenate([work[d, start : start + 16, :] for d in range(4)], axis=0)
             x.append(jnp.concatenate([y[:, :HEAD], y[:, HEAD:]], axis=0))
-        query, key, grad, value = x[0], x[1], x[2], x[3]
-        dscore, weights = core(query, key, value, grad)
-        for k, y in enumerate((tn(dscore, key), nn(dscore, query), nn(weights, grad))):
+        query, key, grad, value = x
+        for k, y in enumerate(core(query, key, value, grad)):
             y = jnp.concatenate([y[:64], y[64:]], axis=1).astype(BF16)
             for d in range(4):
                 start = 384 + k * 64 + c * 16
                 grads[d, start : start + 16, :] = y[d * 16 : (d + 1) * 16, :]
     pair_back, single_back = restore(128, 32), restore(64, 16)
     for d in range(4):
+        x = [grads[d, k * 128 : (k + 1) * 128, :] for k in range(3)]
+        y = nn(pair_back, jnp.concatenate(x, axis=1)).astype(BF16)
         for k in range(3):
-            x = grads[d, k * 128 : (k + 1) * 128, :]
-            outs[d][k * 128 : (k + 1) * 128, :] = nn(pair_back, x).astype(BF16)
-            x = grads[d, 384 + k * 64 : 448 + k * 64, :]
-            outs[d][384 + k * 64 : 448 + k * 64, :] = nn(single_back, x).astype(BF16)
+            outs[d][k * 128 : (k + 1) * 128, :] = y[:, k * LANES : (k + 1) * LANES]
+        x = [grads[d, 384 + k * 64 : 448 + k * 64, :] for k in range(3)]
+        y = nn(single_back, jnp.concatenate(x, axis=1)).astype(BF16)
+        for k in range(3):
+            outs[d][384 + k * 64 : 448 + k * 64, :] = y[:, k * LANES : (k + 1) * LANES]
 
 
 VMEM = pl.BlockSpec(memory_space=pltpu.VMEM)
+HBM = pl.BlockSpec(memory_space=pltpu.HBM)
 LIMIT = 40 * 1024 * 1024
-
-
-def call(body, shapes, dtype, operands, name, flops, scratch=()):
+ROW = 1
+CHUNKS = 4
+COL = 4_000_000_000
+SHIFTS = (2, 3, 1)
+
+
+def call(body, shapes, operands, name, flops, scratch=(), in_space=VMEM, out_space=VMEM):
     return pl.pallas_call(
         body,
-        out_shape=[jax.ShapeDtypeStruct(s, dtype) for s in shapes],
-        in_specs=[VMEM] * len(operands),
-        out_specs=[VMEM] * len(shapes),
+        out_shape=[jax.ShapeDtypeStruct(shape, dtype) for shape, dtype in shapes],
+        in_specs=in_space if isinstance(in_space, list) else [in_space] * len(operands),
+        out_specs=[out_space] * len(shapes),
         scratch_shapes=list(scratch),
         compiler_params=pltpu.CompilerParams(vmem_limit_bytes=LIMIT),
-        cost_estimate=pl.CostEstimate(flops=flops, bytes_accessed=1 << 20, transcendentals=0),
+        cost_estimate=pl.CostEstimate(flops=flops, bytes_accessed=1, transcendentals=0),
         name=name,
     )(*operands)
 
 
+def far_first(blocks):
+    return [blocks[2], blocks[3], blocks[1], blocks[0]]
+
+
 def exchange(blocks, axis):
-    moved = [blocks[0]]
-    for d in range(1, 4):
-        moved.append(lax.ppermute(blocks[d], axis, [(i, i ^ d) for i in range(4)]))
+    moved = list(blocks)
+    for d in SHIFTS:
+        moved[d] = lax.ppermute(blocks[d], axis, [(i, i ^ d) for i in range(4)])
     return moved
 
 
 def pack(arrays, axis, name):
-    blocks = call(functools.partial(pack_kernel, axis), [(192, 4, LANES)] * 4, BF16, arrays, name, 1 << 20)
+    arrays = [pltpu.with_memory_space_constraint(x, pltpu.HBM) for x in arrays]
+    scratch = (pltpu.VMEM((4, *arrays[0].shape), BF16), pltpu.SemaphoreType.DMA((4 * CHUNKS,)))
+    blocks = call(
+        functools.partial(pack_kernel, axis), [((192, 4, LANES), BF16)] * 4, arrays, name, 1, scratch, in_space=HBM
+    )
     return [b.reshape(768, LANES) for b in blocks]
 
 
-def unpack(blocks, axis, shape, name):
-    blocks = [b.reshape(144, 4, LANES) for b in blocks]
-    return call(functools.partial(unpack_kernel, axis), [shape] * 3, BF16, blocks, name, 1 << 20)
+def unpack(row_back, col_back, shape):
+    operands = [b.reshape(144, 4, LANES) for b in far_first(row_back) + far_first(col_back)]
+    scratch = (pltpu.VMEM((6, *shape), BF16), pltpu.SemaphoreType.DMA((6 * CHUNKS,)))
+    return call(unpack_kernel, [(shape, BF16)] * 6, operands, "unpack", 1, scratch, out_space=HBM)
 
 
 def local_fast(row_query, row_key, row_value, row_grad, col_query, col_key, col_value, col_grad):
@@ -268,32 +316,31 @@
     seqs = shape[0] * lax.axis_size("seq")
     row_scale = HEAD ** (-0.5) * seqs ** (-0.5)
     col_scale = HEAD ** (-0.5)
-    row_blocks = exchange(pack((row_query, row_key, row_grad, row_value), "col", "row_pack"), "col")
-    col_blocks = exchange(pack((col_query, col_key, col_grad, col_value), "seq", "col_pack"), "seq")
-    (part,) = call(row_score_kernel, [(16, LANES)], F32, row_blocks, "row_scores", 1 << 28)
+    row_blocks = pack((row_query, row_key, row_grad, row_value), "col", "row_pack")
+    row_blocks = exchange(row_blocks, "col")
+    col_blocks = pack((col_query, col_key, col_grad, col_value), "seq", "col_pack")
+    col_blocks = exchange(col_blocks, "seq")
+    (part,) = call(row_score_kernel, [((16, LANES), F32)], far_first(row_blocks), "row_scores", ROW)
     parts = exchange([part] * 4, "seq")
     col_out = call(
         functools.partial(column_kernel, col_scale),
-        [(576, LANES)] * 4,
-        BF16,
-        col_blocks,
+        [((576, LANES), BF16)] * 4,
+        [*far_first(col_blocks), part],
         "col_grads",
-        1 << 30,
+        COL,
         scratch=(pltpu.VMEM((4, 768, LANES), BF16), pltpu.VMEM((4, 576, LANES), BF16)),
     )
-    col_back = exchange(col_out, "seq")
     row_out = call(
         functools.partial(row_grad_kernel, row_scale),
-        [(576, LANES)] * 4,
-        BF16,
-        parts + row_blocks,
+        [((576, LANES), BF16)] * 4,
+        parts + far_first(row_blocks),
         "row_grads",
-        1 << 28,
+        ROW,
     )
+    row_out, col_out = lax.optimization_barrier((row_out, col_out))
     row_back = exchange(row_out, "col")
-    col_result = unpack(col_back, "seq", shape, "col_unpack")
-    row_result = unpack(row_back, "col", shape, "row_unpack")
-    return (*row_result, *col_result)
+    col_back = exchange(col_out, "seq")
+    return unpack(row_back, col_back, shape)
 
 
 def tied_terms(scores, prob_grad, row_scale):

time: 54.4 us -> 49.1 us (0.903)
  local copies, waits for them, and re-layouts: 3.71 us -> 0 us
  starting transfers between devices: 18.2 us -> 14.5 us
  Pallas kernels: 10.5 us -> 11.9 us
  waiting for transfers between devices: 20.9 us -> 21.8 us
    unnamed x16 -> x0, local copies, waits for them, and re-layouts: 3.71 us -> none
    ppermute x15, starting transfers between devices: 18.2 us -> 14.5 us  [exchange(): moved[d] = lax.ppermute(blocks[d], axis, [(i, i ^ d) for i in range(4)])]
    pallas_call x7 -> x6, Pallas kernels: 10.5 us -> 11.9 us  [call(): pl.pallas_call(body, out_shape=[jax.ShapeDtypeStruct(shape, dtype) for sh...]
    ppermute x15, waiting for transfers between devices: 20.9 us -> 21.8 us  [exchange(): moved[d] = lax.ppermute(blocks[d], axis, [(i, i ^ d) for i in range(4)])]
  transfers between devices with their start and end apart: 15 -> 15, of which waited for: 6 -> 4; matrix products, arithmetic and copies ran while one was open for 0% -> 0% of each run, Pallas kernels for 16% -> 12%
where the time goes in v2:
time: 49.1 us; the launch traced here: 48.9 us
  waiting for transfers between devices  21.8 us (44%)
  starting transfers between devices  14.5 us (30%)
  Pallas kernels  11.9 us (24%)
  between operations  0.71 us (1%)
    ppermute x15, waiting for transfers between devices, exchange(): moved[d] = lax.ppermute(blocks[d], axis, [(i, i ^ d) for i in range(4)])  21.8 us
    ppermute x15, starting transfers between devices, exchange(): moved[d] = lax.ppermute(blocks[d], axis, [(i, i ^ d) for i in range(4)])  14.5 us
    pallas_call x6, Pallas kernels, call(): pl.pallas_call(body, out_shape=[jax.ShapeDtypeStruct(shape, dtype) for sh...  11.9 us
  transfers between devices with their start and end apart: 15, of which 4 were waited for; matrix products, arithmetic and copies ran while one was open for 0% of the time, Pallas kernels for 12%

profile of v2, /device:TPU:0, one launch (start us, length us, event | category | flops | bytes accessed | tf_op | source)
XLA Modules:
  0.0 48.9 jit_solution(7140980922745596008)
XLA Ops:
  0.6 2.0 %row_pack.1 = (bf16[192,4,128]{2,1,0:T(4,128)(2,1)S(1)}, bf16[192,4,128]{2,1,0:T(4,128)(2,1)S(1)}, bf16[192,4,128]{2,1,0:T(4,128)(2,1)S(1)}, bf16[192,4,128]{2,1,0:T(4,128)(2,1)S(1)}) custom-call(bf16[32,4,768]{2,1,0:T(4,128)(2,1)} %refs_0_.2, bf16[32,4,768]{2,1,0:T(4,128)(2,1)} %refs_1_.2, bf16[32,4,768]{2,1,0:T(4,128)(2,1)} %refs_2_.2, ...), custom_call_target="tpu_custom_call" | custom-call | flops 1 | bytes 1 | tf_op jit(solution)/shard_map/row_pack/pallas_call | solution.py:276
  2.6 5.1 %collective-permute-start.1 = (bf16[768,128]{1,0:T(8,128)(2,1)S(1)}, bf16[768,128]{1,0:T(8,128)(2,1)S(1)}, u32[]{:S(2)}, u32[]{:S(2)}) collective-permute-start(bf16[768,128]{1,0:T(8,128)(2,1)S(1)} %bitcast.32), channel_id=1, source_target_pairs={{0,12},{4,8},{8,4},{12,0},{1,13},{5,9},{9,5},{13,1},{2,14},{6,10},... | collective-permute-start | bytes 589832 | tf_op jit(solution)/shard_map/ppermute | solution.py:295
  7.8 0.0 collective-permute-start
  7.8 0.6 %collective-permute-start.2 = (bf16[768,128]{1,0:T(8,128)(2,1)S(1)}, bf16[768,128]{1,0:T(8,128)(2,1)S(1)}, u32[]{:S(2)}, u32[]{:S(2)}) collective-permute-start(bf16[768,128]{1,0:T(8,128)(2,1)S(1)} %bitcast.29), channel_id=1, source_target_pairs={{0,4},{4,0},{8,12},{12,8},{1,5},{5,1},{9,13},{13,9},{2,6},{6,2},{1... | collective-permute-start | bytes 589832 | tf_op jit(solution)/shard_map/ppermute | solution.py:295
  8.4 2.0 %col_pack.1 = (bf16[192,4,128]{2,1,0:T(4,128)(2,1)S(1)}, bf16[192,4,128]{2,1,0:T(4,128)(2,1)S(1)}, bf16[192,4,128]{2,1,0:T(4,128)(2,1)S(1)}, bf16[192,4,128]{2,1,0:T(4,128)(2,1)S(1)}) custom-call(bf16[32,4,768]{2,1,0:T(4,128)(2,1)} %refs_0_.3, bf16[32,4,768]{2,1,0:T(4,128)(2,1)} %refs_1_.3, bf16[32,4,768]{2,1,0:T(4,128)(2,1)} %refs_2_.3, ...), custom_call_target="tpu_custom_call" | custom-call | flops 1 | bytes 1 | tf_op jit(solution)/shard_map/col_pack/pallas_call | solution.py:276
  10.4 0.4 collective-permute-start.7
  10.8 1.3 %collective-permute-start.6 = (bf16[768,128]{1,0:T(8,128)(2,1)S(1)}, bf16[768,128]{1,0:T(8,128)(2,1)S(1)}, u32[]{:S(2)}, u32[]{:S(2)}) collective-permute-start(bf16[768,128]{1,0:T(8,128)(2,1)S(1)} %bitcast.28), channel_id=1, source_target_pairs={{0,2},{1,3},{2,0},{3,1},{4,6},{5,7},{6,4},{7,5},{8,10},{9,11},{10,... | collective-permute-start | bytes 589832 | tf_op jit(solution)/shard_map/ppermute | solution.py:295
  12.2 1.4 %collective-permute-done.1.b3 = bf16[768,128]{1,0:T(8,128)(2,1)S(1)} collective-permute-done((bf16[768,128]{1,0:T(8,128)(2,1)S(1)}, bf16[768,128]{1,0:T(8,128)(2,1)S(1)}, u32[]{:S(2)}, u32[]{:S(2)}) %collective-permute-start.1) | collective-permute-done | bytes 196640 | tf_op jit(solution)/shard_map/ppermute | solution.py:295
  13.6 0.0 collective-permute-start.8
  13.6 10.8 %collective-permute-done.b2 = bf16[768,128]{1,0:T(8,128)(2,1)S(1)} collective-permute-done((bf16[768,128]{1,0:T(8,128)(2,1)S(1)}, bf16[768,128]{1,0:T(8,128)(2,1)S(1)}, u32[]{:S(2)}, u32[]{:S(2)}) %collective-permute-start) | collective-permute-done | bytes 196640 | tf_op jit(solution)/shard_map/ppermute | solution.py:295
  24.5 0.8 %row_scores.1.p0.after = f32[16,128]{1,0:T(8,128)S(1)} custom-call(bf16[768,128]{1,0:T(8,128)(2,1)S(1)} %collective-permute-done.b2, bf16[768,128]{1,0:T(8,128)(2,1)S(1)} %collective-permute-done.1.b3, bf16[768,128]{1,0:T(8,128)(2,1)S(1)} %collective-permute-done.2.b1, bf16[768,128]{1,0:T(8,128)(2,1)S(1)} %bitcast.16), custom_call_target="tpu_custom_call" | custom-call | flops 1 | bytes 1 | tf_op jit(solution)/shard_map/row_scores/pallas_call | solution.py:276
  25.3 0.3 collective-permute-start.5
  25.5 1.3 %collective-permute-start.4 = (f32[16,128]{1,0:T(8,128)S(1)}, f32[16,128]{1,0:T(8,128)S(1)}, u32[]{:S(2)}, u32[]{:S(2)}) collective-permute-start(f32[16,128]{1,0:T(8,128)S(1)} %row_scores.1.p0.after), channel_id=1, source_target_pairs={{0,2},{1,3},{2,0},{3,1},{4,6},{5,7},{6,4},{7,5},{8,10},{9,11},{10,... | collective-permute-start | bytes 24584 | tf_op jit(solution)/shard_map/ppermute | solution.py:295
  26.8 0.3 collective-permute-start.3
  27.1 3.3 %col_grads.1 = (bf16[576,128]{1,0:T(8,128)(2,1)S(1)}, bf16[576,128]{1,0:T(8,128)(2,1)S(1)}, bf16[576,128]{1,0:T(8,128)(2,1)S(1)}, bf16[576,128]{1,0:T(8,128)(2,1)S(1)}) custom-call(bf16[768,128]{1,0:T(8,128)(2,1)S(1)} %collective-permute-done.6.b2, bf16[768,128]{1,0:T(8,128)(2,1)S(1)} %collective-permute-done.7.b3, ...), custom_call_target="tpu_custom_call" | custom-call | flops 4000000000 | bytes 1 | tf_op jit(solution)/shard_map/col_grads/pallas_call | solution.py:276
  30.5 2.3 %row_grads.1 = (bf16[576,128]{1,0:T(8,128)(2,1)S(1)}, bf16[576,128]{1,0:T(8,128)(2,1)S(1)}, bf16[576,128]{1,0:T(8,128)(2,1)S(1)}, bf16[576,128]{1,0:T(8,128)(2,1)S(1)}) custom-call(f32[16,128]{1,0:T(8,128)S(1)} %row_scores.1.p0.after, f32[16,128]{1,0:T(8,128)S(1)} %collective-permute-done.3.p1, f32[16,128]{1,0:T(8,128)S(1)} %collective-permute-done.4.p2, ...), custom_call_target="tpu_custom_call" | custom-call | flops 1 | bytes 1 | tf_op jit(solution)/shard_map/row_grads/pallas_call | solution.py:276
  32.7 0.1 collective-permute-start.9
  32.8 2.5 %collective-permute-start.10 = (bf16[576,128]{1,0:T(8,128)(2,1)S(1)}, bf16[576,128]{1,0:T(8,128)(2,1)S(1)}, u32[]{:S(2)}, u32[]{:S(2)}) collective-permute-start(bf16[576,128]{1,0:T(8,128)(2,1)S(1)} %get-tuple-element.47), channel_id=1, source_target_pairs={{0,12},{4,8},{8,4},{12,0},{1,13},{5,9},{9,5},{13,1},{2,14},{6,10},... | collective-permute-start | bytes 442376 | tf_op jit(solution)/shard_map/ppermute | solution.py:295
  35.4 0.9 %collective-permute-start.11 = (bf16[576,128]{1,0:T(8,128)(2,1)S(1)}, bf16[576,128]{1,0:T(8,128)(2,1)S(1)}, u32[]{:S(2)}, u32[]{:S(2)}) collective-permute-start(bf16[576,128]{1,0:T(8,128)(2,1)S(1)} %get-tuple-element.48), channel_id=1, source_target_pairs={{0,4},{4,0},{8,12},{12,8},{1,5},{5,1},{9,13},{13,9},{2,6},{6,2},{1... | collective-permute-start | bytes 442376 | tf_op jit(solution)/shard_map/ppermute | solution.py:295
  36.3 1.5 %collective-permute-start.12 = (bf16[576,128]{1,0:T(8,128)(2,1)S(1)}, bf16[576,128]{1,0:T(8,128)(2,1)S(1)}, u32[]{:S(2)}, u32[]{:S(2)}) collective-permute-start(bf16[576,128]{1,0:T(8,128)(2,1)S(1)} %get-tuple-element.50), channel_id=1, source_target_pairs={{0,2},{1,3},{2,0},{3,1},{4,6},{5,7},{6,4},{7,5},{8,10},{9,11},{10,... | collective-permute-start | bytes 442376 | tf_op jit(solution)/shard_map/ppermute | solution.py:295
  37.8 8.1 %collective-permute-done.9 = bf16[576,128]{1,0:T(8,128)(2,1)S(1)} collective-permute-done((bf16[576,128]{1,0:T(8,128)(2,1)S(1)}, bf16[576,128]{1,0:T(8,128)(2,1)S(1)}, u32[]{:S(2)}, u32[]{:S(2)}) %collective-permute-start.9) | collective-permute-done | bytes 147488 | tf_op jit(solution)/shard_map/ppermute | solution.py:295
  45.9 1.3 %collective-permute-done.11 = bf16[576,128]{1,0:T(8,128)(2,1)S(1)} collective-permute-done((bf16[576,128]{1,0:T(8,128)(2,1)S(1)}, bf16[576,128]{1,0:T(8,128)(2,1)S(1)}, u32[]{:S(2)}, u32[]{:S(2)}) %collective-permute-start.11) | collective-permute-done | bytes 147488 | tf_op jit(solution)/shard_map/ppermute | solution.py:295
  47.2 0.0 collective-permute-done.14
  47.3 1.6 %unpack.1 = (bf16[32,4,768]{2,1,0:T(4,128)(2,1)}, bf16[32,4,768]{2,1,0:T(4,128)(2,1)}, bf16[32,4,768]{2,1,0:T(4,128)(2,1)}, bf16[32,4,768]{2,1,0:T(4,128)(2,1)},...) custom-call(bf16[144,4,128]{2,1,0:T(4,128)(2,1)S(1)} %bitcast.20, bf16[144,4,128]{2,1,0:T(4,128)(2,1)S(1)} %bitcast.21, ...), custom_call_target="tpu_custom_call" | custom-call | flops 1 | bytes 1 | tf_op jit(solution)/shard_map/unpack/pallas_call | solution.py:276
  (12 shorter events, 0.0 us)
Async XLA Ops:
  2.6 11.0 %collective-permute-start.1 = (bf16[768,128]{1,0:T(8,128)(2,1)S(1)}, bf16[768,128]{1,0:T(8,128)(2,1)S(1)}, u32[]{:S(2)}, u32[]{:S(2)}) collective-permute-start(bf16[768,128]{1,0:T(8,128)(2,1)S(1)} %bitcast.32), channel_id=1, source_target_pairs={{0,12},{4,8},{8,4},{12,0},{1,13},{5,9},{9,5},{13,1},{2,14},{6,10},... | collective-permute-start | bytes 589832 | tf_op jit(solution)/shard_map/ppermute | solution.py:295
  7.8 16.7 %collective-permute-start = (bf16[768,128]{1,0:T(8,128)(2,1)S(1)}, bf16[768,128]{1,0:T(8,128)(2,1)S(1)}, u32[]{:S(2)}, u32[]{:S(2)}) collective-permute-start(bf16[768,128]{1,0:T(8,128)(2,1)S(1)} %bitcast.31), channel_id=1, source_target_pairs={{0,8},{4,12},{8,0},{12,4},{1,9},{5,13},{9,1},{13,5},{2,10},{6,14},... | collective-permute-start | bytes 589832 | tf_op jit(solution)/shard_map/ppermute | solution.py:295
  7.8 16.7 %collective-permute-start.2 = (bf16[768,128]{1,0:T(8,128)(2,1)S(1)}, bf16[768,128]{1,0:T(8,128)(2,1)S(1)}, u32[]{:S(2)}, u32[]{:S(2)}) collective-permute-start(bf16[768,128]{1,0:T(8,128)(2,1)S(1)} %bitcast.29), channel_id=1, source_target_pairs={{0,4},{4,0},{8,12},{12,8},{1,5},{5,1},{9,13},{13,9},{2,6},{6,2},{1... | collective-permute-start | bytes 589832 | tf_op jit(solution)/shard_map/ppermute | solution.py:295
  10.4 16.4 %collective-permute-start.7 = (bf16[768,128]{1,0:T(8,128)(2,1)S(1)}, bf16[768,128]{1,0:T(8,128)(2,1)S(1)}, u32[]{:S(2)}, u32[]{:S(2)}) collective-permute-start(bf16[768,128]{1,0:T(8,128)(2,1)S(1)} %bitcast.30), channel_id=1, source_target_pairs={{0,3},{1,2},{2,1},{3,0},{4,7},{5,6},{6,5},{7,4},{8,11},{9,10},{10,... | collective-permute-start | bytes 589832 | tf_op jit(solution)/shard_map/ppermute | solution.py:295
  10.8 16.3 %collective-permute-start.6 = (bf16[768,128]{1,0:T(8,128)(2,1)S(1)}, bf16[768,128]{1,0:T(8,128)(2,1)S(1)}, u32[]{:S(2)}, u32[]{:S(2)}) collective-permute-start(bf16[768,128]{1,0:T(8,128)(2,1)S(1)} %bitcast.28), channel_id=1, source_target_pairs={{0,2},{1,3},{2,0},{3,1},{4,6},{5,7},{6,4},{7,5},{8,10},{9,11},{10,... | collective-permute-start | bytes 589832 | tf_op jit(solution)/shard_map/ppermute | solution.py:295
  13.6 13.5 %collective-permute-start.8 = (bf16[768,128]{1,0:T(8,128)(2,1)S(1)}, bf16[768,128]{1,0:T(8,128)(2,1)S(1)}, u32[]{:S(2)}, u32[]{:S(2)}) collective-permute-start(bf16[768,128]{1,0:T(8,128)(2,1)S(1)} %bitcast.27), channel_id=1, source_target_pairs={{0,1},{1,0},{2,3},{3,2},{4,5},{5,4},{6,7},{7,6},{8,9},{9,8},{10,11... | collective-permute-start | bytes 589832 | tf_op jit(solution)/shard_map/ppermute | solution.py:295
  25.3 5.2 %collective-permute-start.5 = (f32[16,128]{1,0:T(8,128)S(1)}, f32[16,128]{1,0:T(8,128)S(1)}, u32[]{:S(2)}, u32[]{:S(2)}) collective-permute-start(f32[16,128]{1,0:T(8,128)S(1)} %row_scores.1.p0.after), channel_id=1, source_target_pairs={{0,3},{1,2},{2,1},{3,0},{4,7},{5,6},{6,5},{7,4},{8,11},{9,10},{10,... | collective-permute-start | bytes 24584 | tf_op jit(solution)/shard_map/ppermute | solution.py:295
  25.5 4.9 %collective-permute-start.4 = (f32[16,128]{1,0:T(8,128)S(1)}, f32[16,128]{1,0:T(8,128)S(1)}, u32[]{:S(2)}, u32[]{:S(2)}) collective-permute-start(f32[16,128]{1,0:T(8,128)S(1)} %row_scores.1.p0.after), channel_id=1, source_target_pairs={{0,2},{1,3},{2,0},{3,1},{4,6},{5,7},{6,4},{7,5},{8,10},{9,11},{10,... | collective-permute-start | bytes 24584 | tf_op jit(solution)/shard_map/ppermute | solution.py:295
  26.8 3.7 %collective-permute-start.3 = (f32[16,128]{1,0:T(8,128)S(1)}, f32[16,128]{1,0:T(8,128)S(1)}, u32[]{:S(2)}, u32[]{:S(2)}) collective-permute-start(f32[16,128]{1,0:T(8,128)S(1)} %row_scores.1.p0.after), channel_id=1, source_target_pairs={{0,1},{1,0},{2,3},{3,2},{4,5},{5,4},{6,7},{7,6},{8,9},{9,8},{10,11... | collective-permute-start | bytes 24584 | tf_op jit(solution)/shard_map/ppermute | solution.py:295
  32.7 13.2 %collective-permute-start.9 = (bf16[576,128]{1,0:T(8,128)(2,1)S(1)}, bf16[576,128]{1,0:T(8,128)(2,1)S(1)}, u32[]{:S(2)}, u32[]{:S(2)}) collective-permute-start(bf16[576,128]{1,0:T(8,128)(2,1)S(1)} %get-tuple-element.46), channel_id=1, source_target_pairs={{0,8},{4,12},{8,0},{12,4},{1,9},{5,13},{9,1},{13,5},{2,10},{6,14},... | collective-permute-start | bytes 442376 | tf_op jit(solution)/shard_map/ppermute | solution.py:295
  32.8 13.1 %collective-permute-start.10 = (bf16[576,128]{1,0:T(8,128)(2,1)S(1)}, bf16[576,128]{1,0:T(8,128)(2,1)S(1)}, u32[]{:S(2)}, u32[]{:S(2)}) collective-permute-start(bf16[576,128]{1,0:T(8,128)(2,1)S(1)} %get-tuple-element.47), channel_id=1, source_target_pairs={{0,12},{4,8},{8,4},{12,0},{1,13},{5,9},{9,5},{13,1},{2,14},{6,10},... | collective-permute-start | bytes 442376 | tf_op jit(solution)/shard_map/ppermute | solution.py:295
  35.4 11.9 %collective-permute-start.11 = (bf16[576,128]{1,0:T(8,128)(2,1)S(1)}, bf16[576,128]{1,0:T(8,128)(2,1)S(1)}, u32[]{:S(2)}, u32[]{:S(2)}) collective-permute-start(bf16[576,128]{1,0:T(8,128)(2,1)S(1)} %get-tuple-element.48), channel_id=1, source_target_pairs={{0,4},{4,0},{8,12},{12,8},{1,5},{5,1},{9,13},{13,9},{2,6},{6,2},{1... | collective-permute-start | bytes 442376 | tf_op jit(solution)/shard_map/ppermute | solution.py:295
  36.3 10.9 %collective-permute-start.12 = (bf16[576,128]{1,0:T(8,128)(2,1)S(1)}, bf16[576,128]{1,0:T(8,128)(2,1)S(1)}, u32[]{:S(2)}, u32[]{:S(2)}) collective-permute-start(bf16[576,128]{1,0:T(8,128)(2,1)S(1)} %get-tuple-element.50), channel_id=1, source_target_pairs={{0,2},{1,3},{2,0},{3,1},{4,6},{5,7},{6,4},{7,5},{8,10},{9,11},{10,... | collective-permute-start | bytes 442376 | tf_op jit(solution)/shard_map/ppermute | solution.py:295
  37.8 9.5 %collective-permute-start.13 = (bf16[576,128]{1,0:T(8,128)(2,1)S(1)}, bf16[576,128]{1,0:T(8,128)(2,1)S(1)}, u32[]{:S(2)}, u32[]{:S(2)}) collective-permute-start(bf16[576,128]{1,0:T(8,128)(2,1)S(1)} %get-tuple-element.51), channel_id=1, source_target_pairs={{0,3},{1,2},{2,1},{3,0},{4,7},{5,6},{6,5},{7,4},{8,11},{9,10},{10,... | collective-permute-start | bytes 442376 | tf_op jit(solution)/shard_map/ppermute | solution.py:295
  45.9 1.4 %collective-permute-start.14 = (bf16[576,128]{1,0:T(8,128)(2,1)S(1)}, bf16[576,128]{1,0:T(8,128)(2,1)S(1)}, u32[]{:S(2)}, u32[]{:S(2)}) collective-permute-start(bf16[576,128]{1,0:T(8,128)(2,1)S(1)} %get-tuple-element.52), channel_id=1, source_target_pairs={{0,1},{1,0},{2,3},{3,2},{4,5},{5,4},{6,7},{7,6},{8,9},{9,8},{10,11... | collective-permute-start | bytes 442376 | tf_op jit(solution)/shard_map/ppermute | solution.py:295

commit v3 on v2

--- a/solution.py
+++ b/solution.py
@@ -44,31 +44,33 @@
             copy = pltpu.make_async_copy(arrays[a].at[rows], held.at[a, rows], sem.at[a * CHUNKS + q])
             copy.start()
             copies.append(copy)
-    lane = iota((16, 4, LANES), 2)
+    low_lanes = iota((16, 4, LANES), 2) < HEAD
+    odd = (me & 1) == 1
     for a in range(4):
         for copy in copies[a * CHUNKS : (a + 1) * CHUNKS]:
             copy.wait()
-        for d in (2, 3, 1, 0):
-            dst = me ^ d
-            full = pl.multiple_of(dst * LANES, LANES)
-            tail = pl.multiple_of((4 + (dst >> 1)) * LANES, LANES)
-            odd = (dst & 1) == 1
+        for d in range(4):
+            full = pl.multiple_of((me ^ d) * LANES, LANES)
             blocks[d][a * 32 : (a + 1) * 32] = held[a, :, :, pl.ds(full, LANES)]
+        start = 128 + a * 16
+        for d in (0, 2):
+            tail = pl.multiple_of((4 + ((me ^ d) >> 1)) * LANES, LANES)
             low = held[a, 0:16, :, pl.ds(tail, LANES)]
             high = held[a, 16:32, :, pl.ds(tail, LANES)]
-            low = jnp.where(odd, roll_half(low), low)
-            high = jnp.where(odd, high, roll_half(high))
-            start = 128 + a * 16
-            blocks[d][start : start + 16] = jnp.where(lane < HEAD, low, high)
+            x = roll_half(jnp.where(low_lanes, high, low))
+            even_head = jnp.where(low_lanes, low, x)
+            odd_head = jnp.where(low_lanes, x, high)
+            blocks[d][start : start + 16] = jnp.where(odd, odd_head, even_head)
+            blocks[d + 1][start : start + 16] = jnp.where(odd, even_head, odd_head)
 
 
 def unpack_kernel(*refs):
-    outs, (held, sem) = refs[8:14], refs[14:]
-    lane = iota((16, 4, LANES), 2)
+    outs, (held, sem) = refs[-8:-2], refs[-2:]
+    low_lanes = iota((16, 4, LANES), 2) < HEAD
     copies = []
     for side, axis in ((1, "seq"), (0, "col")):
-        b2, b3, b1, b0 = refs[4 * side : 4 * side + 4]
-        blocks = (b0, b1, b2, b3)
+        blocks = refs[4 * side : 4 * side + 4]
+        blocks = (blocks[3], blocks[2], *blocks[:2]) if side else (blocks[3], blocks[0], blocks[2], blocks[1])
         me = lax.axis_index(axis)
         odd = (me & 1) == 1
         for k in range(3):
@@ -83,8 +85,9 @@
                 y = blocks[d + 1][start : start + 16]
                 even = jnp.where(odd, y, x)
                 other = jnp.where(odd, x, y)
-                held[a, 0:16, :, pl.ds(tail, LANES)] = jnp.where(lane < HEAD, even, roll_half(other))
-                held[a, 16:32, :, pl.ds(tail, LANES)] = jnp.where(lane < HEAD, roll_half(even), other)
+                z = roll_half(jnp.where(low_lanes, other, even))
+                held[a, 0:16, :, pl.ds(tail, LANES)] = jnp.where(low_lanes, even, z)
+                held[a, 16:32, :, pl.ds(tail, LANES)] = jnp.where(low_lanes, z, other)
             for q in range(CHUNKS):
                 rows = pl.ds(q * (32 // CHUNKS), 32 // CHUNKS)
                 copy = pltpu.make_async_copy(held.at[a, rows], outs[a].at[rows], sem.at[a * CHUNKS + q])
@@ -94,6 +97,23 @@
         copy.wait()
 
 
+def pair_rows(blocks, array):
+    parts = []
+    for part in (0, 1):
+        start = array * 128 + part * 64
+        parts.append(jnp.concatenate([b[start : start + 64, :] for b in blocks], axis=0))
+    return jnp.concatenate(parts, axis=1)
+
+
+def single_rows(blocks, array):
+    start = 512 + array * 64
+    return jnp.concatenate([b[start : start + 64, :] for b in blocks], axis=0)
+
+
+def first_head(shape):
+    return (iota(shape, 1) & HEAD) == 0
+
+
 def row_group(blocks, array, part):
     start = array * 128 + part * 64 if part < 2 else 512 + array * 64
     return jnp.concatenate([b[start : start + 64, :] for b in blocks], axis=0)
@@ -103,7 +123,8 @@
     return ((iota(shape, 0) >> 2) & 15) == ((iota(shape, 1) >> 2) & 15)
 
 
-def row_score_kernel(b2, b3, b1, b0, out):
+def row_score_kernel(b3, b2, b1, b0, after0, after1, out):
+    del after0, after1
     blocks = (b0, b1, b2, b3)
     lane = iota((256, LANES), 1)
     mask = same_sequence((256, 256))
@@ -142,40 +163,39 @@
     out[...] = result
 
 
-def row_grad_kernel(row_scale, p0, p1, p2, p3, b2, b3, b1, b0, *outs):
+def row_grad_kernel(row_scale, p0, p1, p2, p3, b2, b3, b1, b0, after, *outs):
+    del after
+    outs[4][...] = jnp.zeros_like(outs[4])
     blocks = (b0, b1, b2, b3)
     total = (p0[...] + p1[...]) + (p2[...] + p3[...])
-    lane = iota((256, LANES), 1)
-    mask = same_sequence((256, 256))
-    row = iota((256, 16), 0)
-    spread = (iota((256, 16), 1) == ((row >> 6) << 2) + (row & 3)).astype(BF16)
-
-    def expand(small, transposed):
-        half = (nt if transposed else nn)(spread, small).astype(BF16)
-        return jnp.where(mask, nt(half, spread), 0.0).astype(BF16)
-
-    mats = []
+    dscores, weights = [], []
     for h in range(3):
         scores = total[:, 16 * h : 16 * h + 16] * row_scale
         dprob = total[:, 48 + 16 * h : 64 + 16 * h]
         e = jnp.exp(scores - jnp.max(scores, axis=1, keepdims=True))
         probs = e / jnp.sum(e, axis=1, keepdims=True)
         delta = jnp.sum(probs * dprob, axis=1, keepdims=True)
-        dscore = (probs * (dprob - delta) * row_scale).astype(BF16)
-        weights = probs.astype(BF16)
-        mats.append((expand(dscore, False), expand(dscore, True), expand(weights, True)))
+        dscores.append((probs * (dprob - delta) * row_scale).astype(BF16))
+        weights.append(probs.astype(BF16))
+    row = iota((256, 16), 0)
+    spread = (iota((256, 16), 1) == ((row >> 6) << 2) + (row & 3)).astype(BF16)
+    shape = (256, 256)
+    mask = ((iota(shape, 0) >> 2) & 15) == ((iota(shape, 1) >> 2) & 15)
+    keep = first_head(shape)
+    plain = nn(spread, jnp.concatenate(dscores, axis=1)).astype(BF16)
+    turned = nt(spread, jnp.concatenate(dscores + weights, axis=0)).astype(BF16)
     for k, array in enumerate((1, 0, 2)):
-        for part in (0, 1, 2):
-            x = row_group(blocks, array, part)
-            if part < 2:
-                y = jnp.where(lane < HEAD, nn(mats[0][k], x), nn(mats[1][k], x))
-                start = k * 128 + part * 64
-            else:
-                y = nn(mats[2][k], x)
-                start = 384 + k * 64
-            y = y.astype(BF16)
-            for d in range(4):
-                outs[d][start : start + 64, :] = y[d * 64 : (d + 1) * 64, :]
+        mats = []
+        for h in range(3):
+            half = plain[:, 16 * h : 16 * h + 16] if k == 0 else turned[:, 48 * k - 48 + 16 * h : 48 * k - 32 + 16 * h]
+            mats.append(jnp.where(mask, nt(half, spread), 0.0).astype(BF16))
+        x = pair_rows(blocks, array)
+        y = jnp.where(keep, nn(mats[0], x), nn(mats[1], x)).astype(BF16)
+        z = nn(mats[2], single_rows(blocks, array)).astype(BF16)
+        for n in range(4):
+            outs[n][k * 128 : k * 128 + 64, :] = y[n * 64 : (n + 1) * 64, :LANES]
+            outs[n][k * 128 + 64 : k * 128 + 128, :] = y[n * 64 : (n + 1) * 64, LANES:]
+            outs[n][384 + k * 64 : 448 + k * 64, :] = z[n * 64 : (n + 1) * 64, :]
 
 
 def reorder(rows, inner):
@@ -196,44 +216,34 @@
     return (r == source).astype(BF16)
 
 
-def column_kernel(col_scale, b2, b3, b1, b0, after, o0, o1, o2, o3, work, grads):
-    blocks, outs = (b0, b1, b2, b3), (o0, o1, o2, o3)
-    del after
-    pair_order, single_order = reorder(128, 32), reorder(128, 16)
-    for d in range(4):
-        x = [blocks[d][a * 128 : (a + 1) * 128, :] for a in range(6)]
-        for a in (0, 2):
-            y = nn(pair_order, jnp.concatenate([x[a], x[a + 1]], axis=1)).astype(BF16)
-            work[d, a * 128 : (a + 1) * 128, :] = y[:, :LANES]
-            work[d, (a + 1) * 128 : (a + 2) * 128, :] = y[:, LANES:]
-        y = nn(single_order, jnp.concatenate([x[4], x[5]], axis=1)).astype(BF16)
-        work[d, 512:640, :] = y[:, :LANES]
-        work[d, 640:768, :] = y[:, LANES:]
+def column_core_pair(col_scale, query, key, value, grad):
+    heads = key.shape[0] // 128
+    shape = (heads, 128, 128)
+    scores = (nt(key, query) * col_scale).reshape(shape)
+    dprob = nt(value, grad).reshape(shape)
+    e = jnp.exp(scores - jnp.max(scores, axis=1, keepdims=True))
+    probs = e * (1.0 / jnp.sum(e, axis=1, keepdims=True))
+    delta = jnp.sum(probs * dprob, axis=1, keepdims=True)
+    dscore = (probs * (dprob - delta) * col_scale).astype(BF16).reshape(heads * 128, 128)
+    weights = probs.astype(BF16).reshape(heads * 128, 128)
+    return tn(dscore, key), nn(dscore, query), nn(weights, grad)
+
+
+def both(x):
+    lane = iota(x.shape, 1)
+    zero = jnp.zeros_like(x)
+    return jnp.concatenate([jnp.where(lane < HEAD, x, zero), jnp.where(lane < HEAD, zero, x)], axis=0)
+
+
+def column_grads(col_scale, columns, work, grads):
     lane = iota((128, LANES), 1)
-
-    def core(query, key, value, grad):
-        heads = key.shape[0] // 128
-        shape = (heads, 128, 128)
-        scores = (nt(key, query) * col_scale).reshape(shape)
-        dprob = nt(value, grad).reshape(shape)
-        e = jnp.exp(scores - jnp.max(scores, axis=1, keepdims=True))
-        probs = e * (1.0 / jnp.sum(e, axis=1, keepdims=True))
-        delta = jnp.sum(probs * dprob, axis=1, keepdims=True)
-        dscore = (probs * (dprob - delta) * col_scale).astype(BF16).reshape(heads * 128, 128)
-        weights = probs.astype(BF16).reshape(heads * 128, 128)
-        return tn(dscore, key), nn(dscore, query), nn(weights, grad)
-
-    def both(x):
-        zero = jnp.zeros_like(x)
-        return jnp.concatenate([jnp.where(lane < HEAD, x, zero), jnp.where(lane < HEAD, zero, x)], axis=0)
-
-    for c in range(4):
+    for c in columns:
         x = []
         for a in range(4):
             start = a * 128 + c * 32
             x.append(jnp.concatenate([work[d, start : start + 32, :] for d in range(4)], axis=0))
         query, key, grad, value = x
-        dquery, dkey, dvalue = core(query, both(key), both(value), grad)
+        dquery, dkey, dvalue = column_core_pair(col_scale, query, both(key), both(value), grad)
         dkey = jnp.where(lane < HEAD, dkey[:128], dkey[128:])
         dvalue = jnp.where(lane < HEAD, dvalue[:128], dvalue[128:])
         for k, y in enumerate((dquery, dkey, dvalue)):
@@ -246,34 +256,70 @@
             y = jnp.concatenate([work[d, start : start + 16, :] for d in range(4)], axis=0)
             x.append(jnp.concatenate([y[:, :HEAD], y[:, HEAD:]], axis=0))
         query, key, grad, value = x
-        for k, y in enumerate(core(query, key, value, grad)):
+        for k, y in enumerate(column_core_pair(col_scale, query, key, value, grad)):
             y = jnp.concatenate([y[:64], y[64:]], axis=1).astype(BF16)
             for d in range(4):
                 start = 384 + k * 64 + c * 16
                 grads[d, start : start + 16, :] = y[d * 16 : (d + 1) * 16, :]
+
+
+def column_first_kernel(col_scale, b2, b3, b1, b0, after, work, grads):
+    del after
+    blocks = (b0, b1, b2, b3)
+    pair_order, single_order = reorder(128, 32), reorder(128, 16)
+    for d in range(4):
+        x = [blocks[d][a * 128 : (a + 1) * 128, :] for a in range(6)]
+        for a in (0, 2):
+            y = nn(pair_order, jnp.concatenate([x[a], x[a + 1]], axis=1)).astype(BF16)
+            work[d, a * 128 : (a + 1) * 128, :] = y[:, :LANES]
+            work[d, (a + 1) * 128 : (a + 2) * 128, :] = y[:, LANES:]
+        y = nn(single_order, jnp.concatenate([x[4], x[5]], axis=1)).astype(BF16)
+        work[d, 512:640, :] = y[:, :LANES]
+        work[d, 640:768, :] = y[:, LANES:]
+    column_grads(col_scale, FIRST_COLUMNS, work, grads)
+
+
+def joined(first, second, d, start, size, split):
+    middle, stop = start + split * size, start + 4 * size
+    return jnp.concatenate([first[d, start:middle, :], second[d, middle:stop, :]], axis=0)
+
+
+def column_second_kernel(col_scale, work, first, after, o0, o1, o2, o3, grads):
+    del after
+    outs = (o0, o1, o2, o3)
+    column_grads(col_scale, SECOND_COLUMNS, work, grads)
+    split = len(FIRST_COLUMNS)
     pair_back, single_back = restore(128, 32), restore(64, 16)
     for d in range(4):
-        x = [grads[d, k * 128 : (k + 1) * 128, :] for k in range(3)]
+        x = [joined(first, grads, d, k * 128, 32, split) for k in range(3)]
         y = nn(pair_back, jnp.concatenate(x, axis=1)).astype(BF16)
         for k in range(3):
             outs[d][k * 128 : (k + 1) * 128, :] = y[:, k * LANES : (k + 1) * LANES]
-        x = [grads[d, 384 + k * 64 : 448 + k * 64, :] for k in range(3)]
+        x = [joined(first, grads, d, 384 + k * 64, 16, split) for k in range(3)]
         y = nn(single_back, jnp.concatenate(x, axis=1)).astype(BF16)
         for k in range(3):
             outs[d][384 + k * 64 : 448 + k * 64, :] = y[:, k * LANES : (k + 1) * LANES]
 
 
+def tick_kernel(*refs):
+    refs[-1][...] = jnp.zeros_like(refs[-1])
+
+
 VMEM = pl.BlockSpec(memory_space=pltpu.VMEM)
+ANY = pl.BlockSpec(memory_space=pl.ANY)
 HBM = pl.BlockSpec(memory_space=pltpu.HBM)
 LIMIT = 40 * 1024 * 1024
 ROW = 1
-CHUNKS = 4
+TICK = 20_000_000_000
+CHUNKS = 2
+FIRST_COLUMNS = (0, 1)
+SECOND_COLUMNS = (2, 3)
 COL = 4_000_000_000
 SHIFTS = (2, 3, 1)
 
 
 def call(body, shapes, operands, name, flops, scratch=(), in_space=VMEM, out_space=VMEM):
-    return pl.pallas_call(
+    kernel = pl.pallas_call(
         body,
         out_shape=[jax.ShapeDtypeStruct(shape, dtype) for shape, dtype in shapes],
         in_specs=in_space if isinstance(in_space, list) else [in_space] * len(operands),
@@ -282,16 +328,21 @@
         compiler_params=pltpu.CompilerParams(vmem_limit_bytes=LIMIT),
         cost_estimate=pl.CostEstimate(flops=flops, bytes_accessed=1, transcendentals=0),
         name=name,
-    )(*operands)
+    )
+    return list(kernel(*operands))
 
 
 def far_first(blocks):
     return [blocks[2], blocks[3], blocks[1], blocks[0]]
 
 
-def exchange(blocks, axis):
+def near_first(blocks):
+    return [blocks[1], blocks[2], blocks[3], blocks[0]]
+
+
+def exchange(blocks, axis, shifts=SHIFTS):
     moved = list(blocks)
-    for d in SHIFTS:
+    for d in shifts:
         moved[d] = lax.ppermute(blocks[d], axis, [(i, i ^ d) for i in range(4)])
     return moved
 
@@ -299,14 +350,18 @@
 def pack(arrays, axis, name):
     arrays = [pltpu.with_memory_space_constraint(x, pltpu.HBM) for x in arrays]
     scratch = (pltpu.VMEM((4, *arrays[0].shape), BF16), pltpu.SemaphoreType.DMA((4 * CHUNKS,)))
-    blocks = call(
-        functools.partial(pack_kernel, axis), [((192, 4, LANES), BF16)] * 4, arrays, name, 1, scratch, in_space=HBM
-    )
+    shapes = [((192, 4, LANES), BF16)] * 4
+    blocks = call(functools.partial(pack_kernel, axis), shapes, arrays, name, 1, scratch, in_space=HBM)
     return [b.reshape(768, LANES) for b in blocks]
 
 
-def unpack(row_back, col_back, shape):
-    operands = [b.reshape(144, 4, LANES) for b in far_first(row_back) + far_first(col_back)]
+def tick(operands, name, flops):
+    return call(tick_kernel, [((8, LANES), F32)], operands, name, flops, in_space=ANY)
+
+
+def unpack(row_back, col_back, after, shape):
+    operands = [b.reshape(144, 4, LANES) for b in [row_back[d] for d in (1, 3, 2, 0)] + far_first(col_back)]
+    operands += after
     scratch = (pltpu.VMEM((6, *shape), BF16), pltpu.SemaphoreType.DMA((6 * CHUNKS,)))
     return call(unpack_kernel, [(shape, BF16)] * 6, operands, "unpack", 1, scratch, out_space=HBM)
 
@@ -320,27 +375,34 @@
     row_blocks = exchange(row_blocks, "col")
     col_blocks = pack((col_query, col_key, col_grad, col_value), "seq", "col_pack")
     col_blocks = exchange(col_blocks, "seq")
-    (part,) = call(row_score_kernel, [((16, LANES), F32)], far_first(row_blocks), "row_scores", ROW)
+    (part,) = call(row_score_kernel, [((16, LANES), F32)], [row_blocks[d] for d in (3, 2, 1, 0)] + far_first(col_blocks)[:2], "row_scores", ROW)
     parts = exchange([part] * 4, "seq")
-    col_out = call(
-        functools.partial(column_kernel, col_scale),
-        [((576, LANES), BF16)] * 4,
+    col_work, col_first = call(
+        functools.partial(column_first_kernel, col_scale),
+        [((4, 768, LANES), BF16), ((4, 576, LANES), BF16)],
         [*far_first(col_blocks), part],
-        "col_grads",
+        "col_grads_first",
         COL,
-        scratch=(pltpu.VMEM((4, 768, LANES), BF16), pltpu.VMEM((4, 576, LANES), BF16)),
-    )
-    row_out = call(
+    )
+    *row_out, token = call(
         functools.partial(row_grad_kernel, row_scale),
-        [((576, LANES), BF16)] * 4,
-        parts + far_first(row_blocks),
+        [((576, LANES), BF16)] * 4 + [((8, LANES), F32)],
+        parts + far_first(row_blocks) + [col_first],
         "row_grads",
         ROW,
     )
-    row_out, col_out = lax.optimization_barrier((row_out, col_out))
-    row_back = exchange(row_out, "col")
+    row_back = exchange(row_out, "col", (1, 2, 3))
+    col_out = call(
+        functools.partial(column_second_kernel, col_scale),
+        [((576, LANES), BF16)] * 4,
+        [col_work, col_first, token],
+        "col_grads_second",
+        COL,
+        scratch=(pltpu.VMEM((4, 576, LANES), BF16),),
+    )
     col_back = exchange(col_out, "seq")
-    return unpack(row_back, col_back, shape)
+    arrived = tick(far_first(row_back)[:3], "row_arrived", TICK)
+    return tuple(unpack(row_back, col_back, arrived, shape))
 
 
 def tied_terms(scores, prob_grad, row_scale):

time: 49.1 us -> 47.1 us (0.959)
  Pallas kernels: 11.9 us -> 10.3 us
  waiting for transfers between devices: 21.8 us -> 21.3 us
    pallas_call x6 -> x8, Pallas kernels: 11.9 us -> 10.3 us  [call(): return list(kernel(*operands))]
  transfers between devices with their start and end apart: 15 -> 15, of which waited for: 4 -> 6; matrix products, arithmetic and copies ran while one was open for 0% -> 0% of each run, Pallas kernels for 12% -> 13%
where the time goes in v3:
time: 47.1 us; the launch traced here: 46.9 us
  waiting for transfers between devices  21.3 us (45%)
  starting transfers between devices  14.6 us (31%)
  Pallas kernels  10.3 us (22%)
  between operations  0.71 us (2%)
    ppermute x15, waiting for transfers between devices, exchange(): moved[d] = lax.ppermute(blocks[d], axis, [(i, i ^ d) for i in range(4)])  21.3 us
    ppermute x15, starting transfers between devices, exchange(): moved[d] = lax.ppermute(blocks[d], axis, [(i, i ^ d) for i in range(4)])  14.6 us
    pallas_call x8, Pallas kernels, call(): return list(kernel(*operands))  10.3 us
  transfers between devices with their start and end apart: 15, of which 6 were waited for; matrix products, arithmetic and copies ran while one was open for 0% of the time, Pallas kernels for 13%

profile of v3, /device:TPU:0, one launch (start us, length us, event | category | flops | bytes accessed | tf_op | source)
XLA Modules:
  0.0 46.9 jit_solution(14811917207124199076)
XLA Ops:
  0.6 1.6 %row_pack.1 = (bf16[192,4,128]{2,1,0:T(4,128)(2,1)S(1)}, bf16[192,4,128]{2,1,0:T(4,128)(2,1)S(1)}, bf16[192,4,128]{2,1,0:T(4,128)(2,1)S(1)}, bf16[192,4,128]{2,1,0:T(4,128)(2,1)S(1)}) custom-call(bf16[32,4,768]{2,1,0:T(4,128)(2,1)} %refs_0_.2, bf16[32,4,768]{2,1,0:T(4,128)(2,1)} %refs_1_.2, bf16[32,4,768]{2,1,0:T(4,128)(2,1)} %refs_2_.2, ...), custom_call_target="tpu_custom_call" | custom-call | flops 1 | bytes 1 | tf_op jit(solution)/shard_map/row_pack/pallas_call | solution.py:332
  2.2 5.1 %collective-permute-start = (bf16[768,128]{1,0:T(8,128)(2,1)S(1)}, bf16[768,128]{1,0:T(8,128)(2,1)S(1)}, u32[]{:S(2)}, u32[]{:S(2)}) collective-permute-start(bf16[768,128]{1,0:T(8,128)(2,1)S(1)} %bitcast.31), channel_id=1, source_target_pairs={{0,12},{4,8},{8,4},{12,0},{1,13},{5,9},{9,5},{13,1},{2,14},{6,10},... | collective-permute-start | bytes 589832 | tf_op jit(solution)/shard_map/ppermute | solution.py:346
  7.4 0.6 %collective-permute-start.2 = (bf16[768,128]{1,0:T(8,128)(2,1)S(1)}, bf16[768,128]{1,0:T(8,128)(2,1)S(1)}, u32[]{:S(2)}, u32[]{:S(2)}) collective-permute-start(bf16[768,128]{1,0:T(8,128)(2,1)S(1)} %bitcast.28), channel_id=1, source_target_pairs={{0,4},{4,0},{8,12},{12,8},{1,5},{5,1},{9,13},{13,9},{2,6},{6,2},{1... | collective-permute-start | bytes 589832 | tf_op jit(solution)/shard_map/ppermute | solution.py:346
  8.0 1.6 %col_pack.1 = (bf16[192,4,128]{2,1,0:T(4,128)(2,1)S(1)}, bf16[192,4,128]{2,1,0:T(4,128)(2,1)S(1)}, bf16[192,4,128]{2,1,0:T(4,128)(2,1)S(1)}, bf16[192,4,128]{2,1,0:T(4,128)(2,1)S(1)}) custom-call(bf16[32,4,768]{2,1,0:T(4,128)(2,1)} %refs_0_.3, bf16[32,4,768]{2,1,0:T(4,128)(2,1)} %refs_1_.3, bf16[32,4,768]{2,1,0:T(4,128)(2,1)} %refs_2_.3, ...), custom_call_target="tpu_custom_call" | custom-call | flops 1 | bytes 1 | tf_op jit(solution)/shard_map/col_pack/pallas_call | solution.py:332
  9.6 1.7 %collective-permute-start.3 = (bf16[768,128]{1,0:T(8,128)(2,1)S(1)}, bf16[768,128]{1,0:T(8,128)(2,1)S(1)}, u32[]{:S(2)}, u32[]{:S(2)}) collective-permute-start(bf16[768,128]{1,0:T(8,128)(2,1)S(1)} %bitcast.32), channel_id=1, source_target_pairs={{0,2},{1,3},{2,0},{3,1},{4,6},{5,7},{6,4},{7,5},{8,10},{9,11},{10,... | collective-permute-start | bytes 589832 | tf_op jit(solution)/shard_map/ppermute | solution.py:346
  11.3 0.0 collective-permute-start.4
  11.3 1.9 %collective-permute-done.b3 = bf16[768,128]{1,0:T(8,128)(2,1)S(1)} collective-permute-done((bf16[768,128]{1,0:T(8,128)(2,1)S(1)}, bf16[768,128]{1,0:T(8,128)(2,1)S(1)}, u32[]{:S(2)}, u32[]{:S(2)}) %collective-permute-start) | collective-permute-done | bytes 196640 | tf_op jit(solution)/shard_map/ppermute | solution.py:346
  13.2 0.0 collective-permute-start.8
  13.2 10.8 %collective-permute-done.1.b2 = bf16[768,128]{1,0:T(8,128)(2,1)S(1)} collective-permute-done((bf16[768,128]{1,0:T(8,128)(2,1)S(1)}, bf16[768,128]{1,0:T(8,128)(2,1)S(1)}, u32[]{:S(2)}, u32[]{:S(2)}) %collective-permute-start.1) | collective-permute-done | bytes 196640 | tf_op jit(solution)/shard_map/ppermute | solution.py:346
  24.1 0.8 %row_scores.1.after.p0 = f32[16,128]{1,0:T(8,128)S(1)} custom-call(bf16[768,128]{1,0:T(8,128)(2,1)S(1)} %collective-permute-done.b3, bf16[768,128]{1,0:T(8,128)(2,1)S(1)} %collective-permute-done.1.b2, bf16[768,128]{1,0:T(8,128)(2,1)S(1)} %collective-permute-done.2.b1, bf16[768,128]{1,0:T(8,128)(2,1)S(1)} %bitcast.16, ...), custom_call_target="tpu_custom_call" | custom-call | flops 1 | bytes 1 | tf_op jit(solution)/shard_map/row_scores/pallas_call | solution.py:332
  24.9 1.5 %collective-permute-start.6 = (f32[16,128]{1,0:T(8,128)S(1)}, f32[16,128]{1,0:T(8,128)S(1)}, u32[]{:S(2)}, u32[]{:S(2)}) collective-permute-start(f32[16,128]{1,0:T(8,128)S(1)} %row_scores.1.after.p0), channel_id=1, source_target_pairs={{0,2},{1,3},{2,0},{3,1},{4,6},{5,7},{6,4},{7,5},{8,10},{9,11},{10,... | collective-permute-start | bytes 24584 | tf_op jit(solution)/shard_map/ppermute | solution.py:346
  26.4 0.3 collective-permute-start.7
  26.8 1.7 %col_grads_first.1 = (bf16[4,768,128]{2,1,0:T(8,128)(2,1)S(1)}, bf16[4,576,128]{2,1,0:T(8,128)(2,1)S(1)}) custom-call(bf16[768,128]{1,0:T(8,128)(2,1)S(1)} %collective-permute-done.3.after0.b2, bf16[768,128]{1,0:T(8,128)(2,1)S(1)} %collective-permute-done.4.after1.b3, bf16[768,128]{1,0:T(8,128)(2,1)S(1)} %collective-permute-done.8.b1, ...), custom_call_target="tpu_custom_call" | custom-call | flops 4000000000 | bytes 1 | tf_op jit(solution)/shard_map/col_grads_first/pallas_call | solution.py:332
  28.5 0.1 collective-permute-done.6.p2
  28.6 0.9 %collective-permute-done.7.p3 = f32[16,128]{1,0:T(8,128)S(1)} collective-permute-done((f32[16,128]{1,0:T(8,128)S(1)}, f32[16,128]{1,0:T(8,128)S(1)}, u32[]{:S(2)}, u32[]{:S(2)}) %collective-permute-start.7) | collective-permute-done | bytes 8224 | tf_op jit(solution)/shard_map/ppermute | solution.py:346
  29.5 1.4 %row_grads.1 = (bf16[576,128]{1,0:T(8,128)(2,1)S(1)}, bf16[576,128]{1,0:T(8,128)(2,1)S(1)}, bf16[576,128]{1,0:T(8,128)(2,1)S(1)}, bf16[576,128]{1,0:T(8,128)(2,1)S(1)}, f32[8,128]{1,0:T(8,128)S(1)}) custom-call(f32[16,128]{1,0:T(8,128)S(1)} %row_scores.1.after.p0, f32[16,128]{1,0:T(8,128)S(1)} %collective-permute-done.5.p1, ...), custom_call_target="tpu_custom_call" | custom-call | flops 1 | bytes 1 | tf_op jit(solution)/shard_map/row_grads/pallas_call | solution.py:332
  30.9 2.5 %collective-permute-start.10 = (bf16[576,128]{1,0:T(8,128)(2,1)S(1)}, bf16[576,128]{1,0:T(8,128)(2,1)S(1)}, u32[]{:S(2)}, u32[]{:S(2)}) collective-permute-start(bf16[576,128]{1,0:T(8,128)(2,1)S(1)} %get-tuple-element.35), channel_id=1, source_target_pairs={{0,12},{4,8},{8,4},{12,0},{1,13},{5,9},{9,5},{13,1},{2,14},{6,10},... | collective-permute-start | bytes 442376 | tf_op jit(solution)/shard_map/ppermute | solution.py:346
  33.5 1.9 %collective-permute-start.9 = (bf16[576,128]{1,0:T(8,128)(2,1)S(1)}, bf16[576,128]{1,0:T(8,128)(2,1)S(1)}, u32[]{:S(2)}, u32[]{:S(2)}) collective-permute-start(bf16[576,128]{1,0:T(8,128)(2,1)S(1)} %get-tuple-element.34), channel_id=1, source_target_pairs={{0,4},{4,0},{8,12},{12,8},{1,5},{5,1},{9,13},{13,9},{2,6},{6,2},{1... | collective-permute-start | bytes 442376 | tf_op jit(solution)/shard_map/ppermute | solution.py:346
  35.4 1.8 %col_grads_second.1 = (bf16[576,128]{1,0:T(8,128)(2,1)S(1)}, bf16[576,128]{1,0:T(8,128)(2,1)S(1)}, bf16[576,128]{1,0:T(8,128)(2,1)S(1)}, bf16[576,128]{1,0:T(8,128)(2,1)S(1)}) custom-call(bf16[4,768,128]{2,1,0:T(8,128)(2,1)S(1)} %get-tuple-element.38.work, bf16[4,576,128]{2,1,0:T(8,128)(2,1)S(1)} %get-tuple-element.33.after.first, ...), custom_call_target="tpu_custom_call" | custom-call | flops 4000000000 | bytes 1 | tf_op jit(solution)/shard_map/col_grads_second/pallas_call | solution.py:332
  37.1 0.7 %collective-permute-start.12 = (bf16[576,128]{1,0:T(8,128)(2,1)S(1)}, bf16[576,128]{1,0:T(8,128)(2,1)S(1)}, u32[]{:S(2)}, u32[]{:S(2)}) collective-permute-start(bf16[576,128]{1,0:T(8,128)(2,1)S(1)} %get-tuple-element.40), channel_id=1, source_target_pairs={{0,2},{1,3},{2,0},{3,1},{4,6},{5,7},{6,4},{7,5},{8,10},{9,11},{10,... | collective-permute-start | bytes 442376 | tf_op jit(solution)/shard_map/ppermute | solution.py:346
  37.8 0.1 collective-permute-start.13
  37.9 1.7 %collective-permute-done.10.refs_1_ = bf16[576,128]{1,0:T(8,128)(2,1)S(1)} collective-permute-done((bf16[576,128]{1,0:T(8,128)(2,1)S(1)}, bf16[576,128]{1,0:T(8,128)(2,1)S(1)}, u32[]{:S(2)}, u32[]{:S(2)}) %collective-permute-start.10) | collective-permute-done | bytes 147488 | tf_op jit(solution)/shard_map/ppermute | solution.py:346
  39.6 5.9 %collective-permute-done.11.refs_0_ = bf16[576,128]{1,0:T(8,128)(2,1)S(1)} collective-permute-done((bf16[576,128]{1,0:T(8,128)(2,1)S(1)}, bf16[576,128]{1,0:T(8,128)(2,1)S(1)}, u32[]{:S(2)}, u32[]{:S(2)}) %collective-permute-start.11) | collective-permute-done | bytes 147488 | tf_op jit(solution)/shard_map/ppermute | solution.py:346
  45.5 1.4 %unpack.1 = (bf16[32,4,768]{2,1,0:T(4,128)(2,1)}, bf16[32,4,768]{2,1,0:T(4,128)(2,1)}, bf16[32,4,768]{2,1,0:T(4,128)(2,1)}, bf16[32,4,768]{2,1,0:T(4,128)(2,1)},...) custom-call(bf16[144,4,128]{2,1,0:T(4,128)(2,1)S(1)} %bitcast.21, bf16[144,4,128]{2,1,0:T(4,128)(2,1)S(1)} %bitcast.19, ...), custom_call_target="tpu_custom_call" | custom-call | flops 1 | bytes 1 | tf_op jit(solution)/shard_map/unpack/pallas_call | solution.py:332
  (14 shorter events, 0.0 us)
Async XLA Ops:
  2.2 11.0 %collective-permute-start = (bf16[768,128]{1,0:T(8,128)(2,1)S(1)}, bf16[768,128]{1,0:T(8,128)(2,1)S(1)}, u32[]{:S(2)}, u32[]{:S(2)}) collective-permute-start(bf16[768,128]{1,0:T(8,128)(2,1)S(1)} %bitcast.31), channel_id=1, source_target_pairs={{0,12},{4,8},{8,4},{12,0},{1,13},{5,9},{9,5},{13,1},{2,14},{6,10},... | collective-permute-start | bytes 589832 | tf_op jit(solution)/shard_map/ppermute | solution.py:346
  7.4 16.7 %collective-permute-start.1 = (bf16[768,128]{1,0:T(8,128)(2,1)S(1)}, bf16[768,128]{1,0:T(8,128)(2,1)S(1)}, u32[]{:S(2)}, u32[]{:S(2)}) collective-permute-start(bf16[768,128]{1,0:T(8,128)(2,1)S(1)} %bitcast.29), channel_id=1, source_target_pairs={{0,8},{4,12},{8,0},{12,4},{1,9},{5,13},{9,1},{13,5},{2,10},{6,14},... | collective-permute-start | bytes 589832 | tf_op jit(solution)/shard_map/ppermute | solution.py:346
  7.4 16.7 %collective-permute-start.2 = (bf16[768,128]{1,0:T(8,128)(2,1)S(1)}, bf16[768,128]{1,0:T(8,128)(2,1)S(1)}, u32[]{:S(2)}, u32[]{:S(2)}) collective-permute-start(bf16[768,128]{1,0:T(8,128)(2,1)S(1)} %bitcast.28), channel_id=1, source_target_pairs={{0,4},{4,0},{8,12},{12,8},{1,5},{5,1},{9,13},{13,9},{2,6},{6,2},{1... | collective-permute-start | bytes 589832 | tf_op jit(solution)/shard_map/ppermute | solution.py:346
  9.6 14.4 %collective-permute-start.3 = (bf16[768,128]{1,0:T(8,128)(2,1)S(1)}, bf16[768,128]{1,0:T(8,128)(2,1)S(1)}, u32[]{:S(2)}, u32[]{:S(2)}) collective-permute-start(bf16[768,128]{1,0:T(8,128)(2,1)S(1)} %bitcast.32), channel_id=1, source_target_pairs={{0,2},{1,3},{2,0},{3,1},{4,6},{5,7},{6,4},{7,5},{8,10},{9,11},{10,... | collective-permute-start | bytes 589832 | tf_op jit(solution)/shard_map/ppermute | solution.py:346
  11.3 12.7 %collective-permute-start.4 = (bf16[768,128]{1,0:T(8,128)(2,1)S(1)}, bf16[768,128]{1,0:T(8,128)(2,1)S(1)}, u32[]{:S(2)}, u32[]{:S(2)}) collective-permute-start(bf16[768,128]{1,0:T(8,128)(2,1)S(1)} %bitcast.30), channel_id=1, source_target_pairs={{0,3},{1,2},{2,1},{3,0},{4,7},{5,6},{6,5},{7,4},{8,11},{9,10},{10,... | collective-permute-start | bytes 589832 | tf_op jit(solution)/shard_map/ppermute | solution.py:346
  13.2 13.5 %collective-permute-start.8 = (bf16[768,128]{1,0:T(8,128)(2,1)S(1)}, bf16[768,128]{1,0:T(8,128)(2,1)S(1)}, u32[]{:S(2)}, u32[]{:S(2)}) collective-permute-start(bf16[768,128]{1,0:T(8,128)(2,1)S(1)} %bitcast.27), channel_id=1, source_target_pairs={{0,1},{1,0},{2,3},{3,2},{4,5},{5,4},{6,7},{7,6},{8,9},{9,8},{10,11... | collective-permute-start | bytes 589832 | tf_op jit(solution)/shard_map/ppermute | solution.py:346
  24.9 3.6 %collective-permute-start.5 = (f32[16,128]{1,0:T(8,128)S(1)}, f32[16,128]{1,0:T(8,128)S(1)}, u32[]{:S(2)}, u32[]{:S(2)}) collective-permute-start(f32[16,128]{1,0:T(8,128)S(1)} %row_scores.1.after.p0), channel_id=1, source_target_pairs={{0,1},{1,0},{2,3},{3,2},{4,5},{5,4},{6,7},{7,6},{8,9},{9,8},{10,11... | collective-permute-start | bytes 24584 | tf_op jit(solution)/shard_map/ppermute | solution.py:346
  24.9 3.7 %collective-permute-start.6 = (f32[16,128]{1,0:T(8,128)S(1)}, f32[16,128]{1,0:T(8,128)S(1)}, u32[]{:S(2)}, u32[]{:S(2)}) collective-permute-start(f32[16,128]{1,0:T(8,128)S(1)} %row_scores.1.after.p0), channel_id=1, source_target_pairs={{0,2},{1,3},{2,0},{3,1},{4,6},{5,7},{6,4},{7,5},{8,10},{9,11},{10,... | collective-permute-start | bytes 24584 | tf_op jit(solution)/shard_map/ppermute | solution.py:346
  26.4 3.1 %collective-permute-start.7 = (f32[16,128]{1,0:T(8,128)S(1)}, f32[16,128]{1,0:T(8,128)S(1)}, u32[]{:S(2)}, u32[]{:S(2)}) collective-permute-start(f32[16,128]{1,0:T(8,128)S(1)} %row_scores.1.after.p0), channel_id=1, source_target_pairs={{0,3},{1,2},{2,1},{3,0},{4,7},{5,6},{6,5},{7,4},{8,11},{9,10},{10,... | collective-permute-start | bytes 24584 | tf_op jit(solution)/shard_map/ppermute | solution.py:346
  30.9 8.7 %collective-permute-start.10 = (bf16[576,128]{1,0:T(8,128)(2,1)S(1)}, bf16[576,128]{1,0:T(8,128)(2,1)S(1)}, u32[]{:S(2)}, u32[]{:S(2)}) collective-permute-start(bf16[576,128]{1,0:T(8,128)(2,1)S(1)} %get-tuple-element.35), channel_id=1, source_target_pairs={{0,12},{4,8},{8,4},{12,0},{1,13},{5,9},{9,5},{13,1},{2,14},{6,10},... | collective-permute-start | bytes 442376 | tf_op jit(solution)/shard_map/ppermute | solution.py:346
  33.5 12.0 %collective-permute-start.11 = (bf16[576,128]{1,0:T(8,128)(2,1)S(1)}, bf16[576,128]{1,0:T(8,128)(2,1)S(1)}, u32[]{:S(2)}, u32[]{:S(2)}) collective-permute-start(bf16[576,128]{1,0:T(8,128)(2,1)S(1)} %get-tuple-element.36), channel_id=1, source_target_pairs={{0,8},{4,12},{8,0},{12,4},{1,9},{5,13},{9,1},{13,5},{2,10},{6,14},... | collective-permute-start | bytes 442376 | tf_op jit(solution)/shard_map/ppermute | solution.py:346
  33.5 12.0 %collective-permute-start.9 = (bf16[576,128]{1,0:T(8,128)(2,1)S(1)}, bf16[576,128]{1,0:T(8,128)(2,1)S(1)}, u32[]{:S(2)}, u32[]{:S(2)}) collective-permute-start(bf16[576,128]{1,0:T(8,128)(2,1)S(1)} %get-tuple-element.34), channel_id=1, source_target_pairs={{0,4},{4,0},{8,12},{12,8},{1,5},{5,1},{9,13},{13,9},{2,6},{6,2},{1... | collective-permute-start | bytes 442376 | tf_op jit(solution)/shard_map/ppermute | solution.py:346
  37.1 8.4 %collective-permute-start.12 = (bf16[576,128]{1,0:T(8,128)(2,1)S(1)}, bf16[576,128]{1,0:T(8,128)(2,1)S(1)}, u32[]{:S(2)}, u32[]{:S(2)}) collective-permute-start(bf16[576,128]{1,0:T(8,128)(2,1)S(1)} %get-tuple-element.40), channel_id=1, source_target_pairs={{0,2},{1,3},{2,0},{3,1},{4,6},{5,7},{6,4},{7,5},{8,10},{9,11},{10,... | collective-permute-start | bytes 442376 | tf_op jit(solution)/shard_map/ppermute | solution.py:346
  37.8 7.7 %collective-permute-start.13 = (bf16[576,128]{1,0:T(8,128)(2,1)S(1)}, bf16[576,128]{1,0:T(8,128)(2,1)S(1)}, u32[]{:S(2)}, u32[]{:S(2)}) collective-permute-start(bf16[576,128]{1,0:T(8,128)(2,1)S(1)} %get-tuple-element.41), channel_id=1, source_target_pairs={{0,3},{1,2},{2,1},{3,0},{4,7},{5,6},{6,5},{7,4},{8,11},{9,10},{10,... | collective-permute-start | bytes 442376 | tf_op jit(solution)/shard_map/ppermute | solution.py:346
  39.6 5.9 %collective-permute-start.14 = (bf16[576,128]{1,0:T(8,128)(2,1)S(1)}, bf16[576,128]{1,0:T(8,128)(2,1)S(1)}, u32[]{:S(2)}, u32[]{:S(2)}) collective-permute-start(bf16[576,128]{1,0:T(8,128)(2,1)S(1)} %get-tuple-element.42), channel_id=1, source_target_pairs={{0,1},{1,0},{2,3},{3,2},{4,5},{5,4},{6,7},{7,6},{8,9},{9,8},{10,11... | collective-permute-start | bytes 442376 | tf_op jit(solution)/shard_map/ppermute | solution.py:346

commit v4 on v3

--- a/solution.py
+++ b/solution.py
@@ -70,7 +70,7 @@
     copies = []
     for side, axis in ((1, "seq"), (0, "col")):
         blocks = refs[4 * side : 4 * side + 4]
-        blocks = (blocks[3], blocks[2], *blocks[:2]) if side else (blocks[3], blocks[0], blocks[2], blocks[1])
+        blocks = by_partner(blocks, (2, 3, 1, 0) if side else RETURN)
         me = lax.axis_index(axis)
         odd = (me & 1) == 1
         for k in range(3):
@@ -123,9 +123,13 @@
     return ((iota(shape, 0) >> 2) & 15) == ((iota(shape, 1) >> 2) & 15)
 
 
-def row_score_kernel(b3, b2, b1, b0, after0, after1, out):
+def by_partner(blocks, order):
+    return [blocks[order.index(d)] for d in range(4)]
+
+
+def row_score_kernel(r0, r1, r2, r3, after0, after1, out):
     del after0, after1
-    blocks = (b0, b1, b2, b3)
+    blocks = by_partner((r0, r1, r2, r3), ENTRY)
     lane = iota((256, LANES), 1)
     mask = same_sequence((256, 256))
     partials = []
@@ -163,7 +167,7 @@
     out[...] = result
 
 
-def row_grad_kernel(row_scale, p0, p1, p2, p3, b2, b3, b1, b0, after, *outs):
+def row_grad_kernel(row_scale, p2, p3, p1, p0, b2, b3, b1, b0, after, *outs):
     del after
     outs[4][...] = jnp.zeros_like(outs[4])
     blocks = (b0, b1, b2, b3)
@@ -312,9 +316,11 @@
 ROW = 1
 TICK = 20_000_000_000
 CHUNKS = 2
-FIRST_COLUMNS = (0, 1)
-SECOND_COLUMNS = (2, 3)
+FIRST_COLUMNS = (0,)
+SECOND_COLUMNS = (1, 2, 3)
 COL = 4_000_000_000
+ENTRY = (2, 1, 3, 0)
+RETURN = (1, 3, 2, 0)
 SHIFTS = (2, 3, 1)
 
 
@@ -360,7 +366,7 @@
 
 
 def unpack(row_back, col_back, after, shape):
-    operands = [b.reshape(144, 4, LANES) for b in [row_back[d] for d in (1, 3, 2, 0)] + far_first(col_back)]
+    operands = [b.reshape(144, 4, LANES) for b in [row_back[d] for d in RETURN] + far_first(col_back)]
     operands += after
     scratch = (pltpu.VMEM((6, *shape), BF16), pltpu.SemaphoreType.DMA((6 * CHUNKS,)))
     return call(unpack_kernel, [(shape, BF16)] * 6, operands, "unpack", 1, scratch, out_space=HBM)
@@ -375,7 +381,7 @@
     row_blocks = exchange(row_blocks, "col")
     col_blocks = pack((col_query, col_key, col_grad, col_value), "seq", "col_pack")
     col_blocks = exchange(col_blocks, "seq")
-    (part,) = call(row_score_kernel, [((16, LANES), F32)], [row_blocks[d] for d in (3, 2, 1, 0)] + far_first(col_blocks)[:2], "row_scores", ROW)
+    (part,) = call(row_score_kernel, [((16, LANES), F32)], [row_blocks[d] for d in ENTRY] + far_first(col_blocks)[:2], "row_scores", ROW)
     parts = exchange([part] * 4, "seq")
     col_work, col_first = call(
         functools.partial(column_first_kernel, col_scale),
@@ -387,7 +393,7 @@
     *row_out, token = call(
         functools.partial(row_grad_kernel, row_scale),
         [((576, LANES), BF16)] * 4 + [((8, LANES), F32)],
-        parts + far_first(row_blocks) + [col_first],
+        far_first(parts) + far_first(row_blocks) + [col_first],
         "row_grads",
         ROW,
     )

time: 47.1 us -> 45.8 us (0.972)
  waiting for transfers between devices: 21.3 us -> 16.5 us
  starting transfers between devices: 14.6 us -> 18.1 us
    ppermute x15, waiting for transfers between devices: 21.3 us -> 16.5 us  [exchange(): moved[d] = lax.ppermute(blocks[d], axis, [(i, i ^ d) for i in range(4)])]
    ppermute x15, starting transfers between devices: 14.6 us -> 18.1 us  [exchange(): moved[d] = lax.ppermute(blocks[d], axis, [(i, i ^ d) for i in range(4)])]
  transfers between devices with their start and end apart: 15 -> 15, of which waited for: 6 -> 5; matrix products, arithmetic and copies ran while one was open for 0% -> 0% of each run, Pallas kernels for 13% -> 13%
where the time goes in v4:
time: 45.8 us; the launch traced here: 45.6 us
  starting transfers between devices  18.1 us (40%)
  waiting for transfers between devices  16.5 us (36%)
  Pallas kernels  10.3 us (22%)
  between operations  0.7 us (2%)
    ppermute x15, starting transfers between devices, exchange(): moved[d] = lax.ppermute(blocks[d], axis, [(i, i ^ d) for i in range(4)])  18.1 us
    ppermute x15, waiting for transfers between devices, exchange(): moved[d] = lax.ppermute(blocks[d], axis, [(i, i ^ d) for i in range(4)])  16.5 us
    pallas_call x8, Pallas kernels, call(): return list(kernel(*operands))  10.3 us
  transfers between devices with their start and end apart: 15, of which 5 were waited for; matrix products, arithmetic and copies ran while one was open for 0% of the time, Pallas kernels for 13%

profile of v4, /device:TPU:0, one launch (start us, length us, event | category | flops | bytes accessed | tf_op | source)
XLA Modules:
  0.0 45.6 jit_solution(788387198703702202)
XLA Ops:
  0.6 1.6 %row_pack.1 = (bf16[192,4,128]{2,1,0:T(4,128)(2,1)S(1)}, bf16[192,4,128]{2,1,0:T(4,128)(2,1)S(1)}, bf16[192,4,128]{2,1,0:T(4,128)(2,1)S(1)}, bf16[192,4,128]{2,1,0:T(4,128)(2,1)S(1)}) custom-call(bf16[32,4,768]{2,1,0:T(4,128)(2,1)} %refs_0_.2, bf16[32,4,768]{2,1,0:T(4,128)(2,1)} %refs_1_.2, bf16[32,4,768]{2,1,0:T(4,128)(2,1)} %refs_2_.2, ...), custom_call_target="tpu_custom_call" | custom-call | flops 1 | bytes 1 | tf_op jit(solution)/shard_map/row_pack/pallas_call | solution.py:338
  2.2 4.1 %collective-permute-start = (bf16[768,128]{1,0:T(8,128)(2,1)S(1)}, bf16[768,128]{1,0:T(8,128)(2,1)S(1)}, u32[]{:S(2)}, u32[]{:S(2)}) collective-permute-start(bf16[768,128]{1,0:T(8,128)(2,1)S(1)} %bitcast.31), channel_id=1, source_target_pairs={{0,8},{4,12},{8,0},{12,4},{1,9},{5,13},{9,1},{13,5},{2,10},{6,14},... | collective-permute-start | bytes 589832 | tf_op jit(solution)/shard_map/ppermute | solution.py:352
  6.3 1.6 %collective-permute-start.1 = (bf16[768,128]{1,0:T(8,128)(2,1)S(1)}, bf16[768,128]{1,0:T(8,128)(2,1)S(1)}, u32[]{:S(2)}, u32[]{:S(2)}) collective-permute-start(bf16[768,128]{1,0:T(8,128)(2,1)S(1)} %bitcast.29), channel_id=1, source_target_pairs={{0,4},{4,0},{8,12},{12,8},{1,5},{5,1},{9,13},{13,9},{2,6},{6,2},{1... | collective-permute-start | bytes 589832 | tf_op jit(solution)/shard_map/ppermute | solution.py:352
  7.9 1.6 %col_pack.1 = (bf16[192,4,128]{2,1,0:T(4,128)(2,1)S(1)}, bf16[192,4,128]{2,1,0:T(4,128)(2,1)S(1)}, bf16[192,4,128]{2,1,0:T(4,128)(2,1)S(1)}, bf16[192,4,128]{2,1,0:T(4,128)(2,1)S(1)}) custom-call(bf16[32,4,768]{2,1,0:T(4,128)(2,1)} %refs_0_.3, bf16[32,4,768]{2,1,0:T(4,128)(2,1)} %refs_1_.3, bf16[32,4,768]{2,1,0:T(4,128)(2,1)} %refs_2_.3, ...), custom_call_target="tpu_custom_call" | custom-call | flops 1 | bytes 1 | tf_op jit(solution)/shard_map/col_pack/pallas_call | solution.py:338
  9.5 1.8 %collective-permute-start.3 = (bf16[768,128]{1,0:T(8,128)(2,1)S(1)}, bf16[768,128]{1,0:T(8,128)(2,1)S(1)}, u32[]{:S(2)}, u32[]{:S(2)}) collective-permute-start(bf16[768,128]{1,0:T(8,128)(2,1)S(1)} %bitcast.32), channel_id=1, source_target_pairs={{0,2},{1,3},{2,0},{3,1},{4,6},{5,7},{6,4},{7,5},{8,10},{9,11},{10,... | collective-permute-start | bytes 589832 | tf_op jit(solution)/shard_map/ppermute | solution.py:352
  11.3 5.9 %collective-permute-done.r0.b2 = bf16[768,128]{1,0:T(8,128)(2,1)S(1)} collective-permute-done((bf16[768,128]{1,0:T(8,128)(2,1)S(1)}, bf16[768,128]{1,0:T(8,128)(2,1)S(1)}, u32[]{:S(2)}, u32[]{:S(2)}) %collective-permute-start) | collective-permute-done | bytes 196640 | tf_op jit(solution)/shard_map/ppermute | solution.py:352
  17.2 3.7 %collective-permute-done.2.r2.b3 = bf16[768,128]{1,0:T(8,128)(2,1)S(1)} collective-permute-done((bf16[768,128]{1,0:T(8,128)(2,1)S(1)}, bf16[768,128]{1,0:T(8,128)(2,1)S(1)}, u32[]{:S(2)}, u32[]{:S(2)}) %collective-permute-start.2) | collective-permute-done | bytes 196640 | tf_op jit(solution)/shard_map/ppermute | solution.py:352
  20.9 0.8 %row_scores.1.after.p0 = f32[16,128]{1,0:T(8,128)S(1)} custom-call(bf16[768,128]{1,0:T(8,128)(2,1)S(1)} %collective-permute-done.r0.b2, bf16[768,128]{1,0:T(8,128)(2,1)S(1)} %collective-permute-done.1.r1.b1, bf16[768,128]{1,0:T(8,128)(2,1)S(1)} %collective-permute-done.2.r2.b3, bf16[768,128]{1,0:T(8,128)(2,1)S(1)} %bitcast.16, ...), custom_call_target="tpu_custom_call" | custom-call | flops 1 | bytes 1 | tf_op jit(solution)/shard_map/row_scores/pallas_call | solution.py:338
  21.7 1.5 %collective-permute-start.5 = (f32[16,128]{1,0:T(8,128)S(1)}, f32[16,128]{1,0:T(8,128)S(1)}, u32[]{:S(2)}, u32[]{:S(2)}) collective-permute-start(f32[16,128]{1,0:T(8,128)S(1)} %row_scores.1.after.p0), channel_id=1, source_target_pairs={{0,2},{1,3},{2,0},{3,1},{4,6},{5,7},{6,4},{7,5},{8,10},{9,11},{10,... | collective-permute-start | bytes 24584 | tf_op jit(solution)/shard_map/ppermute | solution.py:352
  23.2 0.0 collective-permute-start.6
  23.2 0.6 %collective-permute-start.7 = (f32[16,128]{1,0:T(8,128)S(1)}, f32[16,128]{1,0:T(8,128)S(1)}, u32[]{:S(2)}, u32[]{:S(2)}) collective-permute-start(f32[16,128]{1,0:T(8,128)S(1)} %row_scores.1.after.p0), channel_id=1, source_target_pairs={{0,1},{1,0},{2,3},{3,2},{4,5},{5,4},{6,7},{7,6},{8,9},{9,8},{10,11... | collective-permute-start | bytes 24584 | tf_op jit(solution)/shard_map/ppermute | solution.py:352
  23.9 0.0 collective-permute-done.8.b1
  23.9 1.1 %col_grads_first.1 = (bf16[4,768,128]{2,1,0:T(8,128)(2,1)S(1)}, bf16[4,576,128]{2,1,0:T(8,128)(2,1)S(1)}) custom-call(bf16[768,128]{1,0:T(8,128)(2,1)S(1)} %collective-permute-done.3.after0.b2, bf16[768,128]{1,0:T(8,128)(2,1)S(1)} %collective-permute-done.4.after1.b3, bf16[768,128]{1,0:T(8,128)(2,1)S(1)} %collective-permute-done.8.b1, ...), custom_call_target="tpu_custom_call" | custom-call | flops 4000000000 | bytes 1 | tf_op jit(solution)/shard_map/col_grads_first/pallas_call | solution.py:338
  25.0 0.4 collective-permute-done.5.p2
  25.4 0.9 %collective-permute-done.6.p3 = f32[16,128]{1,0:T(8,128)S(1)} collective-permute-done((f32[16,128]{1,0:T(8,128)S(1)}, f32[16,128]{1,0:T(8,128)S(1)}, u32[]{:S(2)}, u32[]{:S(2)}) %collective-permute-start.6) | collective-permute-done | bytes 8224 | tf_op jit(solution)/shard_map/ppermute | solution.py:352
  26.3 1.4 %row_grads.1 = (bf16[576,128]{1,0:T(8,128)(2,1)S(1)}, bf16[576,128]{1,0:T(8,128)(2,1)S(1)}, bf16[576,128]{1,0:T(8,128)(2,1)S(1)}, bf16[576,128]{1,0:T(8,128)(2,1)S(1)}, f32[8,128]{1,0:T(8,128)S(1)}) custom-call(f32[16,128]{1,0:T(8,128)S(1)} %collective-permute-done.5.p2, f32[16,128]{1,0:T(8,128)S(1)} %collective-permute-done.6.p3, ...), custom_call_target="tpu_custom_call" | custom-call | flops 1 | bytes 1 | tf_op jit(solution)/shard_map/row_grads/pallas_call | solution.py:338
  27.7 2.6 %collective-permute-start.10 = (bf16[576,128]{1,0:T(8,128)(2,1)S(1)}, bf16[576,128]{1,0:T(8,128)(2,1)S(1)}, u32[]{:S(2)}, u32[]{:S(2)}) collective-permute-start(bf16[576,128]{1,0:T(8,128)(2,1)S(1)} %get-tuple-element.35), channel_id=1, source_target_pairs={{0,12},{4,8},{8,4},{12,0},{1,13},{5,9},{9,5},{13,1},{2,14},{6,10},... | collective-permute-start | bytes 442376 | tf_op jit(solution)/shard_map/ppermute | solution.py:352
  30.3 3.2 %collective-permute-start.11 = (bf16[576,128]{1,0:T(8,128)(2,1)S(1)}, bf16[576,128]{1,0:T(8,128)(2,1)S(1)}, u32[]{:S(2)}, u32[]{:S(2)}) collective-permute-start(bf16[576,128]{1,0:T(8,128)(2,1)S(1)} %get-tuple-element.36), channel_id=1, source_target_pairs={{0,8},{4,12},{8,0},{12,4},{1,9},{5,13},{9,1},{13,5},{2,10},{6,14},... | collective-permute-start | bytes 442376 | tf_op jit(solution)/shard_map/ppermute | solution.py:352
  33.5 0.5 %collective-permute-start.9 = (bf16[576,128]{1,0:T(8,128)(2,1)S(1)}, bf16[576,128]{1,0:T(8,128)(2,1)S(1)}, u32[]{:S(2)}, u32[]{:S(2)}) collective-permute-start(bf16[576,128]{1,0:T(8,128)(2,1)S(1)} %get-tuple-element.34), channel_id=1, source_target_pairs={{0,4},{4,0},{8,12},{12,8},{1,5},{5,1},{9,13},{13,9},{2,6},{6,2},{1... | collective-permute-start | bytes 442376 | tf_op jit(solution)/shard_map/ppermute | solution.py:352
  34.0 2.4 %col_grads_second.1 = (bf16[576,128]{1,0:T(8,128)(2,1)S(1)}, bf16[576,128]{1,0:T(8,128)(2,1)S(1)}, bf16[576,128]{1,0:T(8,128)(2,1)S(1)}, bf16[576,128]{1,0:T(8,128)(2,1)S(1)}) custom-call(bf16[4,768,128]{2,1,0:T(8,128)(2,1)S(1)} %get-tuple-element.38.work, bf16[4,576,128]{2,1,0:T(8,128)(2,1)S(1)} %get-tuple-element.33.after.first, ...), custom_call_target="tpu_custom_call" | custom-call | flops 4000000000 | bytes 1 | tf_op jit(solution)/shard_map/col_grads_second/pallas_call | solution.py:338
  36.4 0.7 %collective-permute-start.12 = (bf16[576,128]{1,0:T(8,128)(2,1)S(1)}, bf16[576,128]{1,0:T(8,128)(2,1)S(1)}, u32[]{:S(2)}, u32[]{:S(2)}) collective-permute-start(bf16[576,128]{1,0:T(8,128)(2,1)S(1)} %get-tuple-element.40), channel_id=1, source_target_pairs={{0,2},{1,3},{2,0},{3,1},{4,6},{5,7},{6,4},{7,5},{8,10},{9,11},{10,... | collective-permute-start | bytes 442376 | tf_op jit(solution)/shard_map/ppermute | solution.py:352
  37.1 1.5 %collective-permute-start.14 = (bf16[576,128]{1,0:T(8,128)(2,1)S(1)}, bf16[576,128]{1,0:T(8,128)(2,1)S(1)}, u32[]{:S(2)}, u32[]{:S(2)}) collective-permute-start(bf16[576,128]{1,0:T(8,128)(2,1)S(1)} %get-tuple-element.42), channel_id=1, source_target_pairs={{0,1},{1,0},{2,3},{3,2},{4,5},{5,4},{6,7},{7,6},{8,9},{9,8},{10,11... | collective-permute-start | bytes 442376 | tf_op jit(solution)/shard_map/ppermute | solution.py:352
  38.6 5.6 %collective-permute-done.11.refs_0_ = bf16[576,128]{1,0:T(8,128)(2,1)S(1)} collective-permute-done((bf16[576,128]{1,0:T(8,128)(2,1)S(1)}, bf16[576,128]{1,0:T(8,128)(2,1)S(1)}, u32[]{:S(2)}, u32[]{:S(2)}) %collective-permute-start.11) | collective-permute-done | bytes 147488 | tf_op jit(solution)/shard_map/ppermute | solution.py:352
  44.2 1.4 %unpack.1 = (bf16[32,4,768]{2,1,0:T(4,128)(2,1)}, bf16[32,4,768]{2,1,0:T(4,128)(2,1)}, bf16[32,4,768]{2,1,0:T(4,128)(2,1)}, bf16[32,4,768]{2,1,0:T(4,128)(2,1)},...) custom-call(bf16[144,4,128]{2,1,0:T(4,128)(2,1)S(1)} %bitcast.21, bf16[144,4,128]{2,1,0:T(4,128)(2,1)S(1)} %bitcast.19, ...), custom_call_target="tpu_custom_call" | custom-call | flops 1 | bytes 1 | tf_op jit(solution)/shard_map/unpack/pallas_call | solution.py:338
  (14 shorter events, 0.0 us)
Async XLA Ops:
  2.2 15.0 %collective-permute-start = (bf16[768,128]{1,0:T(8,128)(2,1)S(1)}, bf16[768,128]{1,0:T(8,128)(2,1)S(1)}, u32[]{:S(2)}, u32[]{:S(2)}) collective-permute-start(bf16[768,128]{1,0:T(8,128)(2,1)S(1)} %bitcast.31), channel_id=1, source_target_pairs={{0,8},{4,12},{8,0},{12,4},{1,9},{5,13},{9,1},{13,5},{2,10},{6,14},... | collective-permute-start | bytes 589832 | tf_op jit(solution)/shard_map/ppermute | solution.py:352
  6.3 10.9 %collective-permute-start.1 = (bf16[768,128]{1,0:T(8,128)(2,1)S(1)}, bf16[768,128]{1,0:T(8,128)(2,1)S(1)}, u32[]{:S(2)}, u32[]{:S(2)}) collective-permute-start(bf16[768,128]{1,0:T(8,128)(2,1)S(1)} %bitcast.29), channel_id=1, source_target_pairs={{0,4},{4,0},{8,12},{12,8},{1,5},{5,1},{9,13},{13,9},{2,6},{6,2},{1... | collective-permute-start | bytes 589832 | tf_op jit(solution)/shard_map/ppermute | solution.py:352
  7.9 13.0 %collective-permute-start.2 = (bf16[768,128]{1,0:T(8,128)(2,1)S(1)}, bf16[768,128]{1,0:T(8,128)(2,1)S(1)}, u32[]{:S(2)}, u32[]{:S(2)}) collective-permute-start(bf16[768,128]{1,0:T(8,128)(2,1)S(1)} %bitcast.28), channel_id=1, source_target_pairs={{0,12},{4,8},{8,4},{12,0},{1,13},{5,9},{9,5},{13,1},{2,14},{6,10},... | collective-permute-start | bytes 589832 | tf_op jit(solution)/shard_map/ppermute | solution.py:352
  9.5 11.4 %collective-permute-start.3 = (bf16[768,128]{1,0:T(8,128)(2,1)S(1)}, bf16[768,128]{1,0:T(8,128)(2,1)S(1)}, u32[]{:S(2)}, u32[]{:S(2)}) collective-permute-start(bf16[768,128]{1,0:T(8,128)(2,1)S(1)} %bitcast.32), channel_id=1, source_target_pairs={{0,2},{1,3},{2,0},{3,1},{4,6},{5,7},{6,4},{7,5},{8,10},{9,11},{10,... | collective-permute-start | bytes 589832 | tf_op jit(solution)/shard_map/ppermute | solution.py:352
  11.3 9.6 %collective-permute-start.4 = (bf16[768,128]{1,0:T(8,128)(2,1)S(1)}, bf16[768,128]{1,0:T(8,128)(2,1)S(1)}, u32[]{:S(2)}, u32[]{:S(2)}) collective-permute-start(bf16[768,128]{1,0:T(8,128)(2,1)S(1)} %bitcast.30), channel_id=1, source_target_pairs={{0,3},{1,2},{2,1},{3,0},{4,7},{5,6},{6,5},{7,4},{8,11},{9,10},{10,... | collective-permute-start | bytes 589832 | tf_op jit(solution)/shard_map/ppermute | solution.py:352
  17.2 6.7 %collective-permute-start.8 = (bf16[768,128]{1,0:T(8,128)(2,1)S(1)}, bf16[768,128]{1,0:T(8,128)(2,1)S(1)}, u32[]{:S(2)}, u32[]{:S(2)}) collective-permute-start(bf16[768,128]{1,0:T(8,128)(2,1)S(1)} %bitcast.27), channel_id=1, source_target_pairs={{0,1},{1,0},{2,3},{3,2},{4,5},{5,4},{6,7},{7,6},{8,9},{9,8},{10,11... | collective-permute-start | bytes 589832 | tf_op jit(solution)/shard_map/ppermute | solution.py:352
  21.7 3.7 %collective-permute-start.5 = (f32[16,128]{1,0:T(8,128)S(1)}, f32[16,128]{1,0:T(8,128)S(1)}, u32[]{:S(2)}, u32[]{:S(2)}) collective-permute-start(f32[16,128]{1,0:T(8,128)S(1)} %row_scores.1.after.p0), channel_id=1, source_target_pairs={{0,2},{1,3},{2,0},{3,1},{4,6},{5,7},{6,4},{7,5},{8,10},{9,11},{10,... | collective-permute-start | bytes 24584 | tf_op jit(solution)/shard_map/ppermute | solution.py:352
  23.2 3.1 %collective-permute-start.6 = (f32[16,128]{1,0:T(8,128)S(1)}, f32[16,128]{1,0:T(8,128)S(1)}, u32[]{:S(2)}, u32[]{:S(2)}) collective-permute-start(f32[16,128]{1,0:T(8,128)S(1)} %row_scores.1.after.p0), channel_id=1, source_target_pairs={{0,3},{1,2},{2,1},{3,0},{4,7},{5,6},{6,5},{7,4},{8,11},{9,10},{10,... | collective-permute-start | bytes 24584 | tf_op jit(solution)/shard_map/ppermute | solution.py:352
  23.2 3.1 %collective-permute-start.7 = (f32[16,128]{1,0:T(8,128)S(1)}, f32[16,128]{1,0:T(8,128)S(1)}, u32[]{:S(2)}, u32[]{:S(2)}) collective-permute-start(f32[16,128]{1,0:T(8,128)S(1)} %row_scores.1.after.p0), channel_id=1, source_target_pairs={{0,1},{1,0},{2,3},{3,2},{4,5},{5,4},{6,7},{7,6},{8,9},{9,8},{10,11... | collective-permute-start | bytes 24584 | tf_op jit(solution)/shard_map/ppermute | solution.py:352
  27.7 9.3 %collective-permute-start.10 = (bf16[576,128]{1,0:T(8,128)(2,1)S(1)}, bf16[576,128]{1,0:T(8,128)(2,1)S(1)}, u32[]{:S(2)}, u32[]{:S(2)}) collective-permute-start(bf16[576,128]{1,0:T(8,128)(2,1)S(1)} %get-tuple-element.35), channel_id=1, source_target_pairs={{0,12},{4,8},{8,4},{12,0},{1,13},{5,9},{9,5},{13,1},{2,14},{6,10},... | collective-permute-start | bytes 442376 | tf_op jit(solution)/shard_map/ppermute | solution.py:352
  30.3 13.9 %collective-permute-start.11 = (bf16[576,128]{1,0:T(8,128)(2,1)S(1)}, bf16[576,128]{1,0:T(8,128)(2,1)S(1)}, u32[]{:S(2)}, u32[]{:S(2)}) collective-permute-start(bf16[576,128]{1,0:T(8,128)(2,1)S(1)} %get-tuple-element.36), channel_id=1, source_target_pairs={{0,8},{4,12},{8,0},{12,4},{1,9},{5,13},{9,1},{13,5},{2,10},{6,14},... | collective-permute-start | bytes 442376 | tf_op jit(solution)/shard_map/ppermute | solution.py:352
  33.5 10.7 %collective-permute-start.9 = (bf16[576,128]{1,0:T(8,128)(2,1)S(1)}, bf16[576,128]{1,0:T(8,128)(2,1)S(1)}, u32[]{:S(2)}, u32[]{:S(2)}) collective-permute-start(bf16[576,128]{1,0:T(8,128)(2,1)S(1)} %get-tuple-element.34), channel_id=1, source_target_pairs={{0,4},{4,0},{8,12},{12,8},{1,5},{5,1},{9,13},{13,9},{2,6},{6,2},{1... | collective-permute-start | bytes 442376 | tf_op jit(solution)/shard_map/ppermute | solution.py:352
  36.4 7.9 %collective-permute-start.12 = (bf16[576,128]{1,0:T(8,128)(2,1)S(1)}, bf16[576,128]{1,0:T(8,128)(2,1)S(1)}, u32[]{:S(2)}, u32[]{:S(2)}) collective-permute-start(bf16[576,128]{1,0:T(8,128)(2,1)S(1)} %get-tuple-element.40), channel_id=1, source_target_pairs={{0,2},{1,3},{2,0},{3,1},{4,6},{5,7},{6,4},{7,5},{8,10},{9,11},{10,... | collective-permute-start | bytes 442376 | tf_op jit(solution)/shard_map/ppermute | solution.py:352
  37.0 7.2 %collective-permute-start.13 = (bf16[576,128]{1,0:T(8,128)(2,1)S(1)}, bf16[576,128]{1,0:T(8,128)(2,1)S(1)}, u32[]{:S(2)}, u32[]{:S(2)}) collective-permute-start(bf16[576,128]{1,0:T(8,128)(2,1)S(1)} %get-tuple-element.41), channel_id=1, source_target_pairs={{0,3},{1,2},{2,1},{3,0},{4,7},{5,6},{6,5},{7,4},{8,11},{9,10},{10,... | collective-permute-start | bytes 442376 | tf_op jit(solution)/shard_map/ppermute | solution.py:352
  37.1 7.2 %collective-permute-start.14 = (bf16[576,128]{1,0:T(8,128)(2,1)S(1)}, bf16[576,128]{1,0:T(8,128)(2,1)S(1)}, u32[]{:S(2)}, u32[]{:S(2)}) collective-permute-start(bf16[576,128]{1,0:T(8,128)(2,1)S(1)} %get-tuple-element.42), channel_id=1, source_target_pairs={{0,1},{1,0},{2,3},{3,2},{4,5},{5,4},{6,7},{7,6},{8,9},{9,8},{10,11... | collective-permute-start | bytes 442376 | tf_op jit(solution)/shard_map/ppermute | solution.py:352

commit v5 on v4

--- a/solution.py
+++ b/solution.py
@@ -65,7 +65,7 @@
 
 
 def unpack_kernel(*refs):
-    outs, (held, sem) = refs[-8:-2], refs[-2:]
+    outs, (held, sem, tile_sem) = refs[-9:-3], refs[-3:]
     low_lanes = iota((16, 4, LANES), 2) < HEAD
     copies = []
     for side, axis in ((1, "seq"), (0, "col")):
@@ -77,7 +77,14 @@
             a = 3 * side + k
             for d in range(4):
                 full = pl.multiple_of((me ^ d) * LANES, LANES)
-                held[a, :, :, pl.ds(full, LANES)] = blocks[d][k * 32 : (k + 1) * 32]
+                if side:
+                    copy = pltpu.make_async_copy(
+                        blocks[d].at[pl.ds(k * 32, 32)], outs[a].at[:, :, pl.ds(full, LANES)], tile_sem.at[4 * k + d]
+                    )
+                    copy.start()
+                    copies.append(copy)
+                else:
+                    held[a, :, :, pl.ds(full, LANES)] = blocks[d][k * 32 : (k + 1) * 32]
             start = 96 + k * 16
             for d in (0, 2):
                 tail = pl.multiple_of((4 + ((me ^ d) >> 1)) * LANES, LANES)
@@ -88,9 +95,11 @@
                 z = roll_half(jnp.where(low_lanes, other, even))
                 held[a, 0:16, :, pl.ds(tail, LANES)] = jnp.where(low_lanes, even, z)
                 held[a, 16:32, :, pl.ds(tail, LANES)] = jnp.where(low_lanes, z, other)
+            first = 4 * LANES if side else 0
+            lanes = pl.ds(first, 6 * LANES - first)
             for q in range(CHUNKS):
                 rows = pl.ds(q * (32 // CHUNKS), 32 // CHUNKS)
-                copy = pltpu.make_async_copy(held.at[a, rows], outs[a].at[rows], sem.at[a * CHUNKS + q])
+                copy = pltpu.make_async_copy(held.at[a, rows, :, lanes], outs[a].at[rows, :, lanes], sem.at[a * CHUNKS + q])
                 copy.start()
                 copies.append(copy)
     for copy in copies:
@@ -368,7 +377,11 @@
 def unpack(row_back, col_back, after, shape):
     operands = [b.reshape(144, 4, LANES) for b in [row_back[d] for d in RETURN] + far_first(col_back)]
     operands += after
-    scratch = (pltpu.VMEM((6, *shape), BF16), pltpu.SemaphoreType.DMA((6 * CHUNKS,)))
+    scratch = (
+        pltpu.VMEM((6, *shape), BF16),
+        pltpu.SemaphoreType.DMA((6 * CHUNKS,)),
+        pltpu.SemaphoreType.DMA((12,)),
+    )
     return call(unpack_kernel, [(shape, BF16)] * 6, operands, "unpack", 1, scratch, out_space=HBM)
 
 

time: 45.8 us -> 45.8 us (level)
  no operation moved by 1% of the time
where the time goes in v5:
time: 45.8 us; the launch traced here: 45.6 us
  starting transfers between devices  18.1 us (40%)
  waiting for transfers between devices  16.5 us (36%)
  Pallas kernels  10.3 us (22%)
  between operations  0.7 us (2%)
    ppermute x15, starting transfers between devices, exchange(): moved[d] = lax.ppermute(blocks[d], axis, [(i, i ^ d) for i in range(4)])  18.1 us
    ppermute x15, waiting for transfers between devices, exchange(): moved[d] = lax.ppermute(blocks[d], axis, [(i, i ^ d) for i in range(4)])  16.5 us
    pallas_call x8, Pallas kernels, call(): return list(kernel(*operands))  10.3 us
  transfers between devices with their start and end apart: 15, of which 5 were waited for; matrix products, arithmetic and copies ran while one was open for 0% of the time, Pallas kernels for 13%

profile of v5, /device:TPU:0, one launch (start us, length us, event | category | flops | bytes accessed | tf_op | source)
XLA Modules:
  0.0 45.6 jit_solution(12480126401940947573)
XLA Ops:
  0.6 1.6 %row_pack.1 = (bf16[192,4,128]{2,1,0:T(4,128)(2,1)S(1)}, bf16[192,4,128]{2,1,0:T(4,128)(2,1)S(1)}, bf16[192,4,128]{2,1,0:T(4,128)(2,1)S(1)}, bf16[192,4,128]{2,1,0:T(4,128)(2,1)S(1)}) custom-call(bf16[32,4,768]{2,1,0:T(4,128)(2,1)} %refs_0_.2, bf16[32,4,768]{2,1,0:T(4,128)(2,1)} %refs_1_.2, bf16[32,4,768]{2,1,0:T(4,128)(2,1)} %refs_2_.2, ...), custom_call_target="tpu_custom_call" | custom-call | flops 1 | bytes 1 | tf_op jit(solution)/shard_map/row_pack/pallas_call | solution.py:347
  2.2 4.1 %collective-permute-start = (bf16[768,128]{1,0:T(8,128)(2,1)S(1)}, bf16[768,128]{1,0:T(8,128)(2,1)S(1)}, u32[]{:S(2)}, u32[]{:S(2)}) collective-permute-start(bf16[768,128]{1,0:T(8,128)(2,1)S(1)} %bitcast.31), channel_id=1, source_target_pairs={{0,8},{4,12},{8,0},{12,4},{1,9},{5,13},{9,1},{13,5},{2,10},{6,14},... | collective-permute-start | bytes 589832 | tf_op jit(solution)/shard_map/ppermute | solution.py:361
  6.3 1.6 %collective-permute-start.1 = (bf16[768,128]{1,0:T(8,128)(2,1)S(1)}, bf16[768,128]{1,0:T(8,128)(2,1)S(1)}, u32[]{:S(2)}, u32[]{:S(2)}) collective-permute-start(bf16[768,128]{1,0:T(8,128)(2,1)S(1)} %bitcast.29), channel_id=1, source_target_pairs={{0,4},{4,0},{8,12},{12,8},{1,5},{5,1},{9,13},{13,9},{2,6},{6,2},{1... | collective-permute-start | bytes 589832 | tf_op jit(solution)/shard_map/ppermute | solution.py:361
  7.9 1.6 %col_pack.1 = (bf16[192,4,128]{2,1,0:T(4,128)(2,1)S(1)}, bf16[192,4,128]{2,1,0:T(4,128)(2,1)S(1)}, bf16[192,4,128]{2,1,0:T(4,128)(2,1)S(1)}, bf16[192,4,128]{2,1,0:T(4,128)(2,1)S(1)}) custom-call(bf16[32,4,768]{2,1,0:T(4,128)(2,1)} %refs_0_.3, bf16[32,4,768]{2,1,0:T(4,128)(2,1)} %refs_1_.3, bf16[32,4,768]{2,1,0:T(4,128)(2,1)} %refs_2_.3, ...), custom_call_target="tpu_custom_call" | custom-call | flops 1 | bytes 1 | tf_op jit(solution)/shard_map/col_pack/pallas_call | solution.py:347
  9.5 1.8 %collective-permute-start.3 = (bf16[768,128]{1,0:T(8,128)(2,1)S(1)}, bf16[768,128]{1,0:T(8,128)(2,1)S(1)}, u32[]{:S(2)}, u32[]{:S(2)}) collective-permute-start(bf16[768,128]{1,0:T(8,128)(2,1)S(1)} %bitcast.32), channel_id=1, source_target_pairs={{0,2},{1,3},{2,0},{3,1},{4,6},{5,7},{6,4},{7,5},{8,10},{9,11},{10,... | collective-permute-start | bytes 589832 | tf_op jit(solution)/shard_map/ppermute | solution.py:361
  11.3 0.0 collective-permute-start.4
  11.3 5.9 %collective-permute-done.r0.b2 = bf16[768,128]{1,0:T(8,128)(2,1)S(1)} collective-permute-done((bf16[768,128]{1,0:T(8,128)(2,1)S(1)}, bf16[768,128]{1,0:T(8,128)(2,1)S(1)}, u32[]{:S(2)}, u32[]{:S(2)}) %collective-permute-start) | collective-permute-done | bytes 196640 | tf_op jit(solution)/shard_map/ppermute | solution.py:361
  17.2 0.0 collective-permute-start.8
  17.2 3.7 %collective-permute-done.2.r2.b3 = bf16[768,128]{1,0:T(8,128)(2,1)S(1)} collective-permute-done((bf16[768,128]{1,0:T(8,128)(2,1)S(1)}, bf16[768,128]{1,0:T(8,128)(2,1)S(1)}, u32[]{:S(2)}, u32[]{:S(2)}) %collective-permute-start.2) | collective-permute-done | bytes 196640 | tf_op jit(solution)/shard_map/ppermute | solution.py:361
  20.9 0.8 %row_scores.1.after.p0 = f32[16,128]{1,0:T(8,128)S(1)} custom-call(bf16[768,128]{1,0:T(8,128)(2,1)S(1)} %collective-permute-done.r0.b2, bf16[768,128]{1,0:T(8,128)(2,1)S(1)} %collective-permute-done.1.r1.b1, bf16[768,128]{1,0:T(8,128)(2,1)S(1)} %collective-permute-done.2.r2.b3, bf16[768,128]{1,0:T(8,128)(2,1)S(1)} %bitcast.16, ...), custom_call_target="tpu_custom_call" | custom-call | flops 1 | bytes 1 | tf_op jit(solution)/shard_map/row_scores/pallas_call | solution.py:347
  21.7 1.5 %collective-permute-start.5 = (f32[16,128]{1,0:T(8,128)S(1)}, f32[16,128]{1,0:T(8,128)S(1)}, u32[]{:S(2)}, u32[]{:S(2)}) collective-permute-start(f32[16,128]{1,0:T(8,128)S(1)} %row_scores.1.after.p0), channel_id=1, source_target_pairs={{0,2},{1,3},{2,0},{3,1},{4,6},{5,7},{6,4},{7,5},{8,10},{9,11},{10,... | collective-permute-start | bytes 24584 | tf_op jit(solution)/shard_map/ppermute | solution.py:361
  23.2 0.6 %collective-permute-start.7 = (f32[16,128]{1,0:T(8,128)S(1)}, f32[16,128]{1,0:T(8,128)S(1)}, u32[]{:S(2)}, u32[]{:S(2)}) collective-permute-start(f32[16,128]{1,0:T(8,128)S(1)} %row_scores.1.after.p0), channel_id=1, source_target_pairs={{0,1},{1,0},{2,3},{3,2},{4,5},{5,4},{6,7},{7,6},{8,9},{9,8},{10,11... | collective-permute-start | bytes 24584 | tf_op jit(solution)/shard_map/ppermute | solution.py:361
  23.9 1.1 %col_grads_first.1 = (bf16[4,768,128]{2,1,0:T(8,128)(2,1)S(1)}, bf16[4,576,128]{2,1,0:T(8,128)(2,1)S(1)}) custom-call(bf16[768,128]{1,0:T(8,128)(2,1)S(1)} %collective-permute-done.3.after0.b2, bf16[768,128]{1,0:T(8,128)(2,1)S(1)} %collective-permute-done.4.after1.b3, bf16[768,128]{1,0:T(8,128)(2,1)S(1)} %collective-permute-done.8.b1, ...), custom_call_target="tpu_custom_call" | custom-call | flops 4000000000 | bytes 1 | tf_op jit(solution)/shard_map/col_grads_first/pallas_call | solution.py:347
  25.0 0.4 collective-permute-done.5.p2
  25.4 0.9 %collective-permute-done.6.p3 = f32[16,128]{1,0:T(8,128)S(1)} collective-permute-done((f32[16,128]{1,0:T(8,128)S(1)}, f32[16,128]{1,0:T(8,128)S(1)}, u32[]{:S(2)}, u32[]{:S(2)}) %collective-permute-start.6) | collective-permute-done | bytes 8224 | tf_op jit(solution)/shard_map/ppermute | solution.py:361
  26.3 1.4 %row_grads.1 = (bf16[576,128]{1,0:T(8,128)(2,1)S(1)}, bf16[576,128]{1,0:T(8,128)(2,1)S(1)}, bf16[576,128]{1,0:T(8,128)(2,1)S(1)}, bf16[576,128]{1,0:T(8,128)(2,1)S(1)}, f32[8,128]{1,0:T(8,128)S(1)}) custom-call(f32[16,128]{1,0:T(8,128)S(1)} %collective-permute-done.5.p2, f32[16,128]{1,0:T(8,128)S(1)} %collective-permute-done.6.p3, ...), custom_call_target="tpu_custom_call" | custom-call | flops 1 | bytes 1 | tf_op jit(solution)/shard_map/row_grads/pallas_call | solution.py:347
  27.7 2.6 %collective-permute-start.10 = (bf16[576,128]{1,0:T(8,128)(2,1)S(1)}, bf16[576,128]{1,0:T(8,128)(2,1)S(1)}, u32[]{:S(2)}, u32[]{:S(2)}) collective-permute-start(bf16[576,128]{1,0:T(8,128)(2,1)S(1)} %get-tuple-element.35), channel_id=1, source_target_pairs={{0,12},{4,8},{8,4},{12,0},{1,13},{5,9},{9,5},{13,1},{2,14},{6,10},... | collective-permute-start | bytes 442376 | tf_op jit(solution)/shard_map/ppermute | solution.py:361
  30.3 3.2 %collective-permute-start.11 = (bf16[576,128]{1,0:T(8,128)(2,1)S(1)}, bf16[576,128]{1,0:T(8,128)(2,1)S(1)}, u32[]{:S(2)}, u32[]{:S(2)}) collective-permute-start(bf16[576,128]{1,0:T(8,128)(2,1)S(1)} %get-tuple-element.36), channel_id=1, source_target_pairs={{0,8},{4,12},{8,0},{12,4},{1,9},{5,13},{9,1},{13,5},{2,10},{6,14},... | collective-permute-start | bytes 442376 | tf_op jit(solution)/shard_map/ppermute | solution.py:361
  33.5 0.5 %collective-permute-start.9 = (bf16[576,128]{1,0:T(8,128)(2,1)S(1)}, bf16[576,128]{1,0:T(8,128)(2,1)S(1)}, u32[]{:S(2)}, u32[]{:S(2)}) collective-permute-start(bf16[576,128]{1,0:T(8,128)(2,1)S(1)} %get-tuple-element.34), channel_id=1, source_target_pairs={{0,4},{4,0},{8,12},{12,8},{1,5},{5,1},{9,13},{13,9},{2,6},{6,2},{1... | collective-permute-start | bytes 442376 | tf_op jit(solution)/shard_map/ppermute | solution.py:361
  34.0 2.4 %col_grads_second.1 = (bf16[576,128]{1,0:T(8,128)(2,1)S(1)}, bf16[576,128]{1,0:T(8,128)(2,1)S(1)}, bf16[576,128]{1,0:T(8,128)(2,1)S(1)}, bf16[576,128]{1,0:T(8,128)(2,1)S(1)}) custom-call(bf16[4,768,128]{2,1,0:T(8,128)(2,1)S(1)} %get-tuple-element.38.work, bf16[4,576,128]{2,1,0:T(8,128)(2,1)S(1)} %get-tuple-element.33.after.first, ...), custom_call_target="tpu_custom_call" | custom-call | flops 4000000000 | bytes 1 | tf_op jit(solution)/shard_map/col_grads_second/pallas_call | solution.py:347
  36.4 0.7 %collective-permute-start.12 = (bf16[576,128]{1,0:T(8,128)(2,1)S(1)}, bf16[576,128]{1,0:T(8,128)(2,1)S(1)}, u32[]{:S(2)}, u32[]{:S(2)}) collective-permute-start(bf16[576,128]{1,0:T(8,128)(2,1)S(1)} %get-tuple-element.40), channel_id=1, source_target_pairs={{0,2},{1,3},{2,0},{3,1},{4,6},{5,7},{6,4},{7,5},{8,10},{9,11},{10,... | collective-permute-start | bytes 442376 | tf_op jit(solution)/shard_map/ppermute | solution.py:361
  37.1 1.5 %collective-permute-start.14 = (bf16[576,128]{1,0:T(8,128)(2,1)S(1)}, bf16[576,128]{1,0:T(8,128)(2,1)S(1)}, u32[]{:S(2)}, u32[]{:S(2)}) collective-permute-start(bf16[576,128]{1,0:T(8,128)(2,1)S(1)} %get-tuple-element.42), channel_id=1, source_target_pairs={{0,1},{1,0},{2,3},{3,2},{4,5},{5,4},{6,7},{7,6},{8,9},{9,8},{10,11... | collective-permute-start | bytes 442376 | tf_op jit(solution)/shard_map/ppermute | solution.py:361
  38.6 5.6 %collective-permute-done.11.refs_0_ = bf16[576,128]{1,0:T(8,128)(2,1)S(1)} collective-permute-done((bf16[576,128]{1,0:T(8,128)(2,1)S(1)}, bf16[576,128]{1,0:T(8,128)(2,1)S(1)}, u32[]{:S(2)}, u32[]{:S(2)}) %collective-permute-start.11) | collective-permute-done | bytes 147488 | tf_op jit(solution)/shard_map/ppermute | solution.py:361
  44.2 1.3 %unpack.1 = (bf16[32,4,768]{2,1,0:T(4,128)(2,1)}, bf16[32,4,768]{2,1,0:T(4,128)(2,1)}, bf16[32,4,768]{2,1,0:T(4,128)(2,1)}, bf16[32,4,768]{2,1,0:T(4,128)(2,1)},...) custom-call(bf16[144,4,128]{2,1,0:T(4,128)(2,1)S(1)} %bitcast.21, bf16[144,4,128]{2,1,0:T(4,128)(2,1)S(1)} %bitcast.19, ...), custom_call_target="tpu_custom_call" | custom-call | flops 1 | bytes 1 | tf_op jit(solution)/shard_map/unpack/pallas_call | solution.py:347
  (14 shorter events, 0.0 us)
Async XLA Ops:
  2.2 15.0 %collective-permute-start = (bf16[768,128]{1,0:T(8,128)(2,1)S(1)}, bf16[768,128]{1,0:T(8,128)(2,1)S(1)}, u32[]{:S(2)}, u32[]{:S(2)}) collective-permute-start(bf16[768,128]{1,0:T(8,128)(2,1)S(1)} %bitcast.31), channel_id=1, source_target_pairs={{0,8},{4,12},{8,0},{12,4},{1,9},{5,13},{9,1},{13,5},{2,10},{6,14},... | collective-permute-start | bytes 589832 | tf_op jit(solution)/shard_map/ppermute | solution.py:361
  6.3 10.9 %collective-permute-start.1 = (bf16[768,128]{1,0:T(8,128)(2,1)S(1)}, bf16[768,128]{1,0:T(8,128)(2,1)S(1)}, u32[]{:S(2)}, u32[]{:S(2)}) collective-permute-start(bf16[768,128]{1,0:T(8,128)(2,1)S(1)} %bitcast.29), channel_id=1, source_target_pairs={{0,4},{4,0},{8,12},{12,8},{1,5},{5,1},{9,13},{13,9},{2,6},{6,2},{1... | collective-permute-start | bytes 589832 | tf_op jit(solution)/shard_map/ppermute | solution.py:361
  7.9 13.0 %collective-permute-start.2 = (bf16[768,128]{1,0:T(8,128)(2,1)S(1)}, bf16[768,128]{1,0:T(8,128)(2,1)S(1)}, u32[]{:S(2)}, u32[]{:S(2)}) collective-permute-start(bf16[768,128]{1,0:T(8,128)(2,1)S(1)} %bitcast.28), channel_id=1, source_target_pairs={{0,12},{4,8},{8,4},{12,0},{1,13},{5,9},{9,5},{13,1},{2,14},{6,10},... | collective-permute-start | bytes 589832 | tf_op jit(solution)/shard_map/ppermute | solution.py:361
  9.5 11.4 %collective-permute-start.3 = (bf16[768,128]{1,0:T(8,128)(2,1)S(1)}, bf16[768,128]{1,0:T(8,128)(2,1)S(1)}, u32[]{:S(2)}, u32[]{:S(2)}) collective-permute-start(bf16[768,128]{1,0:T(8,128)(2,1)S(1)} %bitcast.32), channel_id=1, source_target_pairs={{0,2},{1,3},{2,0},{3,1},{4,6},{5,7},{6,4},{7,5},{8,10},{9,11},{10,... | collective-permute-start | bytes 589832 | tf_op jit(solution)/shard_map/ppermute | solution.py:361
  11.3 9.6 %collective-permute-start.4 = (bf16[768,128]{1,0:T(8,128)(2,1)S(1)}, bf16[768,128]{1,0:T(8,128)(2,1)S(1)}, u32[]{:S(2)}, u32[]{:S(2)}) collective-permute-start(bf16[768,128]{1,0:T(8,128)(2,1)S(1)} %bitcast.30), channel_id=1, source_target_pairs={{0,3},{1,2},{2,1},{3,0},{4,7},{5,6},{6,5},{7,4},{8,11},{9,10},{10,... | collective-permute-start | bytes 589832 | tf_op jit(solution)/shard_map/ppermute | solution.py:361
  17.2 6.7 %collective-permute-start.8 = (bf16[768,128]{1,0:T(8,128)(2,1)S(1)}, bf16[768,128]{1,0:T(8,128)(2,1)S(1)}, u32[]{:S(2)}, u32[]{:S(2)}) collective-permute-start(bf16[768,128]{1,0:T(8,128)(2,1)S(1)} %bitcast.27), channel_id=1, source_target_pairs={{0,1},{1,0},{2,3},{3,2},{4,5},{5,4},{6,7},{7,6},{8,9},{9,8},{10,11... | collective-permute-start | bytes 589832 | tf_op jit(solution)/shard_map/ppermute | solution.py:361
  21.7 3.7 %collective-permute-start.5 = (f32[16,128]{1,0:T(8,128)S(1)}, f32[16,128]{1,0:T(8,128)S(1)}, u32[]{:S(2)}, u32[]{:S(2)}) collective-permute-start(f32[16,128]{1,0:T(8,128)S(1)} %row_scores.1.after.p0), channel_id=1, source_target_pairs={{0,2},{1,3},{2,0},{3,1},{4,6},{5,7},{6,4},{7,5},{8,10},{9,11},{10,... | collective-permute-start | bytes 24584 | tf_op jit(solution)/shard_map/ppermute | solution.py:361
  23.2 3.1 %collective-permute-start.6 = (f32[16,128]{1,0:T(8,128)S(1)}, f32[16,128]{1,0:T(8,128)S(1)}, u32[]{:S(2)}, u32[]{:S(2)}) collective-permute-start(f32[16,128]{1,0:T(8,128)S(1)} %row_scores.1.after.p0), channel_id=1, source_target_pairs={{0,3},{1,2},{2,1},{3,0},{4,7},{5,6},{6,5},{7,4},{8,11},{9,10},{10,... | collective-permute-start | bytes 24584 | tf_op jit(solution)/shard_map/ppermute | solution.py:361
  23.2 3.1 %collective-permute-start.7 = (f32[16,128]{1,0:T(8,128)S(1)}, f32[16,128]{1,0:T(8,128)S(1)}, u32[]{:S(2)}, u32[]{:S(2)}) collective-permute-start(f32[16,128]{1,0:T(8,128)S(1)} %row_scores.1.after.p0), channel_id=1, source_target_pairs={{0,1},{1,0},{2,3},{3,2},{4,5},{5,4},{6,7},{7,6},{8,9},{9,8},{10,11... | collective-permute-start | bytes 24584 | tf_op jit(solution)/shard_map/ppermute | solution.py:361
  27.7 9.3 %collective-permute-start.10 = (bf16[576,128]{1,0:T(8,128)(2,1)S(1)}, bf16[576,128]{1,0:T(8,128)(2,1)S(1)}, u32[]{:S(2)}, u32[]{:S(2)}) collective-permute-start(bf16[576,128]{1,0:T(8,128)(2,1)S(1)} %get-tuple-element.35), channel_id=1, source_target_pairs={{0,12},{4,8},{8,4},{12,0},{1,13},{5,9},{9,5},{13,1},{2,14},{6,10},... | collective-permute-start | bytes 442376 | tf_op jit(solution)/shard_map/ppermute | solution.py:361
  30.3 13.9 %collective-permute-start.11 = (bf16[576,128]{1,0:T(8,128)(2,1)S(1)}, bf16[576,128]{1,0:T(8,128)(2,1)S(1)}, u32[]{:S(2)}, u32[]{:S(2)}) collective-permute-start(bf16[576,128]{1,0:T(8,128)(2,1)S(1)} %get-tuple-element.36), channel_id=1, source_target_pairs={{0,8},{4,12},{8,0},{12,4},{1,9},{5,13},{9,1},{13,5},{2,10},{6,14},... | collective-permute-start | bytes 442376 | tf_op jit(solution)/shard_map/ppermute | solution.py:361
  33.5 10.7 %collective-permute-start.9 = (bf16[576,128]{1,0:T(8,128)(2,1)S(1)}, bf16[576,128]{1,0:T(8,128)(2,1)S(1)}, u32[]{:S(2)}, u32[]{:S(2)}) collective-permute-start(bf16[576,128]{1,0:T(8,128)(2,1)S(1)} %get-tuple-element.34), channel_id=1, source_target_pairs={{0,4},{4,0},{8,12},{12,8},{1,5},{5,1},{9,13},{13,9},{2,6},{6,2},{1... | collective-permute-start | bytes 442376 | tf_op jit(solution)/shard_map/ppermute | solution.py:361
  36.4 7.9 %collective-permute-start.12 = (bf16[576,128]{1,0:T(8,128)(2,1)S(1)}, bf16[576,128]{1,0:T(8,128)(2,1)S(1)}, u32[]{:S(2)}, u32[]{:S(2)}) collective-permute-start(bf16[576,128]{1,0:T(8,128)(2,1)S(1)} %get-tuple-element.40), channel_id=1, source_target_pairs={{0,2},{1,3},{2,0},{3,1},{4,6},{5,7},{6,4},{7,5},{8,10},{9,11},{10,... | collective-permute-start | bytes 442376 | tf_op jit(solution)/shard_map/ppermute | solution.py:361
  37.0 7.2 %collective-permute-start.13 = (bf16[576,128]{1,0:T(8,128)(2,1)S(1)}, bf16[576,128]{1,0:T(8,128)(2,1)S(1)}, u32[]{:S(2)}, u32[]{:S(2)}) collective-permute-start(bf16[576,128]{1,0:T(8,128)(2,1)S(1)} %get-tuple-element.41), channel_id=1, source_target_pairs={{0,3},{1,2},{2,1},{3,0},{4,7},{5,6},{6,5},{7,4},{8,11},{9,10},{10,... | collective-permute-start | bytes 442376 | tf_op jit(solution)/shard_map/ppermute | solution.py:361
  37.1 7.2 %collective-permute-start.14 = (bf16[576,128]{1,0:T(8,128)(2,1)S(1)}, bf16[576,128]{1,0:T(8,128)(2,1)S(1)}, u32[]{:S(2)}, u32[]{:S(2)}) collective-permute-start(bf16[576,128]{1,0:T(8,128)(2,1)S(1)} %get-tuple-element.42), channel_id=1, source_target_pairs={{0,1},{1,0},{2,3},{3,2},{4,5},{5,4},{6,7},{7,6},{8,9},{9,8},{10,11... | collective-permute-start | bytes 442376 | tf_op jit(solution)/shard_map/ppermute | solution.py:361

commit v6 on v4

--- a/solution.py
+++ b/solution.py
@@ -156,15 +156,8 @@
             high = t.astype(BF16)
             total = total + nn(high, place)
             t = t - high.astype(F32)
-    r = iota((16, 32), 0)
-    c = iota((16, 32), 1)
-    fold = (((c >> 3) == (r >> 2)) & ((c & 3) == (r & 3))).astype(BF16)
-    result = jnp.zeros((16, LANES), F32)
-    for _ in range(3):
-        high = total.astype(BF16)
-        result = result + nn(fold, high)
-        total = total - high.astype(F32)
-    out[...] = result
+    halves = [total[8 * d : 8 * d + 4] + total[8 * d + 4 : 8 * d + 8] for d in range(4)]
+    out[...] = jnp.concatenate(halves, axis=0)
 
 
 def row_grad_kernel(row_scale, p2, p3, p1, p0, b2, b3, b1, b0, after, *outs):

time: 45.8 us -> 45.7 us (level)
  no operation moved by 1% of the time
where the time goes in v6:
time: 45.7 us; the launch traced here: 45.5 us
  starting transfers between devices  18.1 us (40%)
  waiting for transfers between devices  16.5 us (36%)
  Pallas kernels  10.2 us (22%)
  between operations  0.71 us (2%)
    ppermute x15, starting transfers between devices, exchange(): moved[d] = lax.ppermute(blocks[d], axis, [(i, i ^ d) for i in range(4)])  18.1 us
    ppermute x15, waiting for transfers between devices, exchange(): moved[d] = lax.ppermute(blocks[d], axis, [(i, i ^ d) for i in range(4)])  16.5 us
    pallas_call x8, Pallas kernels, call(): return list(kernel(*operands))  10.2 us
  transfers between devices with their start and end apart: 15, of which 5 were waited for; matrix products, arithmetic and copies ran while one was open for 0% of the time, Pallas kernels for 13%

profile of v6, /device:TPU:0, one launch (start us, length us, event | category | flops | bytes accessed | tf_op | source)
XLA Modules:
  0.0 45.5 jit_solution(9651105658665540156)
XLA Ops:
  0.6 1.6 %row_pack.1 = (bf16[192,4,128]{2,1,0:T(4,128)(2,1)S(1)}, bf16[192,4,128]{2,1,0:T(4,128)(2,1)S(1)}, bf16[192,4,128]{2,1,0:T(4,128)(2,1)S(1)}, bf16[192,4,128]{2,1,0:T(4,128)(2,1)S(1)}) custom-call(bf16[32,4,768]{2,1,0:T(4,128)(2,1)} %refs_0_.2, bf16[32,4,768]{2,1,0:T(4,128)(2,1)} %refs_1_.2, bf16[32,4,768]{2,1,0:T(4,128)(2,1)} %refs_2_.2, ...), custom_call_target="tpu_custom_call" | custom-call | flops 1 | bytes 1 | tf_op jit(solution)/shard_map/row_pack/pallas_call | solution.py:331
  2.2 4.1 %collective-permute-start = (bf16[768,128]{1,0:T(8,128)(2,1)S(1)}, bf16[768,128]{1,0:T(8,128)(2,1)S(1)}, u32[]{:S(2)}, u32[]{:S(2)}) collective-permute-start(bf16[768,128]{1,0:T(8,128)(2,1)S(1)} %bitcast.31), channel_id=1, source_target_pairs={{0,8},{4,12},{8,0},{12,4},{1,9},{5,13},{9,1},{13,5},{2,10},{6,14},... | collective-permute-start | bytes 589832 | tf_op jit(solution)/shard_map/ppermute | solution.py:345
  6.3 1.6 %collective-permute-start.1 = (bf16[768,128]{1,0:T(8,128)(2,1)S(1)}, bf16[768,128]{1,0:T(8,128)(2,1)S(1)}, u32[]{:S(2)}, u32[]{:S(2)}) collective-permute-start(bf16[768,128]{1,0:T(8,128)(2,1)S(1)} %bitcast.29), channel_id=1, source_target_pairs={{0,4},{4,0},{8,12},{12,8},{1,5},{5,1},{9,13},{13,9},{2,6},{6,2},{1... | collective-permute-start | bytes 589832 | tf_op jit(solution)/shard_map/ppermute | solution.py:345
  7.9 0.0 collective-permute-start.2
  7.9 1.6 %col_pack.1 = (bf16[192,4,128]{2,1,0:T(4,128)(2,1)S(1)}, bf16[192,4,128]{2,1,0:T(4,128)(2,1)S(1)}, bf16[192,4,128]{2,1,0:T(4,128)(2,1)S(1)}, bf16[192,4,128]{2,1,0:T(4,128)(2,1)S(1)}) custom-call(bf16[32,4,768]{2,1,0:T(4,128)(2,1)} %refs_0_.3, bf16[32,4,768]{2,1,0:T(4,128)(2,1)} %refs_1_.3, bf16[32,4,768]{2,1,0:T(4,128)(2,1)} %refs_2_.3, ...), custom_call_target="tpu_custom_call" | custom-call | flops 1 | bytes 1 | tf_op jit(solution)/shard_map/col_pack/pallas_call | solution.py:331
  9.5 1.8 %collective-permute-start.3 = (bf16[768,128]{1,0:T(8,128)(2,1)S(1)}, bf16[768,128]{1,0:T(8,128)(2,1)S(1)}, u32[]{:S(2)}, u32[]{:S(2)}) collective-permute-start(bf16[768,128]{1,0:T(8,128)(2,1)S(1)} %bitcast.32), channel_id=1, source_target_pairs={{0,2},{1,3},{2,0},{3,1},{4,6},{5,7},{6,4},{7,5},{8,10},{9,11},{10,... | collective-permute-start | bytes 589832 | tf_op jit(solution)/shard_map/ppermute | solution.py:345
  11.3 5.9 %collective-permute-done.r0.b2 = bf16[768,128]{1,0:T(8,128)(2,1)S(1)} collective-permute-done((bf16[768,128]{1,0:T(8,128)(2,1)S(1)}, bf16[768,128]{1,0:T(8,128)(2,1)S(1)}, u32[]{:S(2)}, u32[]{:S(2)}) %collective-permute-start) | collective-permute-done | bytes 196640 | tf_op jit(solution)/shard_map/ppermute | solution.py:345
  17.2 0.0 collective-permute-done.1.r1.b1
  17.2 3.7 %collective-permute-done.2.r2.b3 = bf16[768,128]{1,0:T(8,128)(2,1)S(1)} collective-permute-done((bf16[768,128]{1,0:T(8,128)(2,1)S(1)}, bf16[768,128]{1,0:T(8,128)(2,1)S(1)}, u32[]{:S(2)}, u32[]{:S(2)}) %collective-permute-start.2) | collective-permute-done | bytes 196640 | tf_op jit(solution)/shard_map/ppermute | solution.py:345
  20.9 0.7 %row_scores.1.after.p0 = f32[16,128]{1,0:T(8,128)S(1)} custom-call(bf16[768,128]{1,0:T(8,128)(2,1)S(1)} %collective-permute-done.r0.b2, bf16[768,128]{1,0:T(8,128)(2,1)S(1)} %collective-permute-done.1.r1.b1, bf16[768,128]{1,0:T(8,128)(2,1)S(1)} %collective-permute-done.2.r2.b3, bf16[768,128]{1,0:T(8,128)(2,1)S(1)} %bitcast.16, ...), custom_call_target="tpu_custom_call" | custom-call | flops 1 | bytes 1 | tf_op jit(solution)/shard_map/row_scores/pallas_call | solution.py:331
  21.6 1.6 %collective-permute-start.5 = (f32[16,128]{1,0:T(8,128)S(1)}, f32[16,128]{1,0:T(8,128)S(1)}, u32[]{:S(2)}, u32[]{:S(2)}) collective-permute-start(f32[16,128]{1,0:T(8,128)S(1)} %row_scores.1.after.p0), channel_id=1, source_target_pairs={{0,2},{1,3},{2,0},{3,1},{4,6},{5,7},{6,4},{7,5},{8,10},{9,11},{10,... | collective-permute-start | bytes 24584 | tf_op jit(solution)/shard_map/ppermute | solution.py:345
  23.2 0.6 %collective-permute-start.7 = (f32[16,128]{1,0:T(8,128)S(1)}, f32[16,128]{1,0:T(8,128)S(1)}, u32[]{:S(2)}, u32[]{:S(2)}) collective-permute-start(f32[16,128]{1,0:T(8,128)S(1)} %row_scores.1.after.p0), channel_id=1, source_target_pairs={{0,1},{1,0},{2,3},{3,2},{4,5},{5,4},{6,7},{7,6},{8,9},{9,8},{10,11... | collective-permute-start | bytes 24584 | tf_op jit(solution)/shard_map/ppermute | solution.py:345
  23.8 1.1 %col_grads_first.1 = (bf16[4,768,128]{2,1,0:T(8,128)(2,1)S(1)}, bf16[4,576,128]{2,1,0:T(8,128)(2,1)S(1)}) custom-call(bf16[768,128]{1,0:T(8,128)(2,1)S(1)} %collective-permute-done.3.after0.b2, bf16[768,128]{1,0:T(8,128)(2,1)S(1)} %collective-permute-done.4.after1.b3, bf16[768,128]{1,0:T(8,128)(2,1)S(1)} %collective-permute-done.8.b1, ...), custom_call_target="tpu_custom_call" | custom-call | flops 4000000000 | bytes 1 | tf_op jit(solution)/shard_map/col_grads_first/pallas_call | solution.py:331
  24.9 0.4 collective-permute-done.5.p2
  25.3 0.9 %collective-permute-done.6.p3 = f32[16,128]{1,0:T(8,128)S(1)} collective-permute-done((f32[16,128]{1,0:T(8,128)S(1)}, f32[16,128]{1,0:T(8,128)S(1)}, u32[]{:S(2)}, u32[]{:S(2)}) %collective-permute-start.6) | collective-permute-done | bytes 8224 | tf_op jit(solution)/shard_map/ppermute | solution.py:345
  26.2 1.4 %row_grads.1 = (bf16[576,128]{1,0:T(8,128)(2,1)S(1)}, bf16[576,128]{1,0:T(8,128)(2,1)S(1)}, bf16[576,128]{1,0:T(8,128)(2,1)S(1)}, bf16[576,128]{1,0:T(8,128)(2,1)S(1)}, f32[8,128]{1,0:T(8,128)S(1)}) custom-call(f32[16,128]{1,0:T(8,128)S(1)} %collective-permute-done.5.p2, f32[16,128]{1,0:T(8,128)S(1)} %collective-permute-done.6.p3, ...), custom_call_target="tpu_custom_call" | custom-call | flops 1 | bytes 1 | tf_op jit(solution)/shard_map/row_grads/pallas_call | solution.py:331
  27.7 2.6 %collective-permute-start.10 = (bf16[576,128]{1,0:T(8,128)(2,1)S(1)}, bf16[576,128]{1,0:T(8,128)(2,1)S(1)}, u32[]{:S(2)}, u32[]{:S(2)}) collective-permute-start(bf16[576,128]{1,0:T(8,128)(2,1)S(1)} %get-tuple-element.35), channel_id=1, source_target_pairs={{0,12},{4,8},{8,4},{12,0},{1,13},{5,9},{9,5},{13,1},{2,14},{6,10},... | collective-permute-start | bytes 442376 | tf_op jit(solution)/shard_map/ppermute | solution.py:345
  30.2 3.2 %collective-permute-start.11 = (bf16[576,128]{1,0:T(8,128)(2,1)S(1)}, bf16[576,128]{1,0:T(8,128)(2,1)S(1)}, u32[]{:S(2)}, u32[]{:S(2)}) collective-permute-start(bf16[576,128]{1,0:T(8,128)(2,1)S(1)} %get-tuple-element.36), channel_id=1, source_target_pairs={{0,8},{4,12},{8,0},{12,4},{1,9},{5,13},{9,1},{13,5},{2,10},{6,14},... | collective-permute-start | bytes 442376 | tf_op jit(solution)/shard_map/ppermute | solution.py:345
  33.5 0.5 %collective-permute-start.9 = (bf16[576,128]{1,0:T(8,128)(2,1)S(1)}, bf16[576,128]{1,0:T(8,128)(2,1)S(1)}, u32[]{:S(2)}, u32[]{:S(2)}) collective-permute-start(bf16[576,128]{1,0:T(8,128)(2,1)S(1)} %get-tuple-element.34), channel_id=1, source_target_pairs={{0,4},{4,0},{8,12},{12,8},{1,5},{5,1},{9,13},{13,9},{2,6},{6,2},{1... | collective-permute-start | bytes 442376 | tf_op jit(solution)/shard_map/ppermute | solution.py:345
  33.9 2.4 %col_grads_second.1 = (bf16[576,128]{1,0:T(8,128)(2,1)S(1)}, bf16[576,128]{1,0:T(8,128)(2,1)S(1)}, bf16[576,128]{1,0:T(8,128)(2,1)S(1)}, bf16[576,128]{1,0:T(8,128)(2,1)S(1)}) custom-call(bf16[4,768,128]{2,1,0:T(8,128)(2,1)S(1)} %get-tuple-element.38.work, bf16[4,576,128]{2,1,0:T(8,128)(2,1)S(1)} %get-tuple-element.33.after.first, ...), custom_call_target="tpu_custom_call" | custom-call | flops 4000000000 | bytes 1 | tf_op jit(solution)/shard_map/col_grads_second/pallas_call | solution.py:331
  36.3 0.7 %collective-permute-start.12 = (bf16[576,128]{1,0:T(8,128)(2,1)S(1)}, bf16[576,128]{1,0:T(8,128)(2,1)S(1)}, u32[]{:S(2)}, u32[]{:S(2)}) collective-permute-start(bf16[576,128]{1,0:T(8,128)(2,1)S(1)} %get-tuple-element.40), channel_id=1, source_target_pairs={{0,2},{1,3},{2,0},{3,1},{4,6},{5,7},{6,4},{7,5},{8,10},{9,11},{10,... | collective-permute-start | bytes 442376 | tf_op jit(solution)/shard_map/ppermute | solution.py:345
  37.0 1.5 %collective-permute-start.14 = (bf16[576,128]{1,0:T(8,128)(2,1)S(1)}, bf16[576,128]{1,0:T(8,128)(2,1)S(1)}, u32[]{:S(2)}, u32[]{:S(2)}) collective-permute-start(bf16[576,128]{1,0:T(8,128)(2,1)S(1)} %get-tuple-element.42), channel_id=1, source_target_pairs={{0,1},{1,0},{2,3},{3,2},{4,5},{5,4},{6,7},{7,6},{8,9},{9,8},{10,11... | collective-permute-start | bytes 442376 | tf_op jit(solution)/shard_map/ppermute | solution.py:345
  38.5 5.6 %collective-permute-done.11.refs_0_ = bf16[576,128]{1,0:T(8,128)(2,1)S(1)} collective-permute-done((bf16[576,128]{1,0:T(8,128)(2,1)S(1)}, bf16[576,128]{1,0:T(8,128)(2,1)S(1)}, u32[]{:S(2)}, u32[]{:S(2)}) %collective-permute-start.11) | collective-permute-done | bytes 147488 | tf_op jit(solution)/shard_map/ppermute | solution.py:345
  44.2 1.4 %unpack.1 = (bf16[32,4,768]{2,1,0:T(4,128)(2,1)}, bf16[32,4,768]{2,1,0:T(4,128)(2,1)}, bf16[32,4,768]{2,1,0:T(4,128)(2,1)}, bf16[32,4,768]{2,1,0:T(4,128)(2,1)},...) custom-call(bf16[144,4,128]{2,1,0:T(4,128)(2,1)S(1)} %bitcast.21, bf16[144,4,128]{2,1,0:T(4,128)(2,1)S(1)} %bitcast.19, ...), custom_call_target="tpu_custom_call" | custom-call | flops 1 | bytes 1 | tf_op jit(solution)/shard_map/unpack/pallas_call | solution.py:331
  (14 shorter events, 0.0 us)
Async XLA Ops:
  2.2 15.0 %collective-permute-start = (bf16[768,128]{1,0:T(8,128)(2,1)S(1)}, bf16[768,128]{1,0:T(8,128)(2,1)S(1)}, u32[]{:S(2)}, u32[]{:S(2)}) collective-permute-start(bf16[768,128]{1,0:T(8,128)(2,1)S(1)} %bitcast.31), channel_id=1, source_target_pairs={{0,8},{4,12},{8,0},{12,4},{1,9},{5,13},{9,1},{13,5},{2,10},{6,14},... | collective-permute-start | bytes 589832 | tf_op jit(solution)/shard_map/ppermute | solution.py:345
  6.3 10.9 %collective-permute-start.1 = (bf16[768,128]{1,0:T(8,128)(2,1)S(1)}, bf16[768,128]{1,0:T(8,128)(2,1)S(1)}, u32[]{:S(2)}, u32[]{:S(2)}) collective-permute-start(bf16[768,128]{1,0:T(8,128)(2,1)S(1)} %bitcast.29), channel_id=1, source_target_pairs={{0,4},{4,0},{8,12},{12,8},{1,5},{5,1},{9,13},{13,9},{2,6},{6,2},{1... | collective-permute-start | bytes 589832 | tf_op jit(solution)/shard_map/ppermute | solution.py:345
  7.9 13.0 %collective-permute-start.2 = (bf16[768,128]{1,0:T(8,128)(2,1)S(1)}, bf16[768,128]{1,0:T(8,128)(2,1)S(1)}, u32[]{:S(2)}, u32[]{:S(2)}) collective-permute-start(bf16[768,128]{1,0:T(8,128)(2,1)S(1)} %bitcast.28), channel_id=1, source_target_pairs={{0,12},{4,8},{8,4},{12,0},{1,13},{5,9},{9,5},{13,1},{2,14},{6,10},... | collective-permute-start | bytes 589832 | tf_op jit(solution)/shard_map/ppermute | solution.py:345
  9.5 11.4 %collective-permute-start.3 = (bf16[768,128]{1,0:T(8,128)(2,1)S(1)}, bf16[768,128]{1,0:T(8,128)(2,1)S(1)}, u32[]{:S(2)}, u32[]{:S(2)}) collective-permute-start(bf16[768,128]{1,0:T(8,128)(2,1)S(1)} %bitcast.32), channel_id=1, source_target_pairs={{0,2},{1,3},{2,0},{3,1},{4,6},{5,7},{6,4},{7,5},{8,10},{9,11},{10,... | collective-permute-start | bytes 589832 | tf_op jit(solution)/shard_map/ppermute | solution.py:345
  11.3 9.6 %collective-permute-start.4 = (bf16[768,128]{1,0:T(8,128)(2,1)S(1)}, bf16[768,128]{1,0:T(8,128)(2,1)S(1)}, u32[]{:S(2)}, u32[]{:S(2)}) collective-permute-start(bf16[768,128]{1,0:T(8,128)(2,1)S(1)} %bitcast.30), channel_id=1, source_target_pairs={{0,3},{1,2},{2,1},{3,0},{4,7},{5,6},{6,5},{7,4},{8,11},{9,10},{10,... | collective-permute-start | bytes 589832 | tf_op jit(solution)/shard_map/ppermute | solution.py:345
  17.2 6.6 %collective-permute-start.8 = (bf16[768,128]{1,0:T(8,128)(2,1)S(1)}, bf16[768,128]{1,0:T(8,128)(2,1)S(1)}, u32[]{:S(2)}, u32[]{:S(2)}) collective-permute-start(bf16[768,128]{1,0:T(8,128)(2,1)S(1)} %bitcast.27), channel_id=1, source_target_pairs={{0,1},{1,0},{2,3},{3,2},{4,5},{5,4},{6,7},{7,6},{8,9},{9,8},{10,11... | collective-permute-start | bytes 589832 | tf_op jit(solution)/shard_map/ppermute | solution.py:345
  21.6 3.7 %collective-permute-start.5 = (f32[16,128]{1,0:T(8,128)S(1)}, f32[16,128]{1,0:T(8,128)S(1)}, u32[]{:S(2)}, u32[]{:S(2)}) collective-permute-start(f32[16,128]{1,0:T(8,128)S(1)} %row_scores.1.after.p0), channel_id=1, source_target_pairs={{0,2},{1,3},{2,0},{3,1},{4,6},{5,7},{6,4},{7,5},{8,10},{9,11},{10,... | collective-permute-start | bytes 24584 | tf_op jit(solution)/shard_map/ppermute | solution.py:345
  23.2 3.1 %collective-permute-start.6 = (f32[16,128]{1,0:T(8,128)S(1)}, f32[16,128]{1,0:T(8,128)S(1)}, u32[]{:S(2)}, u32[]{:S(2)}) collective-permute-start(f32[16,128]{1,0:T(8,128)S(1)} %row_scores.1.after.p0), channel_id=1, source_target_pairs={{0,3},{1,2},{2,1},{3,0},{4,7},{5,6},{6,5},{7,4},{8,11},{9,10},{10,... | collective-permute-start | bytes 24584 | tf_op jit(solution)/shard_map/ppermute | solution.py:345
  23.2 3.1 %collective-permute-start.7 = (f32[16,128]{1,0:T(8,128)S(1)}, f32[16,128]{1,0:T(8,128)S(1)}, u32[]{:S(2)}, u32[]{:S(2)}) collective-permute-start(f32[16,128]{1,0:T(8,128)S(1)} %row_scores.1.after.p0), channel_id=1, source_target_pairs={{0,1},{1,0},{2,3},{3,2},{4,5},{5,4},{6,7},{7,6},{8,9},{9,8},{10,11... | collective-permute-start | bytes 24584 | tf_op jit(solution)/shard_map/ppermute | solution.py:345
  27.7 9.3 %collective-permute-start.10 = (bf16[576,128]{1,0:T(8,128)(2,1)S(1)}, bf16[576,128]{1,0:T(8,128)(2,1)S(1)}, u32[]{:S(2)}, u32[]{:S(2)}) collective-permute-start(bf16[576,128]{1,0:T(8,128)(2,1)S(1)} %get-tuple-element.35), channel_id=1, source_target_pairs={{0,12},{4,8},{8,4},{12,0},{1,13},{5,9},{9,5},{13,1},{2,14},{6,10},... | collective-permute-start | bytes 442376 | tf_op jit(solution)/shard_map/ppermute | solution.py:345
  30.2 13.9 %collective-permute-start.11 = (bf16[576,128]{1,0:T(8,128)(2,1)S(1)}, bf16[576,128]{1,0:T(8,128)(2,1)S(1)}, u32[]{:S(2)}, u32[]{:S(2)}) collective-permute-start(bf16[576,128]{1,0:T(8,128)(2,1)S(1)} %get-tuple-element.36), channel_id=1, source_target_pairs={{0,8},{4,12},{8,0},{12,4},{1,9},{5,13},{9,1},{13,5},{2,10},{6,14},... | collective-permute-start | bytes 442376 | tf_op jit(solution)/shard_map/ppermute | solution.py:345
  33.5 10.7 %collective-permute-start.9 = (bf16[576,128]{1,0:T(8,128)(2,1)S(1)}, bf16[576,128]{1,0:T(8,128)(2,1)S(1)}, u32[]{:S(2)}, u32[]{:S(2)}) collective-permute-start(bf16[576,128]{1,0:T(8,128)(2,1)S(1)} %get-tuple-element.34), channel_id=1, source_target_pairs={{0,4},{4,0},{8,12},{12,8},{1,5},{5,1},{9,13},{13,9},{2,6},{6,2},{1... | collective-permute-start | bytes 442376 | tf_op jit(solution)/shard_map/ppermute | solution.py:345
  36.3 7.9 %collective-permute-start.12 = (bf16[576,128]{1,0:T(8,128)(2,1)S(1)}, bf16[576,128]{1,0:T(8,128)(2,1)S(1)}, u32[]{:S(2)}, u32[]{:S(2)}) collective-permute-start(bf16[576,128]{1,0:T(8,128)(2,1)S(1)} %get-tuple-element.40), channel_id=1, source_target_pairs={{0,2},{1,3},{2,0},{3,1},{4,6},{5,7},{6,4},{7,5},{8,10},{9,11},{10,... | collective-permute-start | bytes 442376 | tf_op jit(solution)/shard_map/ppermute | solution.py:345
  37.0 7.2 %collective-permute-start.13 = (bf16[576,128]{1,0:T(8,128)(2,1)S(1)}, bf16[576,128]{1,0:T(8,128)(2,1)S(1)}, u32[]{:S(2)}, u32[]{:S(2)}) collective-permute-start(bf16[576,128]{1,0:T(8,128)(2,1)S(1)} %get-tuple-element.41), channel_id=1, source_target_pairs={{0,3},{1,2},{2,1},{3,0},{4,7},{5,6},{6,5},{7,4},{8,11},{9,10},{10,... | collective-permute-start | bytes 442376 | tf_op jit(solution)/shard_map/ppermute | solution.py:345
  37.0 7.2 %collective-permute-start.14 = (bf16[576,128]{1,0:T(8,128)(2,1)S(1)}, bf16[576,128]{1,0:T(8,128)(2,1)S(1)}, u32[]{:S(2)}, u32[]{:S(2)}) collective-permute-start(bf16[576,128]{1,0:T(8,128)(2,1)S(1)} %get-tuple-element.42), channel_id=1, source_target_pairs={{0,1},{1,0},{2,3},{3,2},{4,5},{5,4},{6,7},{7,6},{8,9},{9,8},{10,11... | collective-permute-start | bytes 442376 | tf_op jit(solution)/shard_map/ppermute | solution.py:345
